TPU v7x, 32 devices: a whole 2x2x4 slice. The times are simulated.
32 devices in a mesh: bx: 4 (over z), by: 8 (over y, x, core).
Axes of the slice: x: 2, y: 2, z: 4, core: 2. Of those that a mesh axis runs over, the one named last changes fastest.
Arguments:
- flow: float32 [5, 32, 128, 128], P(None, 'bx', 'by'), as said below
- adjoint: float32 [5, 32, 128, 128], P(None, 'bx', 'by'), may hold values from -6 to 6
- faces: float32 [6, 3, 32, 128, 128], P(None, None, 'bx', 'by'), may hold values from -6 to 6
- decay: float32 [32, 128, 128], P('bx', 'by'), may hold values from 0.2 to 1
- surface_mask: int32 [32, 128, 128], P('bx', 'by'), may hold values 0 or 1
Outputs:
- adjoint_product: float32 [5, 32, 128, 128], P(None, 'bx', 'by')
- warp_adjoint: float32 [3, 32, 128, 128], P(None, 'bx', 'by')
Inputs may be any that keep to these rules, and one draw needn't show every extreme that they name: `flow`: density between 0.5 and 2 and pressure between 0.5 and 2, up to rounding.
All inputs are finite; a program needn't handle non-finite values. No bound on the sum of `surface_mask` on one device may be relied on, other than what follows from the above.
Results may differ from a plain program's by a relative error of at most 0.00019.
Values sent between devices are 32-bit elements; how exact they have to be, the bound alone decides.
No kernel may reach another device: no remote copies, remote signals or barrier semaphores. Data moves between devices by JAX's collectives and lax.ppermute only.
A program may use at most 64 MiB of HBM per device.

v0:
```python
import functools
import math

import jax
import jax.numpy as jnp
from jax import lax
from jax.experimental import pallas as pl
from jax.experimental.pallas import tpu as pltpu
from jax.sharding import PartitionSpec as P

SWEEPS = 4
KAPPA = 0.15
GAS = 0.4

F32 = jnp.float32

REACH = [[(0, 0)]]
for _ in range(SWEEPS - 1):
    REACH.append(
        sorted({(i + a, k + b) for i, k in REACH[-1] for a, b in ((1, 0), (-1, 0), (0, 1), (0, -1))})
    )


def matching(axis, first):
    count = lax.axis_size(axis)
    pairs = [(i, i + 1) for i in range(first, count - 1, 2)]
    return pairs + [(b, a) for a, b in pairs]


def swap(x, axis, first):
    return lax.ppermute(x, axis, matching(axis, first))


def ends(x, dim, width, even):
    size = x.shape[dim]
    to_first = lax.dynamic_slice_in_dim(x, jnp.where(even, size - width, 0), width, dim)
    to_second = lax.dynamic_slice_in_dim(x, jnp.where(even, 0, size - width), width, dim)
    return to_first, to_second


def flip(x, axis, mask):
    count = lax.axis_size(axis)
    return lax.ppermute(x, axis, [(i, i ^ mask) for i in range(count)])


def collect(x, axis):
    count = lax.axis_size(axis)
    if count not in (2, 4, 8):
        return [lax.all_gather(x, axis)]
    far = {m: flip(x, axis, m) for m in range(2, count, 2)}
    peers = {1: flip(x, axis, 1)}
    for m, value in far.items():
        peers[m] = value
        peers[m + 1] = flip(value, axis, 1)
    return [peers[m] for m in sorted(peers)]


def shift_i(x, step):
    rows = x.shape[0]
    return pltpu.roll(x, (-step) % rows, 0)


def shift_k(x, step):
    lanes = x.shape[1]
    return pltpu.roll(x, (-step) % lanes, 1)


def edge_k(x, step):
    lane = lax.broadcasted_iota(jnp.int32, x.shape, 1)
    edge = x.shape[1] - 1 if step > 0 else 0
    return jnp.where(lane == edge, 0.0, shift_k(x, step))


def move(x, step):
    return shift_i(x, step[0]) if step[0] else edge_k(x, step[1])


def couple(x):
    return (shift_i(x, 1) + shift_i(x, -1)) + (edge_k(x, 1) + edge_k(x, -1))


def row_valid(rows, lanes):
    own = rows - 2 * SWEEPS
    place = lax.axis_index("bx")
    above = jnp.where(place < lax.axis_size("bx") - 1, SWEEPS - 1, 0)
    below = jnp.where(place > 0, SWEEPS - 1, 0)
    row = lax.broadcasted_iota(jnp.int32, (rows, lanes), 0)
    inside = (row < own + above) | (row >= rows - below)
    return jnp.where(inside, 1.0, 0.0).astype(F32)


def maps_kernel(decay_ref, mask_ref, first_ref, second_ref, rate_ref, map_ref, *, rows, nj):
    lanes = decay_ref.shape[-1]
    own = rows - 2 * SWEEPS
    wide = SWEEPS - 1
    rate_ref[0 : own * nj, :] = (
        (1 - mask_ref[...]).astype(F32) * decay_ref[...]
    ).reshape(own * nj, lanes)
    even = lax.axis_index("bx") % 2 == 0
    first = first_ref[...].reshape(wide * nj, lanes)
    second = second_ref[...].reshape(wide * nj, lanes)
    rate_ref[own * nj : (own + wide) * nj, :] = jnp.where(even, first, second)
    rate_ref[(own + wide) * nj : (rows - wide) * nj, :] = jnp.zeros((2 * nj, lanes), F32)
    rate_ref[(rows - wide) * nj : rows * nj, :] = jnp.where(even, second, first)

    valid = row_valid(rows, lanes)
    coef = [{o: None for o in REACH[d]} for d in range(SWEEPS)]
    for j in range(nj - 1, -1, -1):
        rate = rate_ref[pl.ds(j, rows, stride=nj), :]
        gain = KAPPA * (valid - rate)
        old = coef[0][(0, 0)]
        coef[0][(0, 0)] = rate if old is None else rate * old
        for d in range(1, SWEEPS):
            n = own if d == SWEEPS - 1 else rows
            total = {o: None for o in REACH[d]}
            for o, c in coef[d - 1].items():
                for step in ((1, 0), (-1, 0), (0, 1), (0, -1)):
                    moved = move(c, step)[:n]
                    goal = (o[0] + step[0], o[1] + step[1])
                    total[goal] = moved if total[goal] is None else total[goal] + moved
            for o in REACH[d]:
                fresh = gain[:n] * total[o]
                old = coef[d][o]
                coef[d][o] = fresh if old is None else rate[:n] * old + fresh
    at = 0
    for d in range(SWEEPS):
        for o in REACH[d]:
            c = coef[d][o]
            for part in range(c.shape[0] // own):
                map_ref[at] = c[part * own : (part + 1) * own]
                at += 1


def map_slots(rows, own):
    slots, at = {}, 0
    for d in range(SWEEPS):
        n = 1 if d == SWEEPS - 1 else rows // own
        for o in REACH[d]:
            slots[d, o] = (at, n)
            at += n
    return slots, at


def sweeps(v_ref, rate_ref, valid, state, rows, own, nj, emit):
    comps = v_ref.shape[0]
    for j in range(nj - 1, -1, -1):
        rate = rate_ref[pl.ds(j, rows, stride=nj), :]
        rest = valid - rate
        base = [v_ref[c, pl.ds(j, rows, stride=nj), :] for c in range(comps)]
        before = base
        for s in range(SWEEPS):
            n = own if s == SWEEPS - 1 else rows
            now = []
            for c in range(comps):
                source = base[c][:n] + KAPPA * couple(before[c])[:n]
                new = rest[:n] * source
                if state[s][c] is not None:
                    new = new + rate[:n] * state[s][c]
                now.append(new)
            state[s] = now
            before = now
        if emit is not None:
            emit(j, state[SWEEPS - 1])
    return state


def offsets_kernel(
    flow_ref, adj_ref, first_ref, second_ref, jfirst_ref, jsecond_ref, cfirst_ref, csecond_ref,
    rate_ref, v_ref, off_ref, halo_ref, line_ref, *, rows, nj,
):
    lanes = flow_ref.shape[-1]
    own = rows - 2 * SWEEPS
    w = SWEEPS
    even = lax.axis_index("bx") % 2 == 0
    jeven = lax.axis_index("by") % 2 == 0
    place, count = lax.axis_index("bx"), lax.axis_size("bx")
    one, two = first_ref[...], second_ref[...]
    halo_ref[0] = jnp.where(even, one, two)
    halo_ref[1] = jnp.where(even, two, one)
    a, b = jfirst_ref[...], jsecond_ref[...]
    c, d = cfirst_ref[...], csecond_ref[...]
    line_ref[0, :, 0:own, :] = jnp.where(jeven, b, a)
    line_ref[1, :, 0:own, :] = jnp.where(jeven, a, b)
    line_ref[:, :, own : own + w, :] = jnp.where(even, c, d)
    line_ref[:, :, own + w : rows, :] = jnp.where(even, d, c)

    sub = lax.broadcasted_iota(jnp.int32, (nj, lanes), 0)

    def adjoint_at(comp, i):
        if 0 <= i < own:
            return adj_ref[comp, i]
        if i >= own:
            return halo_ref[0, comp * (w + 1) + i - own]
        return halo_ref[1, comp * (w + 1) + (w + 1) + i]

    def flow_at(comp, i):
        if 0 <= i < own:
            return flow_ref[comp, i]
        base = 5 * (w + 1) + comp * w
        if i >= own:
            return halo_ref[0, base + i - own]
        return halo_ref[1, base + w + i]

    for row in range(rows):
        i = row if row < own + w else row - rows
        jump = []
        for comp in range(5):
            here = adjoint_at(comp, i)
            diff = adjoint_at(comp, i - 1) - adjoint_at(comp, i + 1)
            back = jnp.where(sub == 0, line_ref[0, comp, row : row + 1, :], pltpu.roll(here, 1, 0))
            ahead = jnp.where(
                sub == nj - 1, line_ref[1, comp, row : row + 1, :], pltpu.roll(here, nj - 1, 0)
            )
            jump.append(diff + (back - ahead) + (edge_k(here, -1) - edge_k(here, 1)))
        rho = flow_at(0, i)
        m = [flow_at(comp, i) for comp in (1, 2, 3)]
        energy = flow_at(4, i)
        inv = 1.0 / rho
        u = [x * inv for x in m]
        mu = m[0] * u[0] + m[1] * u[1] + m[2] * u[2]
        pressure = GAS * (energy - 0.5 * mu)
        q = (
            rho * jump[0]
            + (m[0] * jump[1] + m[1] * jump[2] + m[2] * jump[3])
            + (energy + pressure) * jump[4]
        )
        for comp in range(3):
            value = 0.5 * (u[comp] * q + pressure * jump[comp + 1])
            if i >= own:
                value = jnp.where(place < count - 1, value, 0.0)
            elif i < 0:
                value = jnp.where(place > 0, value, 0.0)
            v_ref[comp, row * nj : (row + 1) * nj, :] = value

    valid = row_valid(rows, lanes)
    state = [[None] * 3 for _ in range(SWEEPS)]
    state = sweeps(v_ref, rate_ref, valid, state, rows, own, nj, None)
    at = 0
    for s in range(SWEEPS):
        for comp in range(3):
            x = state[s][comp]
            for part in range(x.shape[0] // own):
                off_ref[at] = x[part * own : (part + 1) * own]
                at += 1


def finish_kernel(*refs, rows, nj, count, stacked):
    own = rows - 2 * SWEEPS
    if stacked:
        v_ref, rate_ref, map_ref, off_ref, out_ref, x_ref = refs
    else:
        v_ref, rate_ref = refs[:2]
        maps = refs[2 : 2 + count - 1]
        offs = refs[1 + count : 2 * count]
        out_ref, x_ref, map_ref, off_ref = refs[2 * count :]
    lanes = v_ref.shape[-1]
    me = lax.axis_index("by")
    if not stacked:
        for mask in range(1, count):
            map_ref[me ^ mask] = maps[mask - 1][...]
            off_ref[me ^ mask] = offs[mask - 1][...]
    slots, _ = map_slots(rows, own)

    def load(ref, block, at, n):
        if n == 1:
            return ref[block, at]
        return jnp.concatenate([ref[block, at + part] for part in range(n)], axis=0)

    sizes = [rows // own] * (SWEEPS - 1) + [1]
    starts, at = {}, 0
    for s in range(SWEEPS):
        for comp in range(3):
            starts[s, comp] = at
            at += sizes[s]
    x_ref[...] = jnp.zeros(x_ref.shape, F32)

    def get(s, comp):
        a = starts[s, comp]
        return jnp.concatenate([x_ref[a + part] for part in range(sizes[s])], axis=0)

    def put(s, comp, value):
        for part in range(sizes[s]):
            x_ref[starts[s, comp] + part] = value[part * own : (part + 1) * own]

    def through(hop, carry):
        block = count - 1 - hop
        coef = {key: load(map_ref, block, *slot) for key, slot in slots.items()}
        fresh = {}
        for comp in range(3):
            x = [get(s, comp) for s in range(SWEEPS)]
            total = [load(off_ref, block, starts[s, comp], sizes[s]) for s in range(SWEEPS)]
            for s in range(SWEEPS):
                for o in sorted({o for d in range(SWEEPS - s) for o in REACH[d]}):
                    moved = x[s]
                    if o[0]:
                        moved = shift_i(moved, o[0])
                    if o[1]:
                        moved = shift_k(moved, o[1])
                    for d in range(SWEEPS - s):
                        if o in REACH[d]:
                            n = sizes[s + d] * own
                            total[s + d] = total[s + d] + coef[d, o][:n] * moved[:n]
            for s in range(SWEEPS):
                fresh[s, comp] = total[s]
        for (s, comp), value in fresh.items():
            put(s, comp, value)
        return carry

    lax.fori_loop(0, count - 1 - me, through, 0)

    valid = row_valid(rows, lanes)
    state = [[get(s, comp) for comp in range(3)] for s in range(SWEEPS)]

    def emit(j, values):
        for comp in range(3):
            out_ref[comp, pl.ds(j, own, stride=nj), :] = values[comp]

    sweeps(v_ref, rate_ref, valid, state, rows, own, nj, emit)


def product_kernel(
    flow_ref, adj_ref, faces_ref, first_ref, second_ref, jfirst_ref, jsecond_ref, out_ref, *, nj,
):
    own, lanes = flow_ref.shape[1], flow_ref.shape[-1]
    w = SWEEPS
    even = lax.axis_index("bx") % 2 == 0
    jeven = lax.axis_index("by") % 2 == 0
    sub = lax.broadcasted_iota(jnp.int32, (nj, lanes), 0)
    for i in range(own):
        here = [adj_ref[comp, i] for comp in range(5)]

        def beside(comp, face):
            if face == 0:
                if i + 1 < own:
                    return adj_ref[comp, i + 1]
                at = comp * (w + 1)
                return jnp.where(even, first_ref[at], second_ref[at])
            if face == 1:
                if i > 0:
                    return adj_ref[comp, i - 1]
                at = comp * (w + 1) + w
                return jnp.where(even, second_ref[at], first_ref[at])
            if face in (2, 3):
                one = jfirst_ref[comp, i : i + 1, :]
                two = jsecond_ref[comp, i : i + 1, :]
                if face == 2:
                    line = jnp.where(jeven, one, two)
                    return jnp.where(sub == nj - 1, line, pltpu.roll(here[comp], nj - 1, 0))
                line = jnp.where(jeven, two, one)
                return jnp.where(sub == 0, line, pltpu.roll(here[comp], 1, 0))
            return edge_k(here[comp], 1 if face == 4 else -1)

        rho = flow_ref[0, i]
        m = [flow_ref[comp, i] for comp in (1, 2, 3)]
        energy = flow_ref[4, i]
        inv = 1.0 / rho
        u = [x * inv for x in m]
        uu = u[0] * u[0] + u[1] * u[1] + u[2] * u[2]
        pressure = GAS * (energy - 0.5 * (rho * uu))
        enthalpy = (energy + pressure) * inv
        sound = jnp.sqrt((1.0 + GAS) * pressure * inv)
        total = None
        for face in range(6):
            s = [faces_ref[face, axis, i] for axis in range(3)]
            h = [0.5 * (here[comp] - beside(comp, face)) for comp in range(5)]
            speed = u[0] * s[0] + u[1] * s[1] + u[2] * s[2]
            area = jnp.sqrt(s[0] * s[0] + s[1] * s[1] + s[2] * s[2])
            wave = jnp.abs(speed) + sound * area
            bulk = (u[0] * h[1] + u[1] * h[2] + u[2] * h[3]) + enthalpy * h[4]
            press = (s[0] * h[1] + s[1] * h[2] + s[2] * h[3]) + speed * h[4]
            full = h[0] + bulk
            term = [
                0.5 * GAS * (uu * press) - speed * bulk + wave * h[0],
                s[0] * full - GAS * (u[0] * press) + (speed + wave) * h[1],
                s[1] * full - GAS * (u[1] * press) + (speed + wave) * h[2],
                s[2] * full - GAS * (u[2] * press) + (speed + wave) * h[3],
                GAS * press + (speed + wave) * h[4],
            ]
            total = term if total is None else [a + b for a, b in zip(total, term)]
        for comp in range(5):
            out_ref[comp, i] = total[comp]


def call(kernel, out_shape, args, scratch=(), interpret=False):
    vmem = pl.BlockSpec(memory_space=pltpu.VMEM)
    single = not isinstance(out_shape, (list, tuple))
    held = [*args, *([out_shape] if single else out_shape), *scratch]
    need = sum(4 * math.prod(a.shape) for a in held)
    return pl.pallas_call(
        kernel,
        out_shape=out_shape,
        in_specs=[vmem] * len(args),
        out_specs=vmem if single else [vmem] * len(out_shape),
        scratch_shapes=list(scratch),
        interpret=interpret,
        compiler_params=pltpu.CompilerParams(vmem_limit_bytes=need + (2 << 20)),
    )(*args)


INTERPRET = False


def on_device(flow, adjoint, faces, decay, surface_mask):
    own, nj, lanes = decay.shape
    w = SWEEPS
    rows = own + 2 * w
    nby = lax.axis_size("by")
    bx, by = lax.axis_index("bx"), lax.axis_index("by")
    even, jeven = bx % 2 == 0, by % 2 == 0

    def run(*args):
        return call(*args, interpret=INTERPRET)


    retention = (1 - surface_mask).astype(F32) * decay
    r1, r2 = ends(retention, 0, w - 1, even)
    r1, r2 = swap(r1, "bx", 0), swap(r2, "bx", 1)
    a1, a2 = ends(adjoint, 1, w + 1, even)
    f1, f2 = ends(flow, 1, w, even)

    def pack(a, f):
        return jnp.concatenate(
            [a.reshape(5 * (w + 1), nj, lanes), f.reshape(5 * w, nj, lanes)], axis=0
        )

    m1, m2 = swap(pack(a1, f1), "bx", 0), swap(pack(a2, f2), "bx", 1)
    l1, l2 = ends(adjoint, 2, 1, jeven)
    l1 = swap(l1.reshape(5, own, lanes), "by", 0)
    l2 = swap(l2.reshape(5, own, lanes), "by", 1)
    below, above = jnp.where(jeven, l2, l1), jnp.where(jeven, l1, l2)
    c1, c2 = ends(jnp.stack([below, above]), 2, w, even)
    c1, c2 = swap(c1, "bx", 0), swap(c2, "bx", 1)

    _, n_map = map_slots(rows, own)
    rate, maps = run(
        functools.partial(maps_kernel, rows=rows, nj=nj),
        [
            jax.ShapeDtypeStruct((rows * nj, lanes), F32),
            jax.ShapeDtypeStruct((n_map, own, lanes), F32),
        ],
        [decay, surface_mask, r1, r2],
    )
    all_maps = collect(maps, "by")

    n_off = 3 * ((SWEEPS - 1) * (rows // own) + 1)
    v, offs = run(
        functools.partial(offsets_kernel, rows=rows, nj=nj),
        [
            jax.ShapeDtypeStruct((3, rows * nj, lanes), F32),
            jax.ShapeDtypeStruct((n_off, own, lanes), F32),
        ],
        [flow, adjoint, m1, m2, l1, l2, c1, c2, rate],
        [
            pltpu.VMEM((2, 5 * (2 * w + 1), nj, lanes), F32),
            pltpu.VMEM((2, 5, rows, lanes), F32),
        ],
    )
    all_offs = collect(offs, "by")

    product = run(
        functools.partial(product_kernel, nj=nj),
        jax.ShapeDtypeStruct(flow.shape, F32),
        [flow, adjoint, faces, m1, m2, l1, l2],
    )

    stacked = len(all_maps) == 1 and nby != 2
    scratch = [pltpu.VMEM((n_off, own, lanes), F32)]
    if not stacked:
        scratch += [
            pltpu.VMEM((nby, n_map, own, lanes), F32),
            pltpu.VMEM((nby, n_off, own, lanes), F32),
        ]
    warp = run(
        functools.partial(finish_kernel, rows=rows, nj=nj, count=nby, stacked=stacked),
        jax.ShapeDtypeStruct((3, own * nj, lanes), F32),
        [v, rate, *all_maps, *all_offs],
        scratch,
    )
    return (product, warp.reshape(3, own, nj, lanes))


def solution(mesh):
    return jax.shard_map(
        on_device,
        mesh=mesh,
        in_specs=(
            P(None, "bx", "by", None),
            P(None, "bx", "by", None),
            P(None, None, "bx", "by", None),
            P("bx", "by", None),
            P("bx", "by", None),
        ),
        out_specs=(P(None, "bx", "by", None), P(None, "bx", "by", None)),
        check_vma=False,
    )
```

profile of v0, /device:TPU:8, one launch (start us, length us, event | category | flops | bytes accessed | tf_op | source)
XLA Modules:
  0.0 56.7 jit_solution(9930627256053811878)
XLA Ops:
  0.7 1.0 %constant_dynamic-slice_fusion.4 = (f32[5,4,16,128]{3,2,1,0:T(8,128)S(1)}, f32[5,4,16,128]{3,2,1,0:T(8,128)S(1)}) fusion(f32[5,8,16,128]{3,2,1,0:T(8,128)} %flow_ref.3, s32[]{:T(128)S(6)} %select_n.64, s32[]{:T(128)S(6)} %select_n.62), kind=kLoop, calls=%fused_computation.15 | loop fusion | bytes 655368 | tf_op jit(solution)/shard_map/dynamic_slice | solution.py:37
  1.7 0.0 copy-start
  1.7 0.0 copy-start.3
  1.7 0.0 copy-start.4
  1.7 1.1 %constant_dynamic-slice_fusion.5 = (f32[5,5,16,128]{3,2,1,0:T(8,128)S(1)}, f32[5,5,16,128]{3,2,1,0:T(8,128)S(1)}) fusion(f32[5,8,16,128]{3,2,1,0:T(8,128)} %adj_ref.3, s32[]{:T(128)S(6)} %select_n.63, s32[]{:T(128)S(6)} %select_n.61), kind=kLoop, calls=%fused_computation.16 | loop fusion | bytes 819208 | tf_op jit(solution)/shard_map/dynamic_slice | solution.py:37
  2.8 0.0 copy-start.1
  2.9 0.1 collective-permute-start
  3.0 5.0 %collective-permute-start.1 = (f32[45,16,128]{2,1,0:T(8,128)S(1)}, f32[45,16,128]{2,1,0:T(8,128)S(1)}, u32[]{:S(2)}, u32[]{:S(2)}) collective-permute-start(f32[45,16,128]{2,1,0:T(8,128)S(1)} %pad_maximum_fusion.1), channel_id=1, source_target_pairs={{8,16},{16,8},{9,17},{17,9},{10,18},{18,10},{11,19},{19,11},{12,20... | collective-permute-start | bytes 1105928 | tf_op jit(solution)/shard_map/ppermute | solution.py:31
  8.1 0.0 copy-done
  8.1 0.0 copy-start.2
  8.1 0.1 collective-permute-start.2
  8.2 0.8 %collective-permute-start.3 = (f32[5,8,128]{2,1,0:T(8,128)S(1)}, f32[5,8,128]{2,1,0:T(8,128)S(1)}, u32[]{:S(2)}, u32[]{:S(2)}) collective-permute-start(f32[5,8,128]{2,1,0:T(8,128)S(1)} %bitcast.16), channel_id=1, source_target_pairs={{1,2},{3,4},{5,6},{2,1},{4,3},{6,5},{9,10},{11,12},{13,14},{10,9},... | collective-permute-start | bytes 61448 | tf_op jit(solution)/shard_map/ppermute | solution.py:31
  9.0 0.0 copy-done.3
  9.0 0.0 copy-done.4
  9.1 0.1 collective-permute-start.6
  9.2 0.2 collective-permute-done.2.jfirst_ref
  9.4 1.9 %collective-permute-start.7 = (f32[3,16,128]{2,1,0:T(8,128)S(1)}, f32[3,16,128]{2,1,0:T(8,128)S(1)}, u32[]{:S(2)}, u32[]{:S(2)}) collective-permute-start(f32[3,16,128]{2,1,0:T(8,128)S(1)} %get-tuple-element.16), channel_id=1, source_target_pairs={{8,16},{16,8},{9,17},{17,9},{10,18},{18,10},{11,19},{19,11},{12,20... | collective-permute-start | bytes 73736 | tf_op jit(solution)/shard_map/ppermute | solution.py:31
  11.3 0.0 collective-permute-done.3.jsecond_ref
  11.3 2.2 %collective-permute-done.6.first_ref = f32[3,16,128]{2,1,0:T(8,128)S(1)} collective-permute-done((f32[3,16,128]{2,1,0:T(8,128)S(1)}, f32[3,16,128]{2,1,0:T(8,128)S(1)}, u32[]{:S(2)}, u32[]{:S(2)}) %collective-permute-start.6) | collective-permute-done | bytes 24608 | tf_op jit(solution)/shard_map/ppermute | solution.py:31
  13.5 3.1 %collective-permute-done.7.second_ref = f32[3,16,128]{2,1,0:T(8,128)S(1)} collective-permute-done((f32[3,16,128]{2,1,0:T(8,128)S(1)}, f32[3,16,128]{2,1,0:T(8,128)S(1)}, u32[]{:S(2)}, u32[]{:S(2)}) %collective-permute-start.7) | collective-permute-done | bytes 24608 | tf_op jit(solution)/shard_map/ppermute | solution.py:31
  16.7 2.1 %shard_map.69 = (f32[256,128]{1,0:T(8,128)S(1)}, f32[44,8,128]{2,1,0:T(8,128)S(1)}) custom-call(f32[8,16,128]{2,1,0:T(8,128)S(1)} %copy-done.3, s32[8,16,128]{2,1,0:T(8,128)S(1)} %copy-done.4, f32[3,16,128]{2,1,0:T(8,128)S(1)} %collective-permute-done.6.first_ref, f32[3,16,128]{2,1,0:T(8,128)S(1)} %collective-permute-done.7.second_ref), custom_call_target="tpu_custom_call" | custom-call | tf_op jit(solution)/shard_map/pallas_call | solution.py:389
  18.8 1.6 %collective-permute-start.9 = (f32[44,8,128]{2,1,0:T(8,128)S(1)}, f32[44,8,128]{2,1,0:T(8,128)S(1)}, u32[]{:S(2)}, u32[]{:S(2)}) collective-permute-start(f32[44,8,128]{2,1,0:T(8,128)S(1)} %get-tuple-element.8), channel_id=1, source_target_pairs={{0,2},{1,3},{2,0},{3,1},{4,6},{5,7},{6,4},{7,5},{8,10},{9,11},{10,... | collective-permute-start | bytes 540680 | tf_op jit(solution)/shard_map/ppermute | solution.py:43
  20.4 1.6 %collective-permute-start.11 = (f32[44,8,128]{2,1,0:T(8,128)S(1)}, f32[44,8,128]{2,1,0:T(8,128)S(1)}, u32[]{:S(2)}, u32[]{:S(2)}) collective-permute-start(f32[44,8,128]{2,1,0:T(8,128)S(1)} %get-tuple-element.8), channel_id=1, source_target_pairs={{0,4},{1,5},{2,6},{3,7},{4,0},{5,1},{6,2},{7,3},{8,12},{9,13},{10,... | collective-permute-start | bytes 540680 | tf_op jit(solution)/shard_map/ppermute | solution.py:43
  22.0 0.1 collective-permute-start.4
  22.1 3.8 %collective-permute-done.4.cfirst_ref = f32[2,5,4,128]{3,2,1,0:T(4,128)S(1)} collective-permute-done((f32[2,5,4,128]{3,2,1,0:T(4,128)S(1)}, f32[2,5,4,128]{3,2,1,0:T(4,128)S(1)}, u32[]{:S(2)}, u32[]{:S(2)}) %collective-permute-start.4) | collective-permute-done | bytes 20512 | tf_op jit(solution)/shard_map/ppermute | solution.py:31
  25.9 3.6 %collective-permute-start.5 = (f32[2,5,4,128]{3,2,1,0:T(4,128)S(1)}, f32[2,5,4,128]{3,2,1,0:T(4,128)S(1)}, u32[]{:S(2)}, u32[]{:S(2)}) collective-permute-start(f32[2,5,4,128]{3,2,1,0:T(4,128)S(1)} %get-tuple-element.18), channel_id=1, source_target_pairs={{8,16},{16,8},{9,17},{17,9},{10,18},{18,10},{11,19},{19,11},{12,20... | collective-permute-start | bytes 61448 | tf_op jit(solution)/shard_map/ppermute | solution.py:31
  29.5 2.0 %collective-permute-done.5.csecond_ref = f32[2,5,4,128]{3,2,1,0:T(4,128)S(1)} collective-permute-done((f32[2,5,4,128]{3,2,1,0:T(4,128)S(1)}, f32[2,5,4,128]{3,2,1,0:T(4,128)S(1)}, u32[]{:S(2)}, u32[]{:S(2)}) %collective-permute-start.5) | collective-permute-done | bytes 20512 | tf_op jit(solution)/shard_map/ppermute | solution.py:31
  31.5 0.6 %collective-permute-start.13 = (f32[44,8,128]{2,1,0:T(8,128)S(1)}, f32[44,8,128]{2,1,0:T(8,128)S(1)}, u32[]{:S(2)}, u32[]{:S(2)}) collective-permute-start(f32[44,8,128]{2,1,0:T(8,128)S(1)} %get-tuple-element.8), channel_id=1, source_target_pairs={{0,6},{1,7},{2,4},{3,5},{4,2},{5,3},{6,0},{7,1},{8,14},{9,15},{10,... | collective-permute-start | bytes 540680 | tf_op jit(solution)/shard_map/ppermute | solution.py:43
  32.2 0.0 collective-permute-done.9.refs_3_
  32.2 0.0 collective-permute-start.8
  32.2 0.0 collective-permute-done.11.refs_5_
  32.2 0.5 collective-permute-start.10
  32.7 5.2 %collective-permute-done.13.refs_7_ = f32[44,8,128]{2,1,0:T(8,128)S(1)} collective-permute-done((f32[44,8,128]{2,1,0:T(8,128)S(1)}, f32[44,8,128]{2,1,0:T(8,128)S(1)}, u32[]{:S(2)}, u32[]{:S(2)}) %collective-permute-start.13) | collective-permute-done | bytes 180256 | tf_op jit(solution)/shard_map/ppermute | solution.py:43
  37.9 0.0 collective-permute-start.12
  37.9 0.0 collective-permute-done.first_ref
  37.9 0.5 collective-permute-start.14
  38.5 0.0 collective-permute-done.1.second_ref
  38.5 0.0 copy-done.1
  38.5 3.7 %shard_map.70 = (f32[3,256,128]{2,1,0:T(8,128)S(1)}, f32[21,8,128]{2,1,0:T(8,128)S(1)}) custom-call(f32[5,8,16,128]{3,2,1,0:T(8,128)S(1)} %copy-done.1, f32[5,8,16,128]{3,2,1,0:T(8,128)S(1)} %copy-done, f32[45,16,128]{2,1,0:T(8,128)S(1)} %collective-permute-done.first_ref, f32[45,16,128]{2,1,0:T(8,128)S(1)} %collective-permute-done.1.second_ref, ...), custom_call_target="tpu_custom_call" | custom-call | tf_op jit(solution)/shard_map/pallas_call | solution.py:389
  42.2 1.3 %collective-permute-start.16 = (f32[21,8,128]{2,1,0:T(8,128)S(1)}, f32[21,8,128]{2,1,0:T(8,128)S(1)}, u32[]{:S(2)}, u32[]{:S(2)}) collective-permute-start(f32[21,8,128]{2,1,0:T(8,128)S(1)} %get-tuple-element.9), channel_id=1, source_target_pairs={{0,2},{1,3},{2,0},{3,1},{4,6},{5,7},{6,4},{7,5},{8,10},{9,11},{10,... | collective-permute-start | bytes 258056 | tf_op jit(solution)/shard_map/ppermute | solution.py:43
  43.5 0.0 collective-permute-done.8.refs_2_
  43.5 0.0 collective-permute-start.18
  43.5 0.0 collective-permute-done.10.refs_4_
  43.5 2.3 %collective-permute-start.20 = (f32[21,8,128]{2,1,0:T(8,128)S(1)}, f32[21,8,128]{2,1,0:T(8,128)S(1)}, u32[]{:S(2)}, u32[]{:S(2)}) collective-permute-start(f32[21,8,128]{2,1,0:T(8,128)S(1)} %get-tuple-element.9), channel_id=1, source_target_pairs={{0,6},{1,7},{2,4},{3,5},{4,2},{5,3},{6,0},{7,1},{8,14},{9,15},{10,... | collective-permute-start | bytes 258056 | tf_op jit(solution)/shard_map/ppermute | solution.py:43
  45.8 0.0 collective-permute-done.12.refs_6_
  45.8 0.0 collective-permute-start.15
  45.8 1.0 %collective-permute-done.16.refs_10_ = f32[21,8,128]{2,1,0:T(8,128)S(1)} collective-permute-done((f32[21,8,128]{2,1,0:T(8,128)S(1)}, f32[21,8,128]{2,1,0:T(8,128)S(1)}, u32[]{:S(2)}, u32[]{:S(2)}) %collective-permute-start.16) | collective-permute-done | bytes 86048 | tf_op jit(solution)/shard_map/ppermute | solution.py:43
  46.7 0.0 collective-permute-start.17
  46.7 2.8 %collective-permute-done.18.refs_12_ = f32[21,8,128]{2,1,0:T(8,128)S(1)} collective-permute-done((f32[21,8,128]{2,1,0:T(8,128)S(1)}, f32[21,8,128]{2,1,0:T(8,128)S(1)}, u32[]{:S(2)}, u32[]{:S(2)}) %collective-permute-start.18) | collective-permute-done | bytes 86048 | tf_op jit(solution)/shard_map/ppermute | solution.py:43
  49.5 0.0 collective-permute-start.19
  49.5 0.0 collective-permute-done.20.refs_14_
  49.5 0.5 collective-permute-start.21
  50.0 0.0 copy-done.2
  50.0 1.9 %shard_map.68 = f32[5,8,16,128]{3,2,1,0:T(8,128)} custom-call(f32[5,8,16,128]{3,2,1,0:T(8,128)S(1)} %copy-done.1, f32[5,8,16,128]{3,2,1,0:T(8,128)S(1)} %copy-done, f32[6,3,8,16,128]{4,3,2,1,0:T(8,128)S(1)} %copy-done.2, f32[45,16,128]{2,1,0:T(8,128)S(1)} %collective-permute-done.first_ref, f32[45,16,128]{2,1,0:T(8,128)S(1)} %collective-permute-done.1.second_ref, ...), custom_call_target="tpu_custom_call" | custom-call | tf_op jit(solution)/shard_map/pallas_call | solution.py:389
  51.9 0.0 collective-permute-done.14.refs_8_
  51.9 0.0 collective-permute-done.15.refs_9_
  52.0 0.0 collective-permute-done.17.refs_11_
  52.0 0.0 collective-permute-done.19.refs_13_
  52.0 0.0 collective-permute-done.21.refs_15_
  52.0 4.7 %shard_map.71 = f32[3,128,128]{2,1,0:T(8,128)} custom-call(f32[3,256,128]{2,1,0:T(8,128)S(1)} %get-tuple-element.7.refs_0_, f32[256,128]{1,0:T(8,128)S(1)} %get-tuple-element.6.rate_ref.refs_1_, f32[44,8,128]{2,1,0:T(8,128)S(1)} %collective-permute-done.8.refs_2_, f32[44,8,128]{2,1,0:T(8,128)S(1)} %collective-permute-done.9.refs_3_, ...), custom_call_target="tpu_custom_call" | custom-call | tf_op jit(solution)/shard_map/pallas_call | solution.py:389
  (7 shorter events, 0.1 us)
Async XLA Ops:
  1.7 6.4 %copy-start = (f32[5,8,16,128]{3,2,1,0:T(8,128)S(1)}, f32[5,8,16,128]{3,2,1,0:T(8,128)}, u32[]{:S(2)}) copy-start(f32[5,8,16,128]{3,2,1,0:T(8,128)} %adj_ref.3) | copy-start | bytes 983044
  1.7 7.3 %copy-start.3 = (f32[8,16,128]{2,1,0:T(8,128)S(1)}, f32[8,16,128]{2,1,0:T(8,128)}, u32[]{:S(2)}) copy-start(f32[8,16,128]{2,1,0:T(8,128)} %decay_ref.1) | copy-start | bytes 196612
  1.7 7.3 %copy-start.4 = (s32[8,16,128]{2,1,0:T(8,128)S(1)}, s32[8,16,128]{2,1,0:T(8,128)}, u32[]{:S(2)}) copy-start(s32[8,16,128]{2,1,0:T(8,128)} %mask_ref.1) | copy-start | bytes 196612
  2.8 35.6 %copy-start.1 = (f32[5,8,16,128]{3,2,1,0:T(8,128)S(1)}, f32[5,8,16,128]{3,2,1,0:T(8,128)}, u32[]{:S(2)}) copy-start(f32[5,8,16,128]{3,2,1,0:T(8,128)} %flow_ref.3) | copy-start | bytes 983044
  2.9 35.1 %collective-permute-start = (f32[45,16,128]{2,1,0:T(8,128)S(1)}, f32[45,16,128]{2,1,0:T(8,128)S(1)}, u32[]{:S(2)}, u32[]{:S(2)}) collective-permute-start(f32[45,16,128]{2,1,0:T(8,128)S(1)} %pad_maximum_fusion), channel_id=1, source_target_pairs={{0,8},{16,24},{8,0},{24,16},{1,9},{17,25},{9,1},{25,17},{2,10},{18... | collective-permute-start | bytes 1105928 | tf_op jit(solution)/shard_map/ppermute | solution.py:31
  3.0 35.5 %collective-permute-start.1 = (f32[45,16,128]{2,1,0:T(8,128)S(1)}, f32[45,16,128]{2,1,0:T(8,128)S(1)}, u32[]{:S(2)}, u32[]{:S(2)}) collective-permute-start(f32[45,16,128]{2,1,0:T(8,128)S(1)} %pad_maximum_fusion.1), channel_id=1, source_target_pairs={{8,16},{16,8},{9,17},{17,9},{10,18},{18,10},{11,19},{19,11},{12,20... | collective-permute-start | bytes 1105928 | tf_op jit(solution)/shard_map/ppermute | solution.py:31
  8.1 42.0 %copy-start.2 = (f32[6,3,8,16,128]{4,3,2,1,0:T(8,128)S(1)}, f32[6,3,8,16,128]{4,3,2,1,0:T(8,128)}, u32[]{:S(2)}) copy-start(f32[6,3,8,16,128]{4,3,2,1,0:T(8,128)} %faces_ref.1) | copy-start | bytes 3538948
  8.1 1.3 %collective-permute-start.2 = (f32[5,8,128]{2,1,0:T(8,128)S(1)}, f32[5,8,128]{2,1,0:T(8,128)S(1)}, u32[]{:S(2)}, u32[]{:S(2)}) collective-permute-start(f32[5,8,128]{2,1,0:T(8,128)S(1)} %bitcast.17), channel_id=1, source_target_pairs={{0,1},{2,3},{4,5},{6,7},{1,0},{3,2},{5,4},{7,6},{8,9},{10,11},{12,... | collective-permute-start | bytes 61448 | tf_op jit(solution)/shard_map/ppermute | solution.py:31
  8.2 3.1 %collective-permute-start.3 = (f32[5,8,128]{2,1,0:T(8,128)S(1)}, f32[5,8,128]{2,1,0:T(8,128)S(1)}, u32[]{:S(2)}, u32[]{:S(2)}) collective-permute-start(f32[5,8,128]{2,1,0:T(8,128)S(1)} %bitcast.16), channel_id=1, source_target_pairs={{1,2},{3,4},{5,6},{2,1},{4,3},{6,5},{9,10},{11,12},{13,14},{10,9},... | collective-permute-start | bytes 61448 | tf_op jit(solution)/shard_map/ppermute | solution.py:31
  9.1 4.5 %collective-permute-start.6 = (f32[3,16,128]{2,1,0:T(8,128)S(1)}, f32[3,16,128]{2,1,0:T(8,128)S(1)}, u32[]{:S(2)}, u32[]{:S(2)}) collective-permute-start(f32[3,16,128]{2,1,0:T(8,128)S(1)} %get-tuple-element.17), channel_id=1, source_target_pairs={{0,8},{16,24},{8,0},{24,16},{1,9},{17,25},{9,1},{25,17},{2,10},{18... | collective-permute-start | bytes 73736 | tf_op jit(solution)/shard_map/ppermute | solution.py:31
  9.4 7.3 %collective-permute-start.7 = (f32[3,16,128]{2,1,0:T(8,128)S(1)}, f32[3,16,128]{2,1,0:T(8,128)S(1)}, u32[]{:S(2)}, u32[]{:S(2)}) collective-permute-start(f32[3,16,128]{2,1,0:T(8,128)S(1)} %get-tuple-element.16), channel_id=1, source_target_pairs={{8,16},{16,8},{9,17},{17,9},{10,18},{18,10},{11,19},{19,11},{12,20... | collective-permute-start | bytes 73736 | tf_op jit(solution)/shard_map/ppermute | solution.py:31
  18.8 13.4 %collective-permute-start.9 = (f32[44,8,128]{2,1,0:T(8,128)S(1)}, f32[44,8,128]{2,1,0:T(8,128)S(1)}, u32[]{:S(2)}, u32[]{:S(2)}) collective-permute-start(f32[44,8,128]{2,1,0:T(8,128)S(1)} %get-tuple-element.8), channel_id=1, source_target_pairs={{0,2},{1,3},{2,0},{3,1},{4,6},{5,7},{6,4},{7,5},{8,10},{9,11},{10,... | collective-permute-start | bytes 540680 | tf_op jit(solution)/shard_map/ppermute | solution.py:43
  20.4 11.8 %collective-permute-start.11 = (f32[44,8,128]{2,1,0:T(8,128)S(1)}, f32[44,8,128]{2,1,0:T(8,128)S(1)}, u32[]{:S(2)}, u32[]{:S(2)}) collective-permute-start(f32[44,8,128]{2,1,0:T(8,128)S(1)} %get-tuple-element.8), channel_id=1, source_target_pairs={{0,4},{1,5},{2,6},{3,7},{4,0},{5,1},{6,2},{7,3},{8,12},{9,13},{10,... | collective-permute-start | bytes 540680 | tf_op jit(solution)/shard_map/ppermute | solution.py:43
  22.0 3.8 %collective-permute-start.4 = (f32[2,5,4,128]{3,2,1,0:T(4,128)S(1)}, f32[2,5,4,128]{3,2,1,0:T(4,128)S(1)}, u32[]{:S(2)}, u32[]{:S(2)}) collective-permute-start(f32[2,5,4,128]{3,2,1,0:T(4,128)S(1)} %get-tuple-element.19), channel_id=1, source_target_pairs={{0,8},{16,24},{8,0},{24,16},{1,9},{17,25},{9,1},{25,17},{2,10},{18... | collective-permute-start | bytes 61448 | tf_op jit(solution)/shard_map/ppermute | solution.py:31
  25.9 5.7 %collective-permute-start.5 = (f32[2,5,4,128]{3,2,1,0:T(4,128)S(1)}, f32[2,5,4,128]{3,2,1,0:T(4,128)S(1)}, u32[]{:S(2)}, u32[]{:S(2)}) collective-permute-start(f32[2,5,4,128]{3,2,1,0:T(4,128)S(1)} %get-tuple-element.18), channel_id=1, source_target_pairs={{8,16},{16,8},{9,17},{17,9},{10,18},{18,10},{11,19},{19,11},{12,20... | collective-permute-start | bytes 61448 | tf_op jit(solution)/shard_map/ppermute | solution.py:31
  31.5 6.4 %collective-permute-start.13 = (f32[44,8,128]{2,1,0:T(8,128)S(1)}, f32[44,8,128]{2,1,0:T(8,128)S(1)}, u32[]{:S(2)}, u32[]{:S(2)}) collective-permute-start(f32[44,8,128]{2,1,0:T(8,128)S(1)} %get-tuple-element.8), channel_id=1, source_target_pairs={{0,6},{1,7},{2,4},{3,5},{4,2},{5,3},{6,0},{7,1},{8,14},{9,15},{10,... | collective-permute-start | bytes 540680 | tf_op jit(solution)/shard_map/ppermute | solution.py:43
  32.2 11.3 %collective-permute-start.8 = (f32[44,8,128]{2,1,0:T(8,128)S(1)}, f32[44,8,128]{2,1,0:T(8,128)S(1)}, u32[]{:S(2)}, u32[]{:S(2)}) collective-permute-start(f32[44,8,128]{2,1,0:T(8,128)S(1)} %get-tuple-element.8), channel_id=1, source_target_pairs={{0,1},{1,0},{2,3},{3,2},{4,5},{5,4},{6,7},{7,6},{8,9},{9,8},{10,11... | collective-permute-start | bytes 540680 | tf_op jit(solution)/shard_map/ppermute | solution.py:43
  32.2 11.3 %collective-permute-start.10 = (f32[44,8,128]{2,1,0:T(8,128)S(1)}, f32[44,8,128]{2,1,0:T(8,128)S(1)}, u32[]{:S(2)}, u32[]{:S(2)}) collective-permute-start(f32[44,8,128]{2,1,0:T(8,128)S(1)} %collective-permute-done.9.refs_3_), channel_id=1, source_target_pairs={{0,1},{1,0},{2,3},{3,2},{4,5},{5,4},{6,7},{7,6},{8,9},{9,8},{10,11... | collective-permute-start | bytes 540680 | tf_op jit(solution)/shard_map/ppermute | solution.py:43
  37.9 7.8 %collective-permute-start.12 = (f32[44,8,128]{2,1,0:T(8,128)S(1)}, f32[44,8,128]{2,1,0:T(8,128)S(1)}, u32[]{:S(2)}, u32[]{:S(2)}) collective-permute-start(f32[44,8,128]{2,1,0:T(8,128)S(1)} %collective-permute-done.11.refs_5_), channel_id=1, source_target_pairs={{0,1},{1,0},{2,3},{3,2},{4,5},{5,4},{6,7},{7,6},{8,9},{9,8},{10,11... | collective-permute-start | bytes 540680 | tf_op jit(solution)/shard_map/ppermute | solution.py:43
  37.9 14.0 %collective-permute-start.14 = (f32[44,8,128]{2,1,0:T(8,128)S(1)}, f32[44,8,128]{2,1,0:T(8,128)S(1)}, u32[]{:S(2)}, u32[]{:S(2)}) collective-permute-start(f32[44,8,128]{2,1,0:T(8,128)S(1)} %collective-permute-done.13.refs_7_), channel_id=1, source_target_pairs={{0,1},{1,0},{2,3},{3,2},{4,5},{5,4},{6,7},{7,6},{8,9},{9,8},{10,11... | collective-permute-start | bytes 540680 | tf_op jit(solution)/shard_map/ppermute | solution.py:43
  42.2 4.6 %collective-permute-start.16 = (f32[21,8,128]{2,1,0:T(8,128)S(1)}, f32[21,8,128]{2,1,0:T(8,128)S(1)}, u32[]{:S(2)}, u32[]{:S(2)}) collective-permute-start(f32[21,8,128]{2,1,0:T(8,128)S(1)} %get-tuple-element.9), channel_id=1, source_target_pairs={{0,2},{1,3},{2,0},{3,1},{4,6},{5,7},{6,4},{7,5},{8,10},{9,11},{10,... | collective-permute-start | bytes 258056 | tf_op jit(solution)/shard_map/ppermute | solution.py:43
  43.5 6.1 %collective-permute-start.18 = (f32[21,8,128]{2,1,0:T(8,128)S(1)}, f32[21,8,128]{2,1,0:T(8,128)S(1)}, u32[]{:S(2)}, u32[]{:S(2)}) collective-permute-start(f32[21,8,128]{2,1,0:T(8,128)S(1)} %get-tuple-element.9), channel_id=1, source_target_pairs={{0,4},{1,5},{2,6},{3,7},{4,0},{5,1},{6,2},{7,3},{8,12},{9,13},{10,... | collective-permute-start | bytes 258056 | tf_op jit(solution)/shard_map/ppermute | solution.py:43
  43.5 6.1 %collective-permute-start.20 = (f32[21,8,128]{2,1,0:T(8,128)S(1)}, f32[21,8,128]{2,1,0:T(8,128)S(1)}, u32[]{:S(2)}, u32[]{:S(2)}) collective-permute-start(f32[21,8,128]{2,1,0:T(8,128)S(1)} %get-tuple-element.9), channel_id=1, source_target_pairs={{0,6},{1,7},{2,4},{3,5},{4,2},{5,3},{6,0},{7,1},{8,14},{9,15},{10,... | collective-permute-start | bytes 258056 | tf_op jit(solution)/shard_map/ppermute | solution.py:43
  45.8 6.2 %collective-permute-start.15 = (f32[21,8,128]{2,1,0:T(8,128)S(1)}, f32[21,8,128]{2,1,0:T(8,128)S(1)}, u32[]{:S(2)}, u32[]{:S(2)}) collective-permute-start(f32[21,8,128]{2,1,0:T(8,128)S(1)} %get-tuple-element.9), channel_id=1, source_target_pairs={{0,1},{1,0},{2,3},{3,2},{4,5},{5,4},{6,7},{7,6},{8,9},{9,8},{10,11... | collective-permute-start | bytes 258056 | tf_op jit(solution)/shard_map/ppermute | solution.py:43
  46.7 5.2 %collective-permute-start.17 = (f32[21,8,128]{2,1,0:T(8,128)S(1)}, f32[21,8,128]{2,1,0:T(8,128)S(1)}, u32[]{:S(2)}, u32[]{:S(2)}) collective-permute-start(f32[21,8,128]{2,1,0:T(8,128)S(1)} %collective-permute-done.16.refs_10_), channel_id=1, source_target_pairs={{0,1},{1,0},{2,3},{3,2},{4,5},{5,4},{6,7},{7,6},{8,9},{9,8},{10,11... | collective-permute-start | bytes 258056 | tf_op jit(solution)/shard_map/ppermute | solution.py:43
  49.5 2.4 %collective-permute-start.19 = (f32[21,8,128]{2,1,0:T(8,128)S(1)}, f32[21,8,128]{2,1,0:T(8,128)S(1)}, u32[]{:S(2)}, u32[]{:S(2)}) collective-permute-start(f32[21,8,128]{2,1,0:T(8,128)S(1)} %collective-permute-done.18.refs_12_), channel_id=1, source_target_pairs={{0,1},{1,0},{2,3},{3,2},{4,5},{5,4},{6,7},{7,6},{8,9},{9,8},{10,11... | collective-permute-start | bytes 258056 | tf_op jit(solution)/shard_map/ppermute | solution.py:43
  49.5 2.4 %collective-permute-start.21 = (f32[21,8,128]{2,1,0:T(8,128)S(1)}, f32[21,8,128]{2,1,0:T(8,128)S(1)}, u32[]{:S(2)}, u32[]{:S(2)}) collective-permute-start(f32[21,8,128]{2,1,0:T(8,128)S(1)} %collective-permute-done.20.refs_14_), channel_id=1, source_target_pairs={{0,1},{1,0},{2,3},{3,2},{4,5},{5,4},{6,7},{7,6},{8,9},{9,8},{10,11... | collective-permute-start | bytes 258056 | tf_op jit(solution)/shard_map/ppermute | solution.py:43
where the time goes:
time: 56.9 us; the launch traced here: 56.7 us
  starting transfers between devices  20.6 us (36%)
  waiting for transfers between devices  20.4 us (36%)
  Pallas kernels  12.4 us (22%)
  local copies, waits for them, and re-layouts  2.23 us (4%)
  between operations  0.92 us (2%)
    pallas_call x4, Pallas kernels, call(): pl.pallas_call(kernel, out_shape=out_shape, in_specs=[vmem] * len(args),...  12.4 us
    ppermute x8, starting transfers between devices, swap(): return lax.ppermute(x, axis, matching(axis, first))  11.7 us
    ppermute x8, waiting for transfers between devices, swap(): return lax.ppermute(x, axis, matching(axis, first))  11.4 us
    ppermute x14, waiting for transfers between devices, flip(): return lax.ppermute(x, axis, [(i, i ^ mask) for i in range(count)])  9.03 us
    ppermute x14, starting transfers between devices, flip(): return lax.ppermute(x, axis, [(i, i ^ mask) for i in range(count)])  8.98 us
    dynamic_slice x4, local copies, waits for them, and re-layouts, ends(): lax.dynamic_slice_in_dim(x, jnp.where(even, 0, size - width), width, dim)  2.2 us
  transfers between devices with their start and end apart: 22, of which 8 were waited for; matrix products, arithmetic and copies ran while one was open for 0% of the time, Pallas kernels for 14%

commit v1 on v0

--- a/solution.py
+++ b/solution.py
@@ -97,8 +97,8 @@
         (1 - mask_ref[...]).astype(F32) * decay_ref[...]
     ).reshape(own * nj, lanes)
     even = lax.axis_index("bx") % 2 == 0
-    first = first_ref[...].reshape(wide * nj, lanes)
-    second = second_ref[...].reshape(wide * nj, lanes)
+    first = first_ref[5 : 5 + wide].reshape(wide * nj, lanes)
+    second = second_ref[5 : 5 + wide].reshape(wide * nj, lanes)
     rate_ref[own * nj : (own + wide) * nj, :] = jnp.where(even, first, second)
     rate_ref[(own + wide) * nj : (rows - wide) * nj, :] = jnp.zeros((2 * nj, lanes), F32)
     rate_ref[(rows - wide) * nj : rows * nj, :] = jnp.where(even, second, first)
@@ -164,57 +164,37 @@
     return state
 
 
-def offsets_kernel(
-    flow_ref, adj_ref, first_ref, second_ref, jfirst_ref, jsecond_ref, cfirst_ref, csecond_ref,
-    rate_ref, v_ref, off_ref, halo_ref, line_ref, *, rows, nj,
+def volume_kernel(
+    flow_ref, adj_ref, first_ref, second_ref, jfirst_ref, jsecond_ref,
+    v_ref, out1_ref, out2_ref, *, nj,
 ):
-    lanes = flow_ref.shape[-1]
-    own = rows - 2 * SWEEPS
+    own, lanes = flow_ref.shape[1], flow_ref.shape[-1]
     w = SWEEPS
     even = lax.axis_index("bx") % 2 == 0
     jeven = lax.axis_index("by") % 2 == 0
-    place, count = lax.axis_index("bx"), lax.axis_size("bx")
-    one, two = first_ref[...], second_ref[...]
-    halo_ref[0] = jnp.where(even, one, two)
-    halo_ref[1] = jnp.where(even, two, one)
-    a, b = jfirst_ref[...], jsecond_ref[...]
-    c, d = cfirst_ref[...], csecond_ref[...]
-    line_ref[0, :, 0:own, :] = jnp.where(jeven, b, a)
-    line_ref[1, :, 0:own, :] = jnp.where(jeven, a, b)
-    line_ref[:, :, own : own + w, :] = jnp.where(even, c, d)
-    line_ref[:, :, own + w : rows, :] = jnp.where(even, d, c)
-
     sub = lax.broadcasted_iota(jnp.int32, (nj, lanes), 0)
 
     def adjoint_at(comp, i):
         if 0 <= i < own:
             return adj_ref[comp, i]
         if i >= own:
-            return halo_ref[0, comp * (w + 1) + i - own]
-        return halo_ref[1, comp * (w + 1) + (w + 1) + i]
-
-    def flow_at(comp, i):
-        if 0 <= i < own:
-            return flow_ref[comp, i]
-        base = 5 * (w + 1) + comp * w
-        if i >= own:
-            return halo_ref[0, base + i - own]
-        return halo_ref[1, base + w + i]
-
-    for row in range(rows):
-        i = row if row < own + w else row - rows
+            return jnp.where(even, first_ref[comp], second_ref[comp])
+        return jnp.where(even, second_ref[comp], first_ref[comp])
+
+    for i in range(own):
         jump = []
         for comp in range(5):
             here = adjoint_at(comp, i)
             diff = adjoint_at(comp, i - 1) - adjoint_at(comp, i + 1)
-            back = jnp.where(sub == 0, line_ref[0, comp, row : row + 1, :], pltpu.roll(here, 1, 0))
+            one, two = jfirst_ref[comp, i : i + 1, :], jsecond_ref[comp, i : i + 1, :]
+            back = jnp.where(sub == 0, jnp.where(jeven, two, one), pltpu.roll(here, 1, 0))
             ahead = jnp.where(
-                sub == nj - 1, line_ref[1, comp, row : row + 1, :], pltpu.roll(here, nj - 1, 0)
+                sub == nj - 1, jnp.where(jeven, one, two), pltpu.roll(here, nj - 1, 0)
             )
             jump.append(diff + (back - ahead) + (edge_k(here, -1) - edge_k(here, 1)))
-        rho = flow_at(0, i)
-        m = [flow_at(comp, i) for comp in (1, 2, 3)]
-        energy = flow_at(4, i)
+        rho = flow_ref[0, i]
+        m = [flow_ref[comp, i] for comp in (1, 2, 3)]
+        energy = flow_ref[4, i]
         inv = 1.0 / rho
         u = [x * inv for x in m]
         mu = m[0] * u[0] + m[1] * u[1] + m[2] * u[2]
@@ -225,12 +205,23 @@
             + (energy + pressure) * jump[4]
         )
         for comp in range(3):
-            value = 0.5 * (u[comp] * q + pressure * jump[comp + 1])
-            if i >= own:
-                value = jnp.where(place < count - 1, value, 0.0)
-            elif i < 0:
-                value = jnp.where(place > 0, value, 0.0)
-            v_ref[comp, row * nj : (row + 1) * nj, :] = value
+            v_ref[comp, i] = 0.5 * (u[comp] * q + pressure * jump[comp + 1])
+    low, high = v_ref[:, 0:w], v_ref[:, own - w : own]
+    out1_ref[...] = jnp.where(even, high, low)
+    out2_ref[...] = jnp.where(even, low, high)
+
+
+def offsets_kernel(own_ref, first_ref, second_ref, rate_ref, v_ref, off_ref, *, rows, nj):
+    lanes = own_ref.shape[-1]
+    own = rows - 2 * SWEEPS
+    w = SWEEPS
+    even = lax.axis_index("bx") % 2 == 0
+    for comp in range(3):
+        v_ref[comp, 0 : own * nj, :] = own_ref[comp].reshape(own * nj, lanes)
+        one = first_ref[comp].reshape(w * nj, lanes)
+        two = second_ref[comp].reshape(w * nj, lanes)
+        v_ref[comp, own * nj : (own + w) * nj, :] = jnp.where(even, one, two)
+        v_ref[comp, (own + w) * nj : rows * nj, :] = jnp.where(even, two, one)
 
     valid = row_valid(rows, lanes)
     state = [[None] * 3 for _ in range(SWEEPS)]
@@ -322,7 +313,6 @@
     flow_ref, adj_ref, faces_ref, first_ref, second_ref, jfirst_ref, jsecond_ref, out_ref, *, nj,
 ):
     own, lanes = flow_ref.shape[1], flow_ref.shape[-1]
-    w = SWEEPS
     even = lax.axis_index("bx") % 2 == 0
     jeven = lax.axis_index("by") % 2 == 0
     sub = lax.broadcasted_iota(jnp.int32, (nj, lanes), 0)
@@ -333,13 +323,11 @@
             if face == 0:
                 if i + 1 < own:
                     return adj_ref[comp, i + 1]
-                at = comp * (w + 1)
-                return jnp.where(even, first_ref[at], second_ref[at])
+                return jnp.where(even, first_ref[comp], second_ref[comp])
             if face == 1:
                 if i > 0:
                     return adj_ref[comp, i - 1]
-                at = comp * (w + 1) + w
-                return jnp.where(even, second_ref[at], first_ref[at])
+                return jnp.where(even, second_ref[comp], first_ref[comp])
             if face in (2, 3):
                 one = jfirst_ref[comp, i : i + 1, :]
                 two = jsecond_ref[comp, i : i + 1, :]
@@ -412,24 +400,23 @@
         return call(*args, interpret=INTERPRET)
 
 
-    retention = (1 - surface_mask).astype(F32) * decay
-    r1, r2 = ends(retention, 0, w - 1, even)
-    r1, r2 = swap(r1, "bx", 0), swap(r2, "bx", 1)
-    a1, a2 = ends(adjoint, 1, w + 1, even)
-    f1, f2 = ends(flow, 1, w, even)
-
-    def pack(a, f):
-        return jnp.concatenate(
-            [a.reshape(5 * (w + 1), nj, lanes), f.reshape(5 * w, nj, lanes)], axis=0
-        )
-
-    m1, m2 = swap(pack(a1, f1), "bx", 0), swap(pack(a2, f2), "bx", 1)
     l1, l2 = ends(adjoint, 2, 1, jeven)
     l1 = swap(l1.reshape(5, own, lanes), "by", 0)
     l2 = swap(l2.reshape(5, own, lanes), "by", 1)
-    below, above = jnp.where(jeven, l2, l1), jnp.where(jeven, l1, l2)
-    c1, c2 = ends(jnp.stack([below, above]), 2, w, even)
-    c1, c2 = swap(c1, "bx", 0), swap(c2, "bx", 1)
+    retention = (1 - surface_mask).astype(F32) * decay
+    r1, r2 = ends(retention, 0, w - 1, even)
+    a1, a2 = ends(adjoint, 1, 1, even)
+    m1 = jnp.concatenate([a1.reshape(5, nj, lanes), r1], axis=0)
+    m2 = jnp.concatenate([a2.reshape(5, nj, lanes), r2], axis=0)
+    m1, m2 = swap(m1, "bx", 0), swap(m2, "bx", 1)
+
+    halo = jax.ShapeDtypeStruct((3, w, nj, lanes), F32)
+    inner, h1, h2 = run(
+        functools.partial(volume_kernel, nj=nj),
+        [jax.ShapeDtypeStruct((3, own, nj, lanes), F32), halo, halo],
+        [flow, adjoint, m1, m2, l1, l2],
+    )
+    h1, h2 = swap(h1, "bx", 0), swap(h2, "bx", 1)
 
     _, n_map = map_slots(rows, own)
     rate, maps = run(
@@ -438,7 +425,7 @@
             jax.ShapeDtypeStruct((rows * nj, lanes), F32),
             jax.ShapeDtypeStruct((n_map, own, lanes), F32),
         ],
-        [decay, surface_mask, r1, r2],
+        [decay, surface_mask, m1, m2],
     )
     all_maps = collect(maps, "by")
 
@@ -449,11 +436,7 @@
             jax.ShapeDtypeStruct((3, rows * nj, lanes), F32),
             jax.ShapeDtypeStruct((n_off, own, lanes), F32),
         ],
-        [flow, adjoint, m1, m2, l1, l2, c1, c2, rate],
-        [
-            pltpu.VMEM((2, 5 * (2 * w + 1), nj, lanes), F32),
-            pltpu.VMEM((2, 5, rows, lanes), F32),
-        ],
+        [inner, h1, h2, rate],
     )
     all_offs = collect(offs, "by")
 

time: 56.9 us -> 47.9 us (0.84)
  the two profiles are of different devices: /device:TPU:8 before, /device:TPU:9 now
where the time goes in v1:
time: 47.9 us; the launch traced here: 47.6 us
  starting transfers between devices  24.7 us (52%)
  Pallas kernels  11.3 us (24%)
  waiting for transfers between devices  5.89 us (12%)
  local copies, waits for them, and re-layouts  3.89 us (8%)
  other arithmetic  0.93 us (2%)
  between operations  0.86 us (2%)
    ppermute x14, starting transfers between devices, flip(): return lax.ppermute(x, axis, [(i, i ^ mask) for i in range(count)])  13.6 us
    pallas_call x5, Pallas kernels, call(): pl.pallas_call(kernel, out_shape=out_shape, in_specs=[vmem] * len(args),...  11.3 us
    ppermute x6, starting transfers between devices, swap(): return lax.ppermute(x, axis, matching(axis, first))  11.2 us
    ppermute x6, waiting for transfers between devices, swap(): return lax.ppermute(x, axis, matching(axis, first))  4.94 us
    unnamed x14, local copies, waits for them, and re-layouts  1.97 us
    dynamic_slice x2, local copies, waits for them, and re-layouts, ends(): lax.dynamic_slice_in_dim(x, jnp.where(even, 0, size - width), width, dim)  1.04 us
  transfers between devices with their start and end apart: 20, of which 3 were waited for; matrix products, arithmetic and copies ran while one was open for 2% of the time, Pallas kernels for 14%

profile of v1, /device:TPU:9, one launch (start us, length us, event | category | flops | bytes accessed | tf_op | source)
XLA Modules:
  0.0 47.6 jit_solution(2306441171874153564)
XLA Ops:
  0.6 0.0 copy-start.5
  0.6 0.0 copy-start.6
  0.7 0.9 %convert_multiply_fusion = f32[8,16,128]{2,1,0:T(8,128)S(1)} fusion(f32[8,16,128]{2,1,0:T(8,128)} %decay_ref.1, s32[8,16,128]{2,1,0:T(8,128)} %mask_ref.1), kind=kLoop, calls=%fused_computation.2 | loop fusion | flops 49152 | bytes 196608 | tf_op jit(solution)/shard_map/mul | solution.py:406
  1.6 0.0 copy-start.1
  1.6 0.0 copy-start.3
  1.6 0.9 %dynamic-slice_bitcast_fusion = (f32[5,16,128]{2,1,0:T(8,128)S(1)}, f32[5,16,128]{2,1,0:T(8,128)S(1)}) fusion(f32[5,8,16,128]{3,2,1,0:T(8,128)} %adj_ref.3, s32[]{:T(128)S(6)} %select_n.39, s32[]{:T(128)S(6)} %select_n.37), kind=kLoop, calls=%fused_computation.3 | loop fusion | bytes 163848 | tf_op jit(solution)/shard_map/reshape | solution.py:410
  2.5 3.2 %collective-permute-start.1 = (f32[8,16,128]{2,1,0:T(8,128)S(1)}, f32[8,16,128]{2,1,0:T(8,128)S(1)}, u32[]{:S(2)}, u32[]{:S(2)}) collective-permute-start(f32[8,16,128]{2,1,0:T(8,128)S(1)} %pad_maximum_fusion.1), channel_id=1, source_target_pairs={{8,16},{16,8},{9,17},{17,9},{10,18},{18,10},{11,19},{19,11},{12,20... | collective-permute-start | bytes 196616 | tf_op jit(solution)/shard_map/ppermute | solution.py:31
  5.7 0.1 collective-permute-start
  5.8 1.0 %constant_dynamic-slice_fusion = (f32[5,8,1,128]{3,2,1,0:T(1,128)S(1)}, f32[5,8,1,128]{3,2,1,0:T(1,128)S(1)}) fusion(f32[5,8,16,128]{3,2,1,0:T(8,128)} %adj_ref.3, s32[]{:T(128)S(6)} %select_n.43, s32[]{:T(128)S(6)} %select_n.42), kind=kLoop, calls=%fused_computation.5 | loop fusion | bytes 81928 | tf_op jit(solution)/shard_map/dynamic_slice | solution.py:37
  6.9 1.0 %collective-permute-start.2 = (f32[5,8,128]{2,1,0:T(8,128)S(1)}, f32[5,8,128]{2,1,0:T(8,128)S(1)}, u32[]{:S(2)}, u32[]{:S(2)}) collective-permute-start(f32[5,8,128]{2,1,0:T(8,128)S(1)} %bitcast.9), channel_id=1, source_target_pairs={{0,1},{2,3},{4,5},{6,7},{1,0},{3,2},{5,4},{7,6},{8,9},{10,11},{12,... | collective-permute-start | bytes 61448 | tf_op jit(solution)/shard_map/ppermute | solution.py:31
  7.9 3.0 %collective-permute-start.3 = (f32[5,8,128]{2,1,0:T(8,128)S(1)}, f32[5,8,128]{2,1,0:T(8,128)S(1)}, u32[]{:S(2)}, u32[]{:S(2)}) collective-permute-start(f32[5,8,128]{2,1,0:T(8,128)S(1)} %bitcast.8), channel_id=1, source_target_pairs={{1,2},{3,4},{5,6},{2,1},{4,3},{6,5},{9,10},{11,12},{13,14},{10,9},... | collective-permute-start | bytes 61448 | tf_op jit(solution)/shard_map/ppermute | solution.py:31
  10.9 0.0 collective-permute-done.2.jfirst_ref
  10.9 2.1 %collective-permute-done.3.jsecond_ref = f32[5,8,128]{2,1,0:T(8,128)S(1)} collective-permute-done((f32[5,8,128]{2,1,0:T(8,128)S(1)}, f32[5,8,128]{2,1,0:T(8,128)S(1)}, u32[]{:S(2)}, u32[]{:S(2)}) %collective-permute-start.3) | collective-permute-done | bytes 20512 | tf_op jit(solution)/shard_map/ppermute | solution.py:31
  13.0 0.0 collective-permute-done.1.second_ref
  13.0 0.0 collective-permute-done.first_ref
  13.0 0.0 copy-start
  13.0 1.0 %copy-done = f32[5,8,16,128]{3,2,1,0:T(8,128)S(1)} copy-done((f32[5,8,16,128]{3,2,1,0:T(8,128)S(1)}, f32[5,8,16,128]{3,2,1,0:T(8,128)}, u32[]{:S(2)}) %copy-start) | copy-done | bytes 327704
  14.0 0.0 copy-start.2
  14.0 1.0 %copy-done.2 = f32[5,8,16,128]{3,2,1,0:T(8,128)S(1)} copy-done((f32[5,8,16,128]{3,2,1,0:T(8,128)S(1)}, f32[5,8,16,128]{3,2,1,0:T(8,128)}, u32[]{:S(2)}) %copy-start.2) | copy-done | bytes 327704
  14.9 0.0 copy-start.4
  14.9 0.3 shard_map.69
  15.2 1.8 %collective-permute-start.4 = (f32[3,4,16,128]{3,2,1,0:T(8,128)S(1)}, f32[3,4,16,128]{3,2,1,0:T(8,128)S(1)}, u32[]{:S(2)}, u32[]{:S(2)}) collective-permute-start(f32[3,4,16,128]{3,2,1,0:T(8,128)S(1)} %get-tuple-element.10), channel_id=1, source_target_pairs={{0,8},{16,24},{8,0},{24,16},{1,9},{17,25},{9,1},{25,17},{2,10},{18... | collective-permute-start | bytes 294920 | tf_op jit(solution)/shard_map/ppermute | solution.py:31
  17.0 0.0 copy-done.5
  17.0 0.0 copy-done.6
  17.0 2.1 %shard_map.70 = (f32[256,128]{1,0:T(8,128)S(1)}, f32[44,8,128]{2,1,0:T(8,128)S(1)}) custom-call(f32[8,16,128]{2,1,0:T(8,128)S(1)} %copy-done.5, s32[8,16,128]{2,1,0:T(8,128)S(1)} %copy-done.6, f32[8,16,128]{2,1,0:T(8,128)S(1)} %collective-permute-done.first_ref, f32[8,16,128]{2,1,0:T(8,128)S(1)} %collective-permute-done.1.second_ref), custom_call_target="tpu_custom_call" | custom-call | tf_op jit(solution)/shard_map/pallas_call | solution.py:377
  19.1 1.6 %collective-permute-start.9 = (f32[44,8,128]{2,1,0:T(8,128)S(1)}, f32[44,8,128]{2,1,0:T(8,128)S(1)}, u32[]{:S(2)}, u32[]{:S(2)}) collective-permute-start(f32[44,8,128]{2,1,0:T(8,128)S(1)} %get-tuple-element.14), channel_id=1, source_target_pairs={{0,4},{1,5},{2,6},{3,7},{4,0},{5,1},{6,2},{7,3},{8,12},{9,13},{10,... | collective-permute-start | bytes 540680 | tf_op jit(solution)/shard_map/ppermute | solution.py:43
  20.7 1.8 %collective-permute-start.11 = (f32[44,8,128]{2,1,0:T(8,128)S(1)}, f32[44,8,128]{2,1,0:T(8,128)S(1)}, u32[]{:S(2)}, u32[]{:S(2)}) collective-permute-start(f32[44,8,128]{2,1,0:T(8,128)S(1)} %get-tuple-element.14), channel_id=1, source_target_pairs={{0,6},{1,7},{2,4},{3,5},{4,2},{5,3},{6,0},{7,1},{8,14},{9,15},{10,... | collective-permute-start | bytes 540680 | tf_op jit(solution)/shard_map/ppermute | solution.py:43
  22.5 2.1 %collective-permute-start.5 = (f32[3,4,16,128]{3,2,1,0:T(8,128)S(1)}, f32[3,4,16,128]{3,2,1,0:T(8,128)S(1)}, u32[]{:S(2)}, u32[]{:S(2)}) collective-permute-start(f32[3,4,16,128]{3,2,1,0:T(8,128)S(1)} %get-tuple-element.11), channel_id=1, source_target_pairs={{8,16},{16,8},{9,17},{17,9},{10,18},{18,10},{11,19},{19,11},{12,20... | collective-permute-start | bytes 294920 | tf_op jit(solution)/shard_map/ppermute | solution.py:31
  24.5 0.1 collective-permute-start.7
  24.6 0.0 collective-permute-done.4.first_ref
  24.6 1.2 %collective-permute-start.6 = (f32[44,8,128]{2,1,0:T(8,128)S(1)}, f32[44,8,128]{2,1,0:T(8,128)S(1)}, u32[]{:S(2)}, u32[]{:S(2)}) collective-permute-start(f32[44,8,128]{2,1,0:T(8,128)S(1)} %get-tuple-element.14), channel_id=1, source_target_pairs={{0,1},{1,0},{2,3},{3,2},{4,5},{5,4},{6,7},{7,6},{8,9},{9,8},{10,11... | collective-permute-start | bytes 540680 | tf_op jit(solution)/shard_map/ppermute | solution.py:43
  25.9 2.9 %collective-permute-done.5.second_ref = f32[3,4,16,128]{3,2,1,0:T(8,128)S(1)} collective-permute-done((f32[3,4,16,128]{3,2,1,0:T(8,128)S(1)}, f32[3,4,16,128]{3,2,1,0:T(8,128)S(1)}, u32[]{:S(2)}, u32[]{:S(2)}) %collective-permute-start.5) | collective-permute-done | bytes 98336 | tf_op jit(solution)/shard_map/ppermute | solution.py:31
  28.7 2.5 %shard_map.71 = (f32[3,256,128]{2,1,0:T(8,128)S(1)}, f32[21,8,128]{2,1,0:T(8,128)S(1)}) custom-call(f32[3,8,16,128]{3,2,1,0:T(8,128)S(1)} %get-tuple-element.9.own_ref, f32[3,4,16,128]{3,2,1,0:T(8,128)S(1)} %collective-permute-done.4.first_ref, f32[3,4,16,128]{3,2,1,0:T(8,128)S(1)} %collective-permute-done.5.second_ref, ...), custom_call_target="tpu_custom_call" | custom-call | tf_op jit(solution)/shard_map/pallas_call | solution.py:377
  31.2 0.1 collective-permute-start.14
  31.3 0.0 collective-permute-done.9.refs_5_
  31.3 0.2 collective-permute-start.16
  31.5 0.0 collective-permute-done.11.refs_7_
  31.5 2.4 %collective-permute-start.18 = (f32[21,8,128]{2,1,0:T(8,128)S(1)}, f32[21,8,128]{2,1,0:T(8,128)S(1)}, u32[]{:S(2)}, u32[]{:S(2)}) collective-permute-start(f32[21,8,128]{2,1,0:T(8,128)S(1)} %get-tuple-element.15), channel_id=1, source_target_pairs={{0,6},{1,7},{2,4},{3,5},{4,2},{5,3},{6,0},{7,1},{8,14},{9,15},{10,... | collective-permute-start | bytes 258056 | tf_op jit(solution)/shard_map/ppermute | solution.py:43
  33.9 0.0 collective-permute-done.7.refs_3_
  33.9 1.7 %collective-permute-start.10 = (f32[44,8,128]{2,1,0:T(8,128)S(1)}, f32[44,8,128]{2,1,0:T(8,128)S(1)}, u32[]{:S(2)}, u32[]{:S(2)}) collective-permute-start(f32[44,8,128]{2,1,0:T(8,128)S(1)} %collective-permute-done.9.refs_5_), channel_id=1, source_target_pairs={{0,1},{1,0},{2,3},{3,2},{4,5},{5,4},{6,7},{7,6},{8,9},{9,8},{10,11... | collective-permute-start | bytes 540680 | tf_op jit(solution)/shard_map/ppermute | solution.py:43
  35.6 0.0 collective-permute-done.6.refs_2_
  35.6 0.1 collective-permute-start.12
  35.7 0.0 collective-permute-done.14.refs_10_
  35.7 1.8 %collective-permute-start.8 = (f32[44,8,128]{2,1,0:T(8,128)S(1)}, f32[44,8,128]{2,1,0:T(8,128)S(1)}, u32[]{:S(2)}, u32[]{:S(2)}) collective-permute-start(f32[44,8,128]{2,1,0:T(8,128)S(1)} %collective-permute-done.7.refs_3_), channel_id=1, source_target_pairs={{0,1},{1,0},{2,3},{3,2},{4,5},{5,4},{6,7},{7,6},{8,9},{9,8},{10,11... | collective-permute-start | bytes 540680 | tf_op jit(solution)/shard_map/ppermute | solution.py:43
  37.5 0.0 collective-permute-done.16.refs_12_
  37.5 0.4 collective-permute-start.13
  37.8 0.0 collective-permute-done.18.refs_14_
  37.9 1.9 %collective-permute-start.15 = (f32[21,8,128]{2,1,0:T(8,128)S(1)}, f32[21,8,128]{2,1,0:T(8,128)S(1)}, u32[]{:S(2)}, u32[]{:S(2)}) collective-permute-start(f32[21,8,128]{2,1,0:T(8,128)S(1)} %collective-permute-done.14.refs_10_), channel_id=1, source_target_pairs={{0,1},{1,0},{2,3},{3,2},{4,5},{5,4},{6,7},{7,6},{8,9},{9,8},{10,11... | collective-permute-start | bytes 258056 | tf_op jit(solution)/shard_map/ppermute | solution.py:43
  39.8 0.0 collective-permute-done.13.refs_9_
  39.8 0.0 collective-permute-start.17
  39.8 0.9 %collective-permute-done.15.refs_11_ = f32[21,8,128]{2,1,0:T(8,128)S(1)} collective-permute-done((f32[21,8,128]{2,1,0:T(8,128)S(1)}, f32[21,8,128]{2,1,0:T(8,128)S(1)}, u32[]{:S(2)}, u32[]{:S(2)}) %collective-permute-start.15) | collective-permute-done | bytes 86048 | tf_op jit(solution)/shard_map/ppermute | solution.py:43
  40.7 0.4 collective-permute-start.19
  41.1 0.0 copy-done.1
  41.1 0.0 copy-done.3
  41.1 0.0 copy-done.4
  41.1 1.9 %shard_map.68 = f32[5,8,16,128]{3,2,1,0:T(8,128)} custom-call(f32[5,8,16,128]{3,2,1,0:T(8,128)S(1)} %copy-done.3, f32[5,8,16,128]{3,2,1,0:T(8,128)S(1)} %copy-done.1, f32[6,3,8,16,128]{4,3,2,1,0:T(8,128)S(1)} %copy-done.4, f32[8,16,128]{2,1,0:T(8,128)S(1)} %collective-permute-done.first_ref, f32[8,16,128]{2,1,0:T(8,128)S(1)} %collective-permute-done.1.second_ref, ...), custom_call_target="tpu_custom_call" | custom-call | tf_op jit(solution)/shard_map/pallas_call | solution.py:377
  43.0 0.0 collective-permute-done.17.refs_13_
  43.0 0.0 collective-permute-done.19.refs_15_
  43.0 0.0 collective-permute-done.10.refs_6_
  43.0 0.0 collective-permute-done.12.refs_8_
  43.0 0.0 collective-permute-done.8.refs_4_
  43.0 4.5 %shard_map.72 = f32[3,128,128]{2,1,0:T(8,128)} custom-call(f32[3,256,128]{2,1,0:T(8,128)S(1)} %get-tuple-element.13.refs_0_, f32[256,128]{1,0:T(8,128)S(1)} %get-tuple-element.12.rate_ref.refs_1_, f32[44,8,128]{2,1,0:T(8,128)S(1)} %collective-permute-done.6.refs_2_, f32[44,8,128]{2,1,0:T(8,128)S(1)} %collective-permute-done.7.refs_3_, ...), custom_call_target="tpu_custom_call" | custom-call | tf_op jit(solution)/shard_map/pallas_call | solution.py:377
  (3 shorter events, 0.0 us)
Async XLA Ops:
  0.6 16.4 %copy-start.5 = (f32[8,16,128]{2,1,0:T(8,128)S(1)}, f32[8,16,128]{2,1,0:T(8,128)}, u32[]{:S(2)}) copy-start(f32[8,16,128]{2,1,0:T(8,128)} %decay_ref.1) | copy-start | bytes 196612
  0.6 16.4 %copy-start.6 = (s32[8,16,128]{2,1,0:T(8,128)S(1)}, s32[8,16,128]{2,1,0:T(8,128)}, u32[]{:S(2)}) copy-start(s32[8,16,128]{2,1,0:T(8,128)} %mask_ref.1) | copy-start | bytes 196612
  1.6 39.5 %copy-start.1 = (f32[5,8,16,128]{3,2,1,0:T(8,128)S(1)}, f32[5,8,16,128]{3,2,1,0:T(8,128)}, u32[]{:S(2)}) copy-start(f32[5,8,16,128]{3,2,1,0:T(8,128)} %adj_ref.3) | copy-start | bytes 983044
  1.6 39.5 %copy-start.3 = (f32[5,8,16,128]{3,2,1,0:T(8,128)S(1)}, f32[5,8,16,128]{3,2,1,0:T(8,128)}, u32[]{:S(2)}) copy-start(f32[5,8,16,128]{3,2,1,0:T(8,128)} %flow_ref.3) | copy-start | bytes 983044
  2.5 10.5 %collective-permute-start.1 = (f32[8,16,128]{2,1,0:T(8,128)S(1)}, f32[8,16,128]{2,1,0:T(8,128)S(1)}, u32[]{:S(2)}, u32[]{:S(2)}) collective-permute-start(f32[8,16,128]{2,1,0:T(8,128)S(1)} %pad_maximum_fusion.1), channel_id=1, source_target_pairs={{8,16},{16,8},{9,17},{17,9},{10,18},{18,10},{11,19},{19,11},{12,20... | collective-permute-start | bytes 196616 | tf_op jit(solution)/shard_map/ppermute | solution.py:31
  5.7 7.2 %collective-permute-start = (f32[8,16,128]{2,1,0:T(8,128)S(1)}, f32[8,16,128]{2,1,0:T(8,128)S(1)}, u32[]{:S(2)}, u32[]{:S(2)}) collective-permute-start(f32[8,16,128]{2,1,0:T(8,128)S(1)} %pad_maximum_fusion), channel_id=1, source_target_pairs={{0,8},{16,24},{8,0},{24,16},{1,9},{17,25},{9,1},{25,17},{2,10},{18... | collective-permute-start | bytes 196616 | tf_op jit(solution)/shard_map/ppermute | solution.py:31
  6.9 4.0 %collective-permute-start.2 = (f32[5,8,128]{2,1,0:T(8,128)S(1)}, f32[5,8,128]{2,1,0:T(8,128)S(1)}, u32[]{:S(2)}, u32[]{:S(2)}) collective-permute-start(f32[5,8,128]{2,1,0:T(8,128)S(1)} %bitcast.9), channel_id=1, source_target_pairs={{0,1},{2,3},{4,5},{6,7},{1,0},{3,2},{5,4},{7,6},{8,9},{10,11},{12,... | collective-permute-start | bytes 61448 | tf_op jit(solution)/shard_map/ppermute | solution.py:31
  7.9 5.1 %collective-permute-start.3 = (f32[5,8,128]{2,1,0:T(8,128)S(1)}, f32[5,8,128]{2,1,0:T(8,128)S(1)}, u32[]{:S(2)}, u32[]{:S(2)}) collective-permute-start(f32[5,8,128]{2,1,0:T(8,128)S(1)} %bitcast.8), channel_id=1, source_target_pairs={{1,2},{3,4},{5,6},{2,1},{4,3},{6,5},{9,10},{11,12},{13,14},{10,9},... | collective-permute-start | bytes 61448 | tf_op jit(solution)/shard_map/ppermute | solution.py:31
  13.0 1.0 %copy-start = (f32[5,8,16,128]{3,2,1,0:T(8,128)S(1)}, f32[5,8,16,128]{3,2,1,0:T(8,128)}, u32[]{:S(2)}) copy-start(f32[5,8,16,128]{3,2,1,0:T(8,128)} %adj_ref.3) | copy-start | bytes 983044
  14.0 1.0 %copy-start.2 = (f32[5,8,16,128]{3,2,1,0:T(8,128)S(1)}, f32[5,8,16,128]{3,2,1,0:T(8,128)}, u32[]{:S(2)}) copy-start(f32[5,8,16,128]{3,2,1,0:T(8,128)} %flow_ref.3) | copy-start | bytes 983044
  14.9 26.2 %copy-start.4 = (f32[6,3,8,16,128]{4,3,2,1,0:T(8,128)S(1)}, f32[6,3,8,16,128]{4,3,2,1,0:T(8,128)}, u32[]{:S(2)}) copy-start(f32[6,3,8,16,128]{4,3,2,1,0:T(8,128)} %faces_ref.1) | copy-start | bytes 3538948
  15.2 9.4 %collective-permute-start.4 = (f32[3,4,16,128]{3,2,1,0:T(8,128)S(1)}, f32[3,4,16,128]{3,2,1,0:T(8,128)S(1)}, u32[]{:S(2)}, u32[]{:S(2)}) collective-permute-start(f32[3,4,16,128]{3,2,1,0:T(8,128)S(1)} %get-tuple-element.10), channel_id=1, source_target_pairs={{0,8},{16,24},{8,0},{24,16},{1,9},{17,25},{9,1},{25,17},{2,10},{18... | collective-permute-start | bytes 294920 | tf_op jit(solution)/shard_map/ppermute | solution.py:31
  19.1 12.2 %collective-permute-start.9 = (f32[44,8,128]{2,1,0:T(8,128)S(1)}, f32[44,8,128]{2,1,0:T(8,128)S(1)}, u32[]{:S(2)}, u32[]{:S(2)}) collective-permute-start(f32[44,8,128]{2,1,0:T(8,128)S(1)} %get-tuple-element.14), channel_id=1, source_target_pairs={{0,4},{1,5},{2,6},{3,7},{4,0},{5,1},{6,2},{7,3},{8,12},{9,13},{10,... | collective-permute-start | bytes 540680 | tf_op jit(solution)/shard_map/ppermute | solution.py:43
  20.7 10.8 %collective-permute-start.11 = (f32[44,8,128]{2,1,0:T(8,128)S(1)}, f32[44,8,128]{2,1,0:T(8,128)S(1)}, u32[]{:S(2)}, u32[]{:S(2)}) collective-permute-start(f32[44,8,128]{2,1,0:T(8,128)S(1)} %get-tuple-element.14), channel_id=1, source_target_pairs={{0,6},{1,7},{2,4},{3,5},{4,2},{5,3},{6,0},{7,1},{8,14},{9,15},{10,... | collective-permute-start | bytes 540680 | tf_op jit(solution)/shard_map/ppermute | solution.py:43
  22.5 6.3 %collective-permute-start.5 = (f32[3,4,16,128]{3,2,1,0:T(8,128)S(1)}, f32[3,4,16,128]{3,2,1,0:T(8,128)S(1)}, u32[]{:S(2)}, u32[]{:S(2)}) collective-permute-start(f32[3,4,16,128]{3,2,1,0:T(8,128)S(1)} %get-tuple-element.11), channel_id=1, source_target_pairs={{8,16},{16,8},{9,17},{17,9},{10,18},{18,10},{11,19},{19,11},{12,20... | collective-permute-start | bytes 294920 | tf_op jit(solution)/shard_map/ppermute | solution.py:31
  24.5 9.4 %collective-permute-start.7 = (f32[44,8,128]{2,1,0:T(8,128)S(1)}, f32[44,8,128]{2,1,0:T(8,128)S(1)}, u32[]{:S(2)}, u32[]{:S(2)}) collective-permute-start(f32[44,8,128]{2,1,0:T(8,128)S(1)} %get-tuple-element.14), channel_id=1, source_target_pairs={{0,2},{1,3},{2,0},{3,1},{4,6},{5,7},{6,4},{7,5},{8,10},{9,11},{10,... | collective-permute-start | bytes 540680 | tf_op jit(solution)/shard_map/ppermute | solution.py:43
  24.6 11.0 %collective-permute-start.6 = (f32[44,8,128]{2,1,0:T(8,128)S(1)}, f32[44,8,128]{2,1,0:T(8,128)S(1)}, u32[]{:S(2)}, u32[]{:S(2)}) collective-permute-start(f32[44,8,128]{2,1,0:T(8,128)S(1)} %get-tuple-element.14), channel_id=1, source_target_pairs={{0,1},{1,0},{2,3},{3,2},{4,5},{5,4},{6,7},{7,6},{8,9},{9,8},{10,11... | collective-permute-start | bytes 540680 | tf_op jit(solution)/shard_map/ppermute | solution.py:43
  31.2 4.5 %collective-permute-start.14 = (f32[21,8,128]{2,1,0:T(8,128)S(1)}, f32[21,8,128]{2,1,0:T(8,128)S(1)}, u32[]{:S(2)}, u32[]{:S(2)}) collective-permute-start(f32[21,8,128]{2,1,0:T(8,128)S(1)} %get-tuple-element.15), channel_id=1, source_target_pairs={{0,2},{1,3},{2,0},{3,1},{4,6},{5,7},{6,4},{7,5},{8,10},{9,11},{10,... | collective-permute-start | bytes 258056 | tf_op jit(solution)/shard_map/ppermute | solution.py:43
  31.3 6.2 %collective-permute-start.16 = (f32[21,8,128]{2,1,0:T(8,128)S(1)}, f32[21,8,128]{2,1,0:T(8,128)S(1)}, u32[]{:S(2)}, u32[]{:S(2)}) collective-permute-start(f32[21,8,128]{2,1,0:T(8,128)S(1)} %get-tuple-element.15), channel_id=1, source_target_pairs={{0,4},{1,5},{2,6},{3,7},{4,0},{5,1},{6,2},{7,3},{8,12},{9,13},{10,... | collective-permute-start | bytes 258056 | tf_op jit(solution)/shard_map/ppermute | solution.py:43
  31.5 6.3 %collective-permute-start.18 = (f32[21,8,128]{2,1,0:T(8,128)S(1)}, f32[21,8,128]{2,1,0:T(8,128)S(1)}, u32[]{:S(2)}, u32[]{:S(2)}) collective-permute-start(f32[21,8,128]{2,1,0:T(8,128)S(1)} %get-tuple-element.15), channel_id=1, source_target_pairs={{0,6},{1,7},{2,4},{3,5},{4,2},{5,3},{6,0},{7,1},{8,14},{9,15},{10,... | collective-permute-start | bytes 258056 | tf_op jit(solution)/shard_map/ppermute | solution.py:43
  33.9 9.1 %collective-permute-start.10 = (f32[44,8,128]{2,1,0:T(8,128)S(1)}, f32[44,8,128]{2,1,0:T(8,128)S(1)}, u32[]{:S(2)}, u32[]{:S(2)}) collective-permute-start(f32[44,8,128]{2,1,0:T(8,128)S(1)} %collective-permute-done.9.refs_5_), channel_id=1, source_target_pairs={{0,1},{1,0},{2,3},{3,2},{4,5},{5,4},{6,7},{7,6},{8,9},{9,8},{10,11... | collective-permute-start | bytes 540680 | tf_op jit(solution)/shard_map/ppermute | solution.py:43
  35.6 7.4 %collective-permute-start.12 = (f32[44,8,128]{2,1,0:T(8,128)S(1)}, f32[44,8,128]{2,1,0:T(8,128)S(1)}, u32[]{:S(2)}, u32[]{:S(2)}) collective-permute-start(f32[44,8,128]{2,1,0:T(8,128)S(1)} %collective-permute-done.11.refs_7_), channel_id=1, source_target_pairs={{0,1},{1,0},{2,3},{3,2},{4,5},{5,4},{6,7},{7,6},{8,9},{9,8},{10,11... | collective-permute-start | bytes 540680 | tf_op jit(solution)/shard_map/ppermute | solution.py:43
  35.7 7.4 %collective-permute-start.8 = (f32[44,8,128]{2,1,0:T(8,128)S(1)}, f32[44,8,128]{2,1,0:T(8,128)S(1)}, u32[]{:S(2)}, u32[]{:S(2)}) collective-permute-start(f32[44,8,128]{2,1,0:T(8,128)S(1)} %collective-permute-done.7.refs_3_), channel_id=1, source_target_pairs={{0,1},{1,0},{2,3},{3,2},{4,5},{5,4},{6,7},{7,6},{8,9},{9,8},{10,11... | collective-permute-start | bytes 540680 | tf_op jit(solution)/shard_map/ppermute | solution.py:43
  37.5 2.3 %collective-permute-start.13 = (f32[21,8,128]{2,1,0:T(8,128)S(1)}, f32[21,8,128]{2,1,0:T(8,128)S(1)}, u32[]{:S(2)}, u32[]{:S(2)}) collective-permute-start(f32[21,8,128]{2,1,0:T(8,128)S(1)} %get-tuple-element.15), channel_id=1, source_target_pairs={{0,1},{1,0},{2,3},{3,2},{4,5},{5,4},{6,7},{7,6},{8,9},{9,8},{10,11... | collective-permute-start | bytes 258056 | tf_op jit(solution)/shard_map/ppermute | solution.py:43
  37.9 2.9 %collective-permute-start.15 = (f32[21,8,128]{2,1,0:T(8,128)S(1)}, f32[21,8,128]{2,1,0:T(8,128)S(1)}, u32[]{:S(2)}, u32[]{:S(2)}) collective-permute-start(f32[21,8,128]{2,1,0:T(8,128)S(1)} %collective-permute-done.14.refs_10_), channel_id=1, source_target_pairs={{0,1},{1,0},{2,3},{3,2},{4,5},{5,4},{6,7},{7,6},{8,9},{9,8},{10,11... | collective-permute-start | bytes 258056 | tf_op jit(solution)/shard_map/ppermute | solution.py:43
  39.8 3.2 %collective-permute-start.17 = (f32[21,8,128]{2,1,0:T(8,128)S(1)}, f32[21,8,128]{2,1,0:T(8,128)S(1)}, u32[]{:S(2)}, u32[]{:S(2)}) collective-permute-start(f32[21,8,128]{2,1,0:T(8,128)S(1)} %collective-permute-done.16.refs_12_), channel_id=1, source_target_pairs={{0,1},{1,0},{2,3},{3,2},{4,5},{5,4},{6,7},{7,6},{8,9},{9,8},{10,11... | collective-permute-start | bytes 258056 | tf_op jit(solution)/shard_map/ppermute | solution.py:43
  40.7 2.3 %collective-permute-start.19 = (f32[21,8,128]{2,1,0:T(8,128)S(1)}, f32[21,8,128]{2,1,0:T(8,128)S(1)}, u32[]{:S(2)}, u32[]{:S(2)}) collective-permute-start(f32[21,8,128]{2,1,0:T(8,128)S(1)} %collective-permute-done.18.refs_14_), channel_id=1, source_target_pairs={{0,1},{1,0},{2,3},{3,2},{4,5},{5,4},{6,7},{7,6},{8,9},{9,8},{10,11... | collective-permute-start | bytes 258056 | tf_op jit(solution)/shard_map/ppermute | solution.py:43

commit v2 on v1

--- a/solution.py
+++ b/solution.py
@@ -31,28 +31,30 @@
     return lax.ppermute(x, axis, matching(axis, first))
 
 
-def ends(x, dim, width, even):
-    size = x.shape[dim]
-    to_first = lax.dynamic_slice_in_dim(x, jnp.where(even, size - width, 0), width, dim)
-    to_second = lax.dynamic_slice_in_dim(x, jnp.where(even, 0, size - width), width, dim)
-    return to_first, to_second
-
-
 def flip(x, axis, mask):
     count = lax.axis_size(axis)
     return lax.ppermute(x, axis, [(i, i ^ mask) for i in range(count)])
 
 
+def direct(count):
+    return count in (2, 4, 8)
+
+
 def collect(x, axis):
     count = lax.axis_size(axis)
-    if count not in (2, 4, 8):
+    if not direct(count):
         return [lax.all_gather(x, axis)]
-    far = {m: flip(x, axis, m) for m in range(2, count, 2)}
-    peers = {1: flip(x, axis, 1)}
-    for m, value in far.items():
-        peers[m] = value
-        peers[m + 1] = flip(value, axis, 1)
-    return [peers[m] for m in sorted(peers)]
+    near = flip(x, axis, 1)[None]
+    far = [flip(x, axis, m) for m in range(2, count, 2)]
+    if not far:
+        return [near]
+    far = jnp.stack(far)
+    return [near, far, flip(far, axis, 1)]
+
+
+def sources(count):
+    far = list(range(2, count, 2))
+    return [[1], far, [m + 1 for m in far]] if far else [[1]]
 
 
 def shift_i(x, step):
@@ -89,13 +91,101 @@
     return jnp.where(inside, 1.0, 0.0).astype(F32)
 
 
-def maps_kernel(decay_ref, mask_ref, first_ref, second_ref, rate_ref, map_ref, *, rows, nj):
-    lanes = decay_ref.shape[-1]
+def pack_kernel(
+    flow_hbm, adj_hbm, decay_hbm, mask_hbm,
+    flow_ref, adj_ref, rate_ref, line1_ref, line2_ref, rim1_ref, rim2_ref,
+    decay_ref, mask_ref, sems, *, own, nj,
+):
+    pairs = [(adj_hbm, adj_ref), (decay_hbm, decay_ref), (mask_hbm, mask_ref), (flow_hbm, flow_ref)]
+    copies = [pltpu.make_async_copy(a, b, sems.at[n]) for n, (a, b) in enumerate(pairs)]
+    for copy in copies:
+        copy.start()
+    even = lax.axis_index("bx") % 2 == 0
+    jeven = lax.axis_index("by") % 2 == 0
+    copies[0].wait()
+    for comp in range(5):
+        bottom = adj_ref[comp, pl.ds(0, own, stride=nj), :]
+        top = adj_ref[comp, pl.ds(nj - 1, own, stride=nj), :]
+        line1_ref[comp] = jnp.where(jeven, top, bottom)
+        line2_ref[comp] = jnp.where(jeven, bottom, top)
+        low = adj_ref[comp, 0:nj, :]
+        high = adj_ref[comp, (own - 1) * nj : own * nj, :]
+        rim1_ref[comp] = jnp.where(even, high, low)
+        rim2_ref[comp] = jnp.where(even, low, high)
+    copies[1].wait()
+    copies[2].wait()
+    rate_ref[...] = (1 - mask_ref[...]).astype(F32) * decay_ref[...]
+    for row in range(SWEEPS - 1):
+        low = rate_ref[row * nj : (row + 1) * nj, :]
+        at = own - (SWEEPS - 1) + row
+        high = rate_ref[at * nj : (at + 1) * nj, :]
+        rim1_ref[5 + row] = jnp.where(even, high, low)
+        rim2_ref[5 + row] = jnp.where(even, low, high)
+    copies[3].wait()
+
+
+def pack_rows(parts, width):
+    total = parts[0]
+    row = lax.broadcasted_iota(jnp.int32, total.shape, 0)
+    size = total.shape[0]
+    for n, part in enumerate(parts[1:], 1):
+        moved = pltpu.roll(part, 2 * width * n, 0)
+        place = (row - 2 * width * n + width + size) % size
+        total = jnp.where(place < 2 * width, moved, total)
+    return total
+
+
+def unpack_rows(tile, n, width):
+    return pltpu.roll(tile, (-2 * width * n) % tile.shape[0], 0) if n else tile
+
+
+def layout(groups, own):
+    places, at = {}, 0
+    for keys, width in groups:
+        for key in keys:
+            places[key] = [at, None, 0, width]
+            at += 1
+        if width:
+            share = max(1, own // (2 * width))
+            for n, key in enumerate(keys):
+                places[key][1] = at + n // share
+                places[key][2] = n % share
+            at += -(-len(keys) // share)
+    return places, at
+
+
+def map_layout(own):
+    return layout([([(d, o) for o in REACH[d]], SWEEPS - 1 - d) for d in range(SWEEPS)], own)
+
+
+def off_layout(own):
+    return layout([([(s, c) for c in range(3)], SWEEPS - 1 - s) for s in range(SWEEPS)], own)
+
+
+def store_tiles(ref, places, values, own):
+    halos = {}
+    for key, (main, halo, position, width) in places.items():
+        ref[main] = values[key][0:own]
+        if halo is not None:
+            halos.setdefault((halo, width), []).append(values[key][own : 2 * own])
+    for (halo, width), parts in halos.items():
+        ref[halo] = pack_rows(parts, width)
+
+
+def load_tiles(ref, block, place):
+    main, halo, position, width = place
+    tile = ref[block, main]
+    if halo is None:
+        return tile
+    return jnp.concatenate([tile, unpack_rows(ref[block, halo], position, width)], axis=0)
+
+
+def maps_kernel(own_ref, first_ref, second_ref, ext_ref, map_ref, all_ref, *, rows, nj):
+    lanes = own_ref.shape[-1]
     own = rows - 2 * SWEEPS
     wide = SWEEPS - 1
-    rate_ref[0 : own * nj, :] = (
-        (1 - mask_ref[...]).astype(F32) * decay_ref[...]
-    ).reshape(own * nj, lanes)
+    rate_ref = ext_ref
+    rate_ref[0 : own * nj, :] = own_ref[...]
     even = lax.axis_index("bx") % 2 == 0
     first = first_ref[5 : 5 + wide].reshape(wide * nj, lanes)
     second = second_ref[5 : 5 + wide].reshape(wide * nj, lanes)
@@ -122,23 +212,13 @@
                 fresh = gain[:n] * total[o]
                 old = coef[d][o]
                 coef[d][o] = fresh if old is None else rate[:n] * old + fresh
-    at = 0
-    for d in range(SWEEPS):
-        for o in REACH[d]:
-            c = coef[d][o]
-            for part in range(c.shape[0] // own):
-                map_ref[at] = c[part * own : (part + 1) * own]
+        at = 0
+        for d in range(SWEEPS):
+            for o in REACH[d]:
+                all_ref[at, j] = coef[d][o][:own]
                 at += 1
-
-
-def map_slots(rows, own):
-    slots, at = {}, 0
-    for d in range(SWEEPS):
-        n = 1 if d == SWEEPS - 1 else rows // own
-        for o in REACH[d]:
-            slots[d, o] = (at, n)
-            at += n
-    return slots, at
+    places, _ = map_layout(own)
+    store_tiles(map_ref, places, {(d, o): coef[d][o] for d, o in places}, own)
 
 
 def sweeps(v_ref, rate_ref, valid, state, rows, own, nj, emit):
@@ -211,7 +291,7 @@
     out2_ref[...] = jnp.where(even, low, high)
 
 
-def offsets_kernel(own_ref, first_ref, second_ref, rate_ref, v_ref, off_ref, *, rows, nj):
+def offsets_kernel(own_ref, first_ref, second_ref, rate_ref, off_ref, last_ref, v_ref, *, rows, nj):
     lanes = own_ref.shape[-1]
     own = rows - 2 * SWEEPS
     w = SWEEPS
@@ -225,88 +305,83 @@
 
     valid = row_valid(rows, lanes)
     state = [[None] * 3 for _ in range(SWEEPS)]
-    state = sweeps(v_ref, rate_ref, valid, state, rows, own, nj, None)
-    at = 0
-    for s in range(SWEEPS):
+
+    def emit(j, values):
         for comp in range(3):
-            x = state[s][comp]
-            for part in range(x.shape[0] // own):
-                off_ref[at] = x[part * own : (part + 1) * own]
-                at += 1
-
-
-def finish_kernel(*refs, rows, nj, count, stacked):
-    own = rows - 2 * SWEEPS
-    if stacked:
-        v_ref, rate_ref, map_ref, off_ref, out_ref, x_ref = refs
+            last_ref[comp, j] = values[comp]
+
+    state = sweeps(v_ref, rate_ref, valid, state, rows, own, nj, emit)
+    places, _ = off_layout(own)
+    store_tiles(off_ref, places, {(s, c): state[s][c] for s, c in places}, own)
+
+
+def finish_kernel(*refs, own, nj, count):
+    last_ref, all_ref = refs[:2]
+    if direct(count):
+        groups = sources(count)
+        n = len(groups)
+        maps, offs = refs[2 : 2 + n], refs[2 + n : 2 + 2 * n]
+        out_ref, x_ref, map_ref, off_ref = refs[2 + 2 * n :]
     else:
-        v_ref, rate_ref = refs[:2]
-        maps = refs[2 : 2 + count - 1]
-        offs = refs[1 + count : 2 * count]
-        out_ref, x_ref, map_ref, off_ref = refs[2 * count :]
-    lanes = v_ref.shape[-1]
+        map_ref, off_ref, out_ref, x_ref = refs[2:]
     me = lax.axis_index("by")
-    if not stacked:
-        for mask in range(1, count):
-            map_ref[me ^ mask] = maps[mask - 1][...]
-            off_ref[me ^ mask] = offs[mask - 1][...]
-    slots, _ = map_slots(rows, own)
-
-    def load(ref, block, at, n):
-        if n == 1:
-            return ref[block, at]
-        return jnp.concatenate([ref[block, at + part] for part in range(n)], axis=0)
-
-    sizes = [rows // own] * (SWEEPS - 1) + [1]
-    starts, at = {}, 0
-    for s in range(SWEEPS):
-        for comp in range(3):
-            starts[s, comp] = at
-            at += sizes[s]
+    if direct(count):
+        for group, mask_list in enumerate(groups):
+            for n, mask in enumerate(mask_list):
+                map_ref[me ^ mask] = maps[group][n]
+                off_ref[me ^ mask] = offs[group][n]
+    map_places, _ = map_layout(own)
+    off_places, _ = off_layout(own)
+
+    def size(s):
+        return own if s == SWEEPS - 1 else 2 * own
+
+    def get(s, comp):
+        return x_ref[s, comp, 0 : size(s), :]
+
+    def offset_of(x, o):
+        if o[0]:
+            x = shift_i(x, o[0])
+        return shift_k(x, o[1]) if o[1] else x
+
     x_ref[...] = jnp.zeros(x_ref.shape, F32)
-
-    def get(s, comp):
-        a = starts[s, comp]
-        return jnp.concatenate([x_ref[a + part] for part in range(sizes[s])], axis=0)
-
-    def put(s, comp, value):
-        for part in range(sizes[s]):
-            x_ref[starts[s, comp] + part] = value[part * own : (part + 1) * own]
 
     def through(hop, carry):
         block = count - 1 - hop
-        coef = {key: load(map_ref, block, *slot) for key, slot in slots.items()}
+        coef = {key: load_tiles(map_ref, block, place) for key, place in map_places.items()}
         fresh = {}
         for comp in range(3):
-            x = [get(s, comp) for s in range(SWEEPS)]
-            total = [load(off_ref, block, starts[s, comp], sizes[s]) for s in range(SWEEPS)]
+            total = [load_tiles(off_ref, block, off_places[s, comp]) for s in range(SWEEPS)]
             for s in range(SWEEPS):
+                x = get(s, comp)
                 for o in sorted({o for d in range(SWEEPS - s) for o in REACH[d]}):
-                    moved = x[s]
-                    if o[0]:
-                        moved = shift_i(moved, o[0])
-                    if o[1]:
-                        moved = shift_k(moved, o[1])
+                    moved = offset_of(x, o)
                     for d in range(SWEEPS - s):
                         if o in REACH[d]:
-                            n = sizes[s + d] * own
+                            n = size(s + d)
                             total[s + d] = total[s + d] + coef[d, o][:n] * moved[:n]
             for s in range(SWEEPS):
                 fresh[s, comp] = total[s]
         for (s, comp), value in fresh.items():
-            put(s, comp, value)
+            x_ref[s, comp, 0 : size(s), :] = value
         return carry
 
     lax.fori_loop(0, count - 1 - me, through, 0)
 
-    valid = row_valid(rows, lanes)
-    state = [[get(s, comp) for comp in range(3)] for s in range(SWEEPS)]
-
-    def emit(j, values):
-        for comp in range(3):
-            out_ref[comp, pl.ds(j, own, stride=nj), :] = values[comp]
-
-    sweeps(v_ref, rate_ref, valid, state, rows, own, nj, emit)
+    total = [[last_ref[comp, j] for j in range(nj)] for comp in range(3)]
+    at = 0
+    for d in range(SWEEPS):
+        x = [get(SWEEPS - 1 - d, comp) for comp in range(3)]
+        for o in REACH[d]:
+            moved = [offset_of(x[comp], o)[:own] for comp in range(3)]
+            for j in range(nj):
+                c = all_ref[at, j]
+                for comp in range(3):
+                    total[comp][j] = total[comp][j] + c * moved[comp]
+            at += 1
+    for comp in range(3):
+        for j in range(nj):
+            out_ref[comp, pl.ds(j, own, stride=nj), :] = total[comp][j]
 
 
 def product_kernel(
@@ -369,7 +444,7 @@
             out_ref[comp, i] = total[comp]
 
 
-def call(kernel, out_shape, args, scratch=(), interpret=False):
+def call(kernel, out_shape, args, scratch=(), space=pltpu.VMEM, interpret=False):
     vmem = pl.BlockSpec(memory_space=pltpu.VMEM)
     single = not isinstance(out_shape, (list, tuple))
     held = [*args, *([out_shape] if single else out_shape), *scratch]
@@ -377,7 +452,7 @@
     return pl.pallas_call(
         kernel,
         out_shape=out_shape,
-        in_specs=[vmem] * len(args),
+        in_specs=[pl.BlockSpec(memory_space=space)] * len(args),
         out_specs=vmem if single else [vmem] * len(out_shape),
         scratch_shapes=list(scratch),
         interpret=interpret,
@@ -393,50 +468,61 @@
     w = SWEEPS
     rows = own + 2 * w
     nby = lax.axis_size("by")
-    bx, by = lax.axis_index("bx"), lax.axis_index("by")
-    even, jeven = bx % 2 == 0, by % 2 == 0
 
     def run(*args):
         return call(*args, interpret=INTERPRET)
 
 
-    l1, l2 = ends(adjoint, 2, 1, jeven)
-    l1 = swap(l1.reshape(5, own, lanes), "by", 0)
-    l2 = swap(l2.reshape(5, own, lanes), "by", 1)
-    retention = (1 - surface_mask).astype(F32) * decay
-    r1, r2 = ends(retention, 0, w - 1, even)
-    a1, a2 = ends(adjoint, 1, 1, even)
-    m1 = jnp.concatenate([a1.reshape(5, nj, lanes), r1], axis=0)
-    m2 = jnp.concatenate([a2.reshape(5, nj, lanes), r2], axis=0)
+    def shape(*dims):
+        return jax.ShapeDtypeStruct(dims, F32)
+
+    flat = [flow.reshape(5, own * nj, lanes), adjoint.reshape(5, own * nj, lanes)]
+    flat += [decay.reshape(own * nj, lanes), surface_mask.reshape(own * nj, lanes)]
+    rim = shape(5 + w - 1, nj, lanes)
+    flow, adjoint, retention, l1, l2, m1, m2 = run(
+        functools.partial(pack_kernel, own=own, nj=nj),
+        [shape(5, own * nj, lanes)] * 2
+        + [shape(own * nj, lanes)]
+        + [shape(5, own, lanes)] * 2
+        + [rim] * 2,
+        flat,
+        [
+            pltpu.VMEM((own * nj, lanes), F32),
+            pltpu.VMEM((own * nj, lanes), jnp.int32),
+            pltpu.SemaphoreType.DMA((4,)),
+        ],
+        pltpu.HBM,
+    )
+    flow, adjoint = flow.reshape(5, own, nj, lanes), adjoint.reshape(5, own, nj, lanes)
+    l1, l2 = swap(l1, "by", 0), swap(l2, "by", 1)
     m1, m2 = swap(m1, "bx", 0), swap(m2, "bx", 1)
 
-    halo = jax.ShapeDtypeStruct((3, w, nj, lanes), F32)
+    halo = shape(3, w, nj, lanes)
     inner, h1, h2 = run(
         functools.partial(volume_kernel, nj=nj),
-        [jax.ShapeDtypeStruct((3, own, nj, lanes), F32), halo, halo],
+        [shape(3, own, nj, lanes), halo, halo],
         [flow, adjoint, m1, m2, l1, l2],
     )
     h1, h2 = swap(h1, "bx", 0), swap(h2, "bx", 1)
 
-    _, n_map = map_slots(rows, own)
-    rate, maps = run(
+    _, n_map = map_layout(own)
+    _, n_off = off_layout(own)
+    rate, maps, all_coef = run(
         functools.partial(maps_kernel, rows=rows, nj=nj),
         [
-            jax.ShapeDtypeStruct((rows * nj, lanes), F32),
-            jax.ShapeDtypeStruct((n_map, own, lanes), F32),
+            shape(rows * nj, lanes),
+            shape(n_map, own, lanes),
+            shape(sum(map(len, REACH)), nj, own, lanes),
         ],
-        [decay, surface_mask, m1, m2],
+        [retention, m1, m2],
     )
     all_maps = collect(maps, "by")
 
-    n_off = 3 * ((SWEEPS - 1) * (rows // own) + 1)
-    v, offs = run(
+    offs, last = run(
         functools.partial(offsets_kernel, rows=rows, nj=nj),
-        [
-            jax.ShapeDtypeStruct((3, rows * nj, lanes), F32),
-            jax.ShapeDtypeStruct((n_off, own, lanes), F32),
-        ],
+        [shape(n_off, own, lanes), shape(3, nj, own, lanes)],
         [inner, h1, h2, rate],
+        [pltpu.VMEM((3, rows * nj, lanes), F32)],
     )
     all_offs = collect(offs, "by")
 
@@ -446,17 +532,16 @@
         [flow, adjoint, faces, m1, m2, l1, l2],
     )
 
-    stacked = len(all_maps) == 1 and nby != 2
-    scratch = [pltpu.VMEM((n_off, own, lanes), F32)]
-    if not stacked:
+    scratch = [pltpu.VMEM((SWEEPS, 3, 2 * own, lanes), F32)]
+    if direct(nby):
         scratch += [
             pltpu.VMEM((nby, n_map, own, lanes), F32),
             pltpu.VMEM((nby, n_off, own, lanes), F32),
         ]
     warp = run(
-        functools.partial(finish_kernel, rows=rows, nj=nj, count=nby, stacked=stacked),
-        jax.ShapeDtypeStruct((3, own * nj, lanes), F32),
-        [v, rate, *all_maps, *all_offs],
+        functools.partial(finish_kernel, own=own, nj=nj, count=nby),
+        shape(3, own * nj, lanes),
+        [last, all_coef, *all_maps, *all_offs],
         scratch,
     )
     return (product, warp.reshape(3, own, nj, lanes))

time: 47.9 us -> 46.7 us (0.975)
  the two profiles are of different devices: /device:TPU:9 before, /device:TPU:17 now
where the time goes in v2:
time: 46.7 us; the launch traced here: 46.4 us
  starting transfers between devices  19.8 us (42%)
  waiting for transfers between devices  12.4 us (27%)
  Pallas kernels  9.71 us (21%)
  local copies, waits for them, and re-layouts  3.71 us (8%)
  between operations  0.8 us (2%)
    ppermute x6, starting transfers between devices, swap(): return lax.ppermute(x, axis, matching(axis, first))  11.2 us
    pallas_call x6, Pallas kernels, call(): pl.pallas_call(kernel, out_shape=out_shape, in_specs=[pl.BlockSpec(memory...  9.71 us
    ppermute x6, waiting for transfers between devices, swap(): return lax.ppermute(x, axis, matching(axis, first))  8.73 us
    ppermute x10, starting transfers between devices, flip(): return lax.ppermute(x, axis, [(i, i ^ mask) for i in range(count)])  8.55 us
    unnamed x10, local copies, waits for them, and re-layouts  3.71 us
    ppermute x10, waiting for transfers between devices, flip(): return lax.ppermute(x, axis, [(i, i ^ mask) for i in range(count)])  3.66 us
  transfers between devices with their start and end apart: 16, of which 7 were waited for; matrix products, arithmetic and copies ran while one was open for 0% of the time, Pallas kernels for 10%

profile of v2, /device:TPU:17, one launch (start us, length us, event | category | flops | bytes accessed | tf_op | source)
XLA Modules:
  0.0 46.4 jit_solution(7537035914500331017)
XLA Ops:
  0.6 0.0 copy-start
  0.6 0.0 copy-start.1
  0.7 1.1 %copy-done.1 = f32[5,8,16,128]{3,2,1,0:T(8,128)S(1)} copy-done((f32[5,8,16,128]{3,2,1,0:T(8,128)S(1)}, f32[5,8,16,128]{3,2,1,0:T(8,128)}, u32[]{:S(2)}) %copy-start.1) | copy-done | bytes 327704
  1.7 0.0 copy-start.2
  1.7 1.0 %copy-done.2 = f32[5,8,16,128]{3,2,1,0:T(8,128)S(1)} copy-done((f32[5,8,16,128]{3,2,1,0:T(8,128)S(1)}, f32[5,8,16,128]{3,2,1,0:T(8,128)}, u32[]{:S(2)}) %copy-start.2) | copy-done | bytes 327704
  2.7 0.0 copy-start.3
  2.7 0.8 %copy-done.3 = f32[8,16,128]{2,1,0:T(8,128)S(1)} copy-done((f32[8,16,128]{2,1,0:T(8,128)S(1)}, f32[8,16,128]{2,1,0:T(8,128)}, u32[]{:S(2)}) %copy-start.3) | copy-done | bytes 65560
  3.5 0.0 copy-start.4
  3.5 0.8 %copy-done.4 = s32[8,16,128]{2,1,0:T(8,128)S(1)} copy-done((s32[8,16,128]{2,1,0:T(8,128)S(1)}, s32[8,16,128]{2,1,0:T(8,128)}, u32[]{:S(2)}) %copy-start.4) | copy-done | bytes 65560
  4.4 0.5 shard_map.68
  4.8 1.4 %collective-permute-start = (f32[8,16,128]{2,1,0:T(8,128)S(1)}, f32[8,16,128]{2,1,0:T(8,128)S(1)}, u32[]{:S(2)}, u32[]{:S(2)}) collective-permute-start(f32[8,16,128]{2,1,0:T(8,128)S(1)} %get-tuple-element.19), channel_id=1, source_target_pairs={{0,8},{16,24},{8,0},{24,16},{1,9},{17,25},{9,1},{25,17},{2,10},{18... | collective-permute-start | bytes 196616 | tf_op jit(solution)/shard_map/ppermute | solution.py:31
  6.2 1.9 %collective-permute-start.1 = (f32[8,16,128]{2,1,0:T(8,128)S(1)}, f32[8,16,128]{2,1,0:T(8,128)S(1)}, u32[]{:S(2)}, u32[]{:S(2)}) collective-permute-start(f32[8,16,128]{2,1,0:T(8,128)S(1)} %get-tuple-element.20), channel_id=1, source_target_pairs={{8,16},{16,8},{9,17},{17,9},{10,18},{18,10},{11,19},{19,11},{12,20... | collective-permute-start | bytes 196616 | tf_op jit(solution)/shard_map/ppermute | solution.py:31
  8.1 0.0 collective-permute-done.first_ref
  8.1 3.1 %collective-permute-done.1.second_ref = f32[8,16,128]{2,1,0:T(8,128)S(1)} collective-permute-done((f32[8,16,128]{2,1,0:T(8,128)S(1)}, f32[8,16,128]{2,1,0:T(8,128)S(1)}, u32[]{:S(2)}, u32[]{:S(2)}) %collective-permute-start.1) | collective-permute-done | bytes 65568 | tf_op jit(solution)/shard_map/ppermute | solution.py:31
  11.2 2.1 %shard_map.71 = (f32[256,128]{1,0:T(8,128)S(1)}, f32[36,8,128]{2,1,0:T(8,128)S(1)}, f32[30,16,8,128]{3,2,1,0:T(8,128)S(1)}) custom-call(f32[128,128]{1,0:T(8,128)S(1)} %get-tuple-element.26.own_ref, f32[8,16,128]{2,1,0:T(8,128)S(1)} %collective-permute-done.first_ref, f32[8,16,128]{2,1,0:T(8,128)S(1)} %collective-permute-done.1.second_ref), custom_call_target="tpu_custom_call" | custom-call | tf_op jit(solution)/shard_map/pallas_call | solution.py:452
  13.3 2.2 %collective-permute-start.9 = (f32[36,8,128]{2,1,0:T(8,128)S(1)}, f32[36,8,128]{2,1,0:T(8,128)S(1)}, u32[]{:S(2)}, u32[]{:S(2)}) collective-permute-start(f32[36,8,128]{2,1,0:T(8,128)S(1)} %get-tuple-element.30), channel_id=1, source_target_pairs={{0,6},{1,7},{2,4},{3,5},{4,2},{5,3},{6,0},{7,1},{8,14},{9,15},{10,... | collective-permute-start | bytes 442376 | tf_op jit(solution)/shard_map/ppermute | solution.py:36
  15.5 0.2 collective-permute-start.8
  15.7 0.3 collective-permute-start.7
  16.0 2.9 %collective-permute-start.2 = (f32[5,8,128]{2,1,0:T(8,128)S(1)}, f32[5,8,128]{2,1,0:T(8,128)S(1)}, u32[]{:S(2)}, u32[]{:S(2)}) collective-permute-start(f32[5,8,128]{2,1,0:T(8,128)S(1)} %get-tuple-element.21), channel_id=1, source_target_pairs={{0,1},{2,3},{4,5},{6,7},{1,0},{3,2},{5,4},{7,6},{8,9},{10,11},{12,... | collective-permute-start | bytes 61448 | tf_op jit(solution)/shard_map/ppermute | solution.py:31
  18.9 3.0 %collective-permute-start.3 = (f32[5,8,128]{2,1,0:T(8,128)S(1)}, f32[5,8,128]{2,1,0:T(8,128)S(1)}, u32[]{:S(2)}, u32[]{:S(2)}) collective-permute-start(f32[5,8,128]{2,1,0:T(8,128)S(1)} %get-tuple-element.22), channel_id=1, source_target_pairs={{1,2},{3,4},{5,6},{2,1},{4,3},{6,5},{9,10},{11,12},{13,14},{10,9},... | collective-permute-start | bytes 61448 | tf_op jit(solution)/shard_map/ppermute | solution.py:31
  21.9 0.0 collective-permute-done.2.jfirst_ref
  21.9 2.4 %collective-permute-done.3.jsecond_ref = f32[5,8,128]{2,1,0:T(8,128)S(1)} collective-permute-done((f32[5,8,128]{2,1,0:T(8,128)S(1)}, f32[5,8,128]{2,1,0:T(8,128)S(1)}, u32[]{:S(2)}, u32[]{:S(2)}) %collective-permute-start.3) | collective-permute-done | bytes 20512 | tf_op jit(solution)/shard_map/ppermute | solution.py:31
  24.3 0.3 shard_map.70
  24.6 0.1 collective-permute-start.4
  24.7 1.9 %collective-permute-start.5 = (f32[3,4,16,128]{3,2,1,0:T(8,128)S(1)}, f32[3,4,16,128]{3,2,1,0:T(8,128)S(1)}, u32[]{:S(2)}, u32[]{:S(2)}) collective-permute-start(f32[3,4,16,128]{3,2,1,0:T(8,128)S(1)} %get-tuple-element.25), channel_id=1, source_target_pairs={{8,16},{16,8},{9,17},{17,9},{10,18},{18,10},{11,19},{19,11},{12,20... | collective-permute-start | bytes 294920 | tf_op jit(solution)/shard_map/ppermute | solution.py:31
  26.6 0.0 collective-permute-done.9
  26.6 0.0 collective-permute-done.8
  26.6 0.0 collective-permute-done.7
  26.7 0.1 collective-permute-start.10
  26.8 1.4 %collective-permute-done.4.first_ref = f32[3,4,16,128]{3,2,1,0:T(8,128)S(1)} collective-permute-done((f32[3,4,16,128]{3,2,1,0:T(8,128)S(1)}, f32[3,4,16,128]{3,2,1,0:T(8,128)S(1)}, u32[]{:S(2)}, u32[]{:S(2)}) %collective-permute-start.4) | collective-permute-done | bytes 98336 | tf_op jit(solution)/shard_map/ppermute | solution.py:31
  28.1 1.9 %collective-permute-done.5.second_ref = f32[3,4,16,128]{3,2,1,0:T(8,128)S(1)} collective-permute-done((f32[3,4,16,128]{3,2,1,0:T(8,128)S(1)}, f32[3,4,16,128]{3,2,1,0:T(8,128)S(1)}, u32[]{:S(2)}, u32[]{:S(2)}) %collective-permute-start.5) | collective-permute-done | bytes 98336 | tf_op jit(solution)/shard_map/ppermute | solution.py:31
  30.0 2.5 %shard_map.72 = (f32[18,8,128]{2,1,0:T(8,128)S(1)}, f32[3,16,8,128]{3,2,1,0:T(8,128)S(1)}) custom-call(f32[3,8,16,128]{3,2,1,0:T(8,128)S(1)} %get-tuple-element.23.own_ref, f32[3,4,16,128]{3,2,1,0:T(8,128)S(1)} %collective-permute-done.4.first_ref, f32[3,4,16,128]{3,2,1,0:T(8,128)S(1)} %collective-permute-done.5.second_ref, ...), custom_call_target="tpu_custom_call" | custom-call | tf_op jit(solution)/shard_map/pallas_call | solution.py:452
  32.5 0.1 collective-permute-start.14
  32.6 3.6 %collective-permute-start.13 = (f32[18,8,128]{2,1,0:T(8,128)S(1)}, f32[18,8,128]{2,1,0:T(8,128)S(1)}, u32[]{:S(2)}, u32[]{:S(2)}) collective-permute-start(f32[18,8,128]{2,1,0:T(8,128)S(1)} %get-tuple-element.31), channel_id=1, source_target_pairs={{0,4},{1,5},{2,6},{3,7},{4,0},{5,1},{6,2},{7,3},{8,12},{9,13},{10,... | collective-permute-start | bytes 221192 | tf_op jit(solution)/shard_map/ppermute | solution.py:36
  36.2 0.0 collective-permute-start.12
  36.2 0.5 %collective-permute-done.14 = f32[18,8,128]{2,1,0:T(8,128)S(1)} collective-permute-done((f32[18,8,128]{2,1,0:T(8,128)S(1)}, f32[18,8,128]{2,1,0:T(8,128)S(1)}, u32[]{:S(2)}, u32[]{:S(2)}) %collective-permute-start.14) | collective-permute-done | bytes 73760 | tf_op jit(solution)/shard_map/ppermute | solution.py:36
  36.7 1.6 %collective-permute-done.13 = f32[18,8,128]{2,1,0:T(8,128)S(1)} collective-permute-done((f32[18,8,128]{2,1,0:T(8,128)S(1)}, f32[18,8,128]{2,1,0:T(8,128)S(1)}, u32[]{:S(2)}, u32[]{:S(2)}) %collective-permute-start.13) | collective-permute-done | bytes 73760 | tf_op jit(solution)/shard_map/ppermute | solution.py:36
  38.3 1.5 %collective-permute-done.12 = f32[18,8,128]{2,1,0:T(8,128)S(1)} collective-permute-done((f32[18,8,128]{2,1,0:T(8,128)S(1)}, f32[18,8,128]{2,1,0:T(8,128)S(1)}, u32[]{:S(2)}, u32[]{:S(2)}) %collective-permute-start.12) | collective-permute-done | bytes 73760 | tf_op jit(solution)/shard_map/ppermute | solution.py:36
  39.9 1.6 %collective-permute-start.15 = (f32[3,18,8,128]{3,2,1,0:T(8,128)S(1)}, f32[3,18,8,128]{3,2,1,0:T(8,128)S(1)}, u32[]{:S(2)}, u32[]{:S(2)}) collective-permute-start(f32[3,18,8,128]{3,2,1,0:T(8,128)S(1)} %pad_maximum_fusion.1.refs_6_), channel_id=1, source_target_pairs={{0,1},{1,0},{2,3},{3,2},{4,5},{5,4},{6,7},{7,6},{8,9},{9,8},{10,11... | collective-permute-start | bytes 663560 | tf_op jit(solution)/shard_map/ppermute | solution.py:36
  41.4 0.1 collective-permute-start.6
  41.5 0.4 collective-permute-start.11
  42.0 0.0 copy-done
  42.0 1.9 %shard_map.69 = f32[5,8,16,128]{3,2,1,0:T(8,128)} custom-call(f32[5,8,16,128]{3,2,1,0:T(8,128)S(1)} %bitcast.16, f32[5,8,16,128]{3,2,1,0:T(8,128)S(1)} %bitcast.18, f32[6,3,8,16,128]{4,3,2,1,0:T(8,128)S(1)} %copy-done, f32[8,16,128]{2,1,0:T(8,128)S(1)} %collective-permute-done.first_ref, f32[8,16,128]{2,1,0:T(8,128)S(1)} %collective-permute-done.1.second_ref, ...), custom_call_target="tpu_custom_call" | custom-call | tf_op jit(solution)/shard_map/pallas_call | solution.py:452
  43.9 0.0 collective-permute-done.6
  43.9 0.0 collective-permute-done.11
  43.9 0.0 collective-permute-done.15.refs_7_
  43.9 0.0 collective-permute-done.10.refs_4_
  43.9 2.5 %shard_map.73 = f32[3,128,128]{2,1,0:T(8,128)} custom-call(f32[3,16,8,128]{3,2,1,0:T(8,128)S(1)} %get-tuple-element.28.refs_0_, f32[30,16,8,128]{3,2,1,0:T(8,128)S(1)} %get-tuple-element.29.refs_1_, f32[1,36,8,128]{3,2,1,0:T(8,128)S(1)} %bitcast.21, f32[3,36,8,128]{3,2,1,0:T(8,128)S(1)} %pad_maximum_fusion.refs_3_, ...), custom_call_target="tpu_custom_call" | custom-call | tf_op jit(solution)/shard_map/pallas_call | solution.py:452
  (2 shorter events, 0.0 us)
Async XLA Ops:
  0.6 41.3 %copy-start = (f32[6,3,8,16,128]{4,3,2,1,0:T(8,128)S(1)}, f32[6,3,8,16,128]{4,3,2,1,0:T(8,128)}, u32[]{:S(2)}) copy-start(f32[6,3,8,16,128]{4,3,2,1,0:T(8,128)} %faces_ref.1) | copy-start | bytes 3538948
  0.6 1.1 %copy-start.1 = (f32[5,8,16,128]{3,2,1,0:T(8,128)S(1)}, f32[5,8,16,128]{3,2,1,0:T(8,128)}, u32[]{:S(2)}) copy-start(f32[5,8,16,128]{3,2,1,0:T(8,128)} %param.5) | copy-start | bytes 983044
  1.7 1.0 %copy-start.2 = (f32[5,8,16,128]{3,2,1,0:T(8,128)S(1)}, f32[5,8,16,128]{3,2,1,0:T(8,128)}, u32[]{:S(2)}) copy-start(f32[5,8,16,128]{3,2,1,0:T(8,128)} %param.6) | copy-start | bytes 983044
  2.7 0.8 %copy-start.3 = (f32[8,16,128]{2,1,0:T(8,128)S(1)}, f32[8,16,128]{2,1,0:T(8,128)}, u32[]{:S(2)}) copy-start(f32[8,16,128]{2,1,0:T(8,128)} %param.8) | copy-start | bytes 196612
  3.5 0.8 %copy-start.4 = (s32[8,16,128]{2,1,0:T(8,128)S(1)}, s32[8,16,128]{2,1,0:T(8,128)}, u32[]{:S(2)}) copy-start(s32[8,16,128]{2,1,0:T(8,128)} %param.9) | copy-start | bytes 196612
  4.8 3.3 %collective-permute-start = (f32[8,16,128]{2,1,0:T(8,128)S(1)}, f32[8,16,128]{2,1,0:T(8,128)S(1)}, u32[]{:S(2)}, u32[]{:S(2)}) collective-permute-start(f32[8,16,128]{2,1,0:T(8,128)S(1)} %get-tuple-element.19), channel_id=1, source_target_pairs={{0,8},{16,24},{8,0},{24,16},{1,9},{17,25},{9,1},{25,17},{2,10},{18... | collective-permute-start | bytes 196616 | tf_op jit(solution)/shard_map/ppermute | solution.py:31
  6.2 5.0 %collective-permute-start.1 = (f32[8,16,128]{2,1,0:T(8,128)S(1)}, f32[8,16,128]{2,1,0:T(8,128)S(1)}, u32[]{:S(2)}, u32[]{:S(2)}) collective-permute-start(f32[8,16,128]{2,1,0:T(8,128)S(1)} %get-tuple-element.20), channel_id=1, source_target_pairs={{8,16},{16,8},{9,17},{17,9},{10,18},{18,10},{11,19},{19,11},{12,20... | collective-permute-start | bytes 196616 | tf_op jit(solution)/shard_map/ppermute | solution.py:31
  13.3 13.4 %collective-permute-start.9 = (f32[36,8,128]{2,1,0:T(8,128)S(1)}, f32[36,8,128]{2,1,0:T(8,128)S(1)}, u32[]{:S(2)}, u32[]{:S(2)}) collective-permute-start(f32[36,8,128]{2,1,0:T(8,128)S(1)} %get-tuple-element.30), channel_id=1, source_target_pairs={{0,6},{1,7},{2,4},{3,5},{4,2},{5,3},{6,0},{7,1},{8,14},{9,15},{10,... | collective-permute-start | bytes 442376 | tf_op jit(solution)/shard_map/ppermute | solution.py:36
  15.5 11.1 %collective-permute-start.8 = (f32[36,8,128]{2,1,0:T(8,128)S(1)}, f32[36,8,128]{2,1,0:T(8,128)S(1)}, u32[]{:S(2)}, u32[]{:S(2)}) collective-permute-start(f32[36,8,128]{2,1,0:T(8,128)S(1)} %get-tuple-element.30), channel_id=1, source_target_pairs={{0,4},{1,5},{2,6},{3,7},{4,0},{5,1},{6,2},{7,3},{8,12},{9,13},{10,... | collective-permute-start | bytes 442376 | tf_op jit(solution)/shard_map/ppermute | solution.py:36
  15.7 10.9 %collective-permute-start.7 = (f32[36,8,128]{2,1,0:T(8,128)S(1)}, f32[36,8,128]{2,1,0:T(8,128)S(1)}, u32[]{:S(2)}, u32[]{:S(2)}) collective-permute-start(f32[36,8,128]{2,1,0:T(8,128)S(1)} %get-tuple-element.30), channel_id=1, source_target_pairs={{0,2},{1,3},{2,0},{3,1},{4,6},{5,7},{6,4},{7,5},{8,10},{9,11},{10,... | collective-permute-start | bytes 442376 | tf_op jit(solution)/shard_map/ppermute | solution.py:36
  16.0 6.0 %collective-permute-start.2 = (f32[5,8,128]{2,1,0:T(8,128)S(1)}, f32[5,8,128]{2,1,0:T(8,128)S(1)}, u32[]{:S(2)}, u32[]{:S(2)}) collective-permute-start(f32[5,8,128]{2,1,0:T(8,128)S(1)} %get-tuple-element.21), channel_id=1, source_target_pairs={{0,1},{2,3},{4,5},{6,7},{1,0},{3,2},{5,4},{7,6},{8,9},{10,11},{12,... | collective-permute-start | bytes 61448 | tf_op jit(solution)/shard_map/ppermute | solution.py:31
  18.9 5.4 %collective-permute-start.3 = (f32[5,8,128]{2,1,0:T(8,128)S(1)}, f32[5,8,128]{2,1,0:T(8,128)S(1)}, u32[]{:S(2)}, u32[]{:S(2)}) collective-permute-start(f32[5,8,128]{2,1,0:T(8,128)S(1)} %get-tuple-element.22), channel_id=1, source_target_pairs={{1,2},{3,4},{5,6},{2,1},{4,3},{6,5},{9,10},{11,12},{13,14},{10,9},... | collective-permute-start | bytes 61448 | tf_op jit(solution)/shard_map/ppermute | solution.py:31
  24.6 3.5 %collective-permute-start.4 = (f32[3,4,16,128]{3,2,1,0:T(8,128)S(1)}, f32[3,4,16,128]{3,2,1,0:T(8,128)S(1)}, u32[]{:S(2)}, u32[]{:S(2)}) collective-permute-start(f32[3,4,16,128]{3,2,1,0:T(8,128)S(1)} %get-tuple-element.24), channel_id=1, source_target_pairs={{0,8},{16,24},{8,0},{24,16},{1,9},{17,25},{9,1},{25,17},{2,10},{18... | collective-permute-start | bytes 294920 | tf_op jit(solution)/shard_map/ppermute | solution.py:31
  24.7 5.4 %collective-permute-start.5 = (f32[3,4,16,128]{3,2,1,0:T(8,128)S(1)}, f32[3,4,16,128]{3,2,1,0:T(8,128)S(1)}, u32[]{:S(2)}, u32[]{:S(2)}) collective-permute-start(f32[3,4,16,128]{3,2,1,0:T(8,128)S(1)} %get-tuple-element.25), channel_id=1, source_target_pairs={{8,16},{16,8},{9,17},{17,9},{10,18},{18,10},{11,19},{19,11},{12,20... | collective-permute-start | bytes 294920 | tf_op jit(solution)/shard_map/ppermute | solution.py:31
  26.7 17.2 %collective-permute-start.10 = (f32[3,36,8,128]{3,2,1,0:T(8,128)S(1)}, f32[3,36,8,128]{3,2,1,0:T(8,128)S(1)}, u32[]{:S(2)}, u32[]{:S(2)}) collective-permute-start(f32[3,36,8,128]{3,2,1,0:T(8,128)S(1)} %pad_maximum_fusion.refs_3_), channel_id=1, source_target_pairs={{0,1},{1,0},{2,3},{3,2},{4,5},{5,4},{6,7},{7,6},{8,9},{9,8},{10,11... | collective-permute-start | bytes 1327112 | tf_op jit(solution)/shard_map/ppermute | solution.py:36
  32.5 4.2 %collective-permute-start.14 = (f32[18,8,128]{2,1,0:T(8,128)S(1)}, f32[18,8,128]{2,1,0:T(8,128)S(1)}, u32[]{:S(2)}, u32[]{:S(2)}) collective-permute-start(f32[18,8,128]{2,1,0:T(8,128)S(1)} %get-tuple-element.31), channel_id=1, source_target_pairs={{0,6},{1,7},{2,4},{3,5},{4,2},{5,3},{6,0},{7,1},{8,14},{9,15},{10,... | collective-permute-start | bytes 221192 | tf_op jit(solution)/shard_map/ppermute | solution.py:36
  32.6 5.7 %collective-permute-start.13 = (f32[18,8,128]{2,1,0:T(8,128)S(1)}, f32[18,8,128]{2,1,0:T(8,128)S(1)}, u32[]{:S(2)}, u32[]{:S(2)}) collective-permute-start(f32[18,8,128]{2,1,0:T(8,128)S(1)} %get-tuple-element.31), channel_id=1, source_target_pairs={{0,4},{1,5},{2,6},{3,7},{4,0},{5,1},{6,2},{7,3},{8,12},{9,13},{10,... | collective-permute-start | bytes 221192 | tf_op jit(solution)/shard_map/ppermute | solution.py:36
  36.2 3.6 %collective-permute-start.12 = (f32[18,8,128]{2,1,0:T(8,128)S(1)}, f32[18,8,128]{2,1,0:T(8,128)S(1)}, u32[]{:S(2)}, u32[]{:S(2)}) collective-permute-start(f32[18,8,128]{2,1,0:T(8,128)S(1)} %get-tuple-element.31), channel_id=1, source_target_pairs={{0,2},{1,3},{2,0},{3,1},{4,6},{5,7},{6,4},{7,5},{8,10},{9,11},{10,... | collective-permute-start | bytes 221192 | tf_op jit(solution)/shard_map/ppermute | solution.py:36
  39.9 4.0 %collective-permute-start.15 = (f32[3,18,8,128]{3,2,1,0:T(8,128)S(1)}, f32[3,18,8,128]{3,2,1,0:T(8,128)S(1)}, u32[]{:S(2)}, u32[]{:S(2)}) collective-permute-start(f32[3,18,8,128]{3,2,1,0:T(8,128)S(1)} %pad_maximum_fusion.1.refs_6_), channel_id=1, source_target_pairs={{0,1},{1,0},{2,3},{3,2},{4,5},{5,4},{6,7},{7,6},{8,9},{9,8},{10,11... | collective-permute-start | bytes 663560 | tf_op jit(solution)/shard_map/ppermute | solution.py:36
  41.4 2.5 %collective-permute-start.6 = (f32[36,8,128]{2,1,0:T(8,128)S(1)}, f32[36,8,128]{2,1,0:T(8,128)S(1)}, u32[]{:S(2)}, u32[]{:S(2)}) collective-permute-start(f32[36,8,128]{2,1,0:T(8,128)S(1)} %get-tuple-element.30), channel_id=1, source_target_pairs={{0,1},{1,0},{2,3},{3,2},{4,5},{5,4},{6,7},{7,6},{8,9},{9,8},{10,11... | collective-permute-start | bytes 442376 | tf_op jit(solution)/shard_map/ppermute | solution.py:36
  41.5 2.4 %collective-permute-start.11 = (f32[18,8,128]{2,1,0:T(8,128)S(1)}, f32[18,8,128]{2,1,0:T(8,128)S(1)}, u32[]{:S(2)}, u32[]{:S(2)}) collective-permute-start(f32[18,8,128]{2,1,0:T(8,128)S(1)} %get-tuple-element.31), channel_id=1, source_target_pairs={{0,1},{1,0},{2,3},{3,2},{4,5},{5,4},{6,7},{7,6},{8,9},{9,8},{10,11... | collective-permute-start | bytes 221192 | tf_op jit(solution)/shard_map/ppermute | solution.py:36

commit v3 on v2

--- a/solution.py
+++ b/solution.py
@@ -57,28 +57,36 @@
     return [[1], far, [m + 1 for m in far]] if far else [[1]]
 
 
-def shift_i(x, step):
-    rows = x.shape[0]
-    return pltpu.roll(x, (-step) % rows, 0)
-
-
-def shift_k(x, step):
-    lanes = x.shape[1]
-    return pltpu.roll(x, (-step) % lanes, 1)
-
-
-def edge_k(x, step):
-    lane = lax.broadcasted_iota(jnp.int32, x.shape, 1)
-    edge = x.shape[1] - 1 if step > 0 else 0
-    return jnp.where(lane == edge, 0.0, shift_k(x, step))
-
-
-def move(x, step):
-    return shift_i(x, step[0]) if step[0] else edge_k(x, step[1])
-
-
-def couple(x):
-    return (shift_i(x, 1) + shift_i(x, -1)) + (edge_k(x, 1) + edge_k(x, -1))
+def shift_i(x, step, n):
+    size = x[0].shape[0]
+    turned = [pltpu.roll(tile, (-step) % size, 0) for tile in x]
+    row = lax.broadcasted_iota(jnp.int32, x[0].shape, 0)
+    edge = row == (size - 1 if step > 0 else 0)
+    return [jnp.where(edge, turned[1 - t], turned[t]) for t in range(n)]
+
+
+def roll_k(tile, step):
+    return pltpu.roll(tile, (-step) % tile.shape[1], 1)
+
+
+def edge_k(tile, step):
+    lane = lax.broadcasted_iota(jnp.int32, tile.shape, 1)
+    edge = tile.shape[1] - 1 if step > 0 else 0
+    return jnp.where(lane == edge, 0.0, roll_k(tile, step))
+
+
+def move(x, step, n):
+    return shift_i(x, step[0], n) if step[0] else [edge_k(tile, step[1]) for tile in x[:n]]
+
+
+def couple(x, n):
+    up, down = shift_i(x, 1, n), shift_i(x, -1, n)
+    return [(up[t] + down[t]) + (edge_k(x[t], 1) + edge_k(x[t], -1)) for t in range(n)]
+
+
+def at_j(ref, j, rows, nj, tiles):
+    size = rows // tiles
+    return [ref[pl.ds(j + t * size * nj, size, stride=nj), :] for t in range(tiles)]
 
 
 def row_valid(rows, lanes):
@@ -88,7 +96,8 @@
     below = jnp.where(place > 0, SWEEPS - 1, 0)
     row = lax.broadcasted_iota(jnp.int32, (rows, lanes), 0)
     inside = (row < own + above) | (row >= rows - below)
-    return jnp.where(inside, 1.0, 0.0).astype(F32)
+    valid = jnp.where(inside, 1.0, 0.0).astype(F32)
+    return [valid[t * own : (t + 1) * own] for t in range(rows // own)]
 
 
 def pack_kernel(
@@ -162,12 +171,12 @@
     return layout([([(s, c) for c in range(3)], SWEEPS - 1 - s) for s in range(SWEEPS)], own)
 
 
-def store_tiles(ref, places, values, own):
+def store_tiles(ref, places, values):
     halos = {}
     for key, (main, halo, position, width) in places.items():
-        ref[main] = values[key][0:own]
+        ref[main] = values[key][0]
         if halo is not None:
-            halos.setdefault((halo, width), []).append(values[key][own : 2 * own])
+            halos.setdefault((halo, width), []).append(values[key][1])
     for (halo, width), parts in halos.items():
         ref[halo] = pack_rows(parts, width)
 
@@ -176,11 +185,13 @@
     main, halo, position, width = place
     tile = ref[block, main]
     if halo is None:
-        return tile
-    return jnp.concatenate([tile, unpack_rows(ref[block, halo], position, width)], axis=0)
-
-
-def maps_kernel(own_ref, first_ref, second_ref, ext_ref, map_ref, all_ref, *, rows, nj):
+        return [tile]
+    return [tile, unpack_rows(ref[block, halo], position, width)]
+
+
+def maps_kernel(
+    own_ref, first_ref, second_ref, rate_t, gain_t, map_ref, all_ref, ext_ref, side_ref, *, rows, nj,
+):
     lanes = own_ref.shape[-1]
     own = rows - 2 * SWEEPS
     wide = SWEEPS - 1
@@ -194,54 +205,79 @@
     rate_ref[(rows - wide) * nj : rows * nj, :] = jnp.where(even, second, first)
 
     valid = row_valid(rows, lanes)
-    coef = [{o: None for o in REACH[d]} for d in range(SWEEPS)]
-    for j in range(nj - 1, -1, -1):
-        rate = rate_ref[pl.ds(j, rows, stride=nj), :]
-        gain = KAPPA * (valid - rate)
-        old = coef[0][(0, 0)]
-        coef[0][(0, 0)] = rate if old is None else rate * old
-        for d in range(1, SWEEPS):
-            n = own if d == SWEEPS - 1 else rows
-            total = {o: None for o in REACH[d]}
-            for o, c in coef[d - 1].items():
-                for step in ((1, 0), (-1, 0), (0, 1), (0, -1)):
-                    moved = move(c, step)[:n]
-                    goal = (o[0] + step[0], o[1] + step[1])
-                    total[goal] = moved if total[goal] is None else total[goal] + moved
+    for j in range(nj):
+        rate = at_j(rate_ref, j, rows, nj, 2)
+        for t in range(2):
+            rate_t[j, t] = rate[t]
+            gain_t[j, t] = KAPPA * (valid[t] - rate[t])
+    places, _ = map_layout(own)
+    final, at, begin = {}, 0, 0
+    for d in range(SWEEPS):
+        n = 1 if d == SWEEPS - 1 else 2
+        index = {o: at + i for i, o in enumerate(REACH[d])}
+        before = {o: begin + i for i, o in enumerate(REACH[d - 1])} if d else {}
+        coef = {o: None for o in REACH[d]}
+        for j in range(nj - 1, -1, -1):
+            rate = [rate_t[j, t] for t in range(n)]
+            if d == 0:
+                old = coef[0, 0]
+                coef[0, 0] = rate if old is None else [r * c for r, c in zip(rate, old)]
+            else:
+                total = {o: None for o in REACH[d]}
+                for o, i in before.items():
+                    c = [all_ref[i, j], side_ref[i, j]]
+                    for step in ((1, 0), (-1, 0), (0, 1), (0, -1)):
+                        moved = move(c, step, n)
+                        goal = (o[0] + step[0], o[1] + step[1])
+                        held = total[goal]
+                        total[goal] = moved if held is None else [p + q for p, q in zip(held, moved)]
+                gain = [gain_t[j, t] for t in range(n)]
+                for o in REACH[d]:
+                    fresh = [gain[t] * total[o][t] for t in range(n)]
+                    old = coef[o]
+                    if old is not None:
+                        fresh = [rate[t] * old[t] + fresh[t] for t in range(n)]
+                    coef[o] = fresh
             for o in REACH[d]:
-                fresh = gain[:n] * total[o]
-                old = coef[d][o]
-                coef[d][o] = fresh if old is None else rate[:n] * old + fresh
-        at = 0
-        for d in range(SWEEPS):
-            for o in REACH[d]:
-                all_ref[at, j] = coef[d][o][:own]
-                at += 1
-    places, _ = map_layout(own)
-    store_tiles(map_ref, places, {(d, o): coef[d][o] for d, o in places}, own)
-
-
-def sweeps(v_ref, rate_ref, valid, state, rows, own, nj, emit):
+                all_ref[index[o], j] = coef[o][0]
+                if n == 2:
+                    side_ref[index[o], j] = coef[o][1]
+        final.update({(d, o): coef[o] for o in REACH[d]})
+        begin, at = at, at + len(REACH[d])
+    store_tiles(map_ref, places, final)
+
+
+def sweeps(v_ref, rate_t, gain_t, warp_ref, rows, nj, last_ref):
     comps = v_ref.shape[0]
-    for j in range(nj - 1, -1, -1):
-        rate = rate_ref[pl.ds(j, rows, stride=nj), :]
-        rest = valid - rate
-        base = [v_ref[c, pl.ds(j, rows, stride=nj), :] for c in range(comps)]
-        before = base
-        for s in range(SWEEPS):
-            n = own if s == SWEEPS - 1 else rows
-            now = []
+    ends_at = {}
+    for s in range(SWEEPS):
+        n = 1 if s == SWEEPS - 1 else 2
+        state = [None] * comps
+        for j in range(nj - 1, -1, -1):
+            rate = [rate_t[j, t] for t in range(n)]
+            gain = [gain_t[j, t] for t in range(n)]
             for c in range(comps):
-                source = base[c][:n] + KAPPA * couple(before[c])[:n]
-                new = rest[:n] * source
-                if state[s][c] is not None:
-                    new = new + rate[:n] * state[s][c]
-                now.append(new)
-            state[s] = now
-            before = now
-        if emit is not None:
-            emit(j, state[SWEEPS - 1])
-    return state
+                if s == 0:
+                    before = at_j(v_ref.at[c], j, rows, nj, 2)
+                    base = [gain[t] * (before[t] * (1.0 / KAPPA)) for t in range(n)]
+                    for t in range(n):
+                        warp_ref[SWEEPS - 1, c, j, t] = base[t]
+                else:
+                    before = [warp_ref[s - 1, c, j, t] for t in range(2)]
+                    base = [warp_ref[SWEEPS - 1, c, j, t] for t in range(n)]
+                near = couple(before, n)
+                new = [base[t] + gain[t] * near[t] for t in range(n)]
+                if state[c] is not None:
+                    new = [new[t] + rate[t] * state[c][t] for t in range(n)]
+                state[c] = new
+                if s == SWEEPS - 1:
+                    last_ref[c, j] = new[0]
+                else:
+                    for t in range(n):
+                        warp_ref[s, c, j, t] = new[t]
+        for c in range(comps):
+            ends_at[s, c] = state[c]
+    return ends_at
 
 
 def volume_kernel(
@@ -291,7 +327,9 @@
     out2_ref[...] = jnp.where(even, low, high)
 
 
-def offsets_kernel(own_ref, first_ref, second_ref, rate_ref, off_ref, last_ref, v_ref, *, rows, nj):
+def offsets_kernel(
+    own_ref, first_ref, second_ref, rate_t, gain_t, off_ref, last_ref, v_ref, warp_ref, *, rows, nj,
+):
     lanes = own_ref.shape[-1]
     own = rows - 2 * SWEEPS
     w = SWEEPS
@@ -303,16 +341,9 @@
         v_ref[comp, own * nj : (own + w) * nj, :] = jnp.where(even, one, two)
         v_ref[comp, (own + w) * nj : rows * nj, :] = jnp.where(even, two, one)
 
-    valid = row_valid(rows, lanes)
-    state = [[None] * 3 for _ in range(SWEEPS)]
-
-    def emit(j, values):
-        for comp in range(3):
-            last_ref[comp, j] = values[comp]
-
-    state = sweeps(v_ref, rate_ref, valid, state, rows, own, nj, emit)
+    ends_at = sweeps(v_ref, rate_t, gain_t, warp_ref, rows, nj, last_ref)
     places, _ = off_layout(own)
-    store_tiles(off_ref, places, {(s, c): state[s][c] for s, c in places}, own)
+    store_tiles(off_ref, places, ends_at)
 
 
 def finish_kernel(*refs, own, nj, count):
@@ -321,9 +352,9 @@
         groups = sources(count)
         n = len(groups)
         maps, offs = refs[2 : 2 + n], refs[2 + n : 2 + 2 * n]
-        out_ref, x_ref, map_ref, off_ref = refs[2 + 2 * n :]
+        out_ref, x_ref, near_ref, map_ref, off_ref = refs[2 + 2 * n :]
     else:
-        map_ref, off_ref, out_ref, x_ref = refs[2:]
+        map_ref, off_ref, out_ref, x_ref, near_ref = refs[2:]
     me = lax.axis_index("by")
     if direct(count):
         for group, mask_list in enumerate(groups):
@@ -333,18 +364,25 @@
     map_places, _ = map_layout(own)
     off_places, _ = off_layout(own)
 
-    def size(s):
-        return own if s == SWEEPS - 1 else 2 * own
+    def tiles(s):
+        return 1 if s == SWEEPS - 1 else 2
 
     def get(s, comp):
-        return x_ref[s, comp, 0 : size(s), :]
-
-    def offset_of(x, o):
-        if o[0]:
-            x = shift_i(x, o[0])
-        return shift_k(x, o[1]) if o[1] else x
+        return [x_ref[s, comp, t] for t in range(tiles(s))]
 
     x_ref[...] = jnp.zeros(x_ref.shape, F32)
+
+    def shifted(x, reach, n):
+        deep = max(abs(o[0]) for o in reach)
+        by_row = {0: x}
+        for step in range(1, deep + 1):
+            count_out = 2 if step < deep else n
+            by_row[step] = shift_i(by_row[step - 1], 1, count_out)
+            by_row[-step] = shift_i(by_row[1 - step], -1, count_out)
+        out = {}
+        for i, k in reach:
+            out[i, k] = [roll_k(tile, k) if k else tile for tile in by_row[i][:n]]
+        return out
 
     def through(hop, carry):
         block = count - 1 - hop
@@ -354,34 +392,41 @@
             total = [load_tiles(off_ref, block, off_places[s, comp]) for s in range(SWEEPS)]
             for s in range(SWEEPS):
                 x = get(s, comp)
-                for o in sorted({o for d in range(SWEEPS - s) for o in REACH[d]}):
-                    moved = offset_of(x, o)
-                    for d in range(SWEEPS - s):
-                        if o in REACH[d]:
-                            n = size(s + d)
-                            total[s + d] = total[s + d] + coef[d, o][:n] * moved[:n]
+                for d in range(SWEEPS - s):
+                    n = tiles(s + d)
+                    moved = shifted(x, REACH[d], n)
+                    for o in REACH[d]:
+                        for t in range(n):
+                            total[s + d][t] = total[s + d][t] + coef[d, o][t] * moved[o][t]
             for s in range(SWEEPS):
                 fresh[s, comp] = total[s]
         for (s, comp), value in fresh.items():
-            x_ref[s, comp, 0 : size(s), :] = value
+            for t, tile in enumerate(value):
+                x_ref[s, comp, t] = tile
         return carry
 
     lax.fori_loop(0, count - 1 - me, through, 0)
 
-    total = [[last_ref[comp, j] for j in range(nj)] for comp in range(3)]
-    at = 0
-    for d in range(SWEEPS):
-        x = [get(SWEEPS - 1 - d, comp) for comp in range(3)]
-        for o in REACH[d]:
-            moved = [offset_of(x[comp], o)[:own] for comp in range(3)]
-            for j in range(nj):
+    for comp in range(3):
+        at = 0
+        for d in range(SWEEPS):
+            moved = shifted(get(SWEEPS - 1 - d, comp), REACH[d], 1)
+            for o in REACH[d]:
+                near_ref[at, comp] = moved[o][0]
+                at += 1
+    part = nj // 2 if nj % 2 == 0 else nj
+    for begin in range(0, nj, part):
+        span = range(begin, begin + part)
+        total = [[last_ref[comp, j] for j in span] for comp in range(3)]
+        for at in range(near_ref.shape[0]):
+            moved = [near_ref[at, comp] for comp in range(3)]
+            for n, j in enumerate(span):
                 c = all_ref[at, j]
                 for comp in range(3):
-                    total[comp][j] = total[comp][j] + c * moved[comp]
-            at += 1
-    for comp in range(3):
-        for j in range(nj):
-            out_ref[comp, pl.ds(j, own, stride=nj), :] = total[comp][j]
+                    total[comp][n] = total[comp][n] + c * moved[comp]
+        for comp in range(3):
+            for n, j in enumerate(span):
+                out_ref[comp, pl.ds(j, own, stride=nj), :] = total[comp][n]
 
 
 def product_kernel(
@@ -478,6 +523,7 @@
 
     flat = [flow.reshape(5, own * nj, lanes), adjoint.reshape(5, own * nj, lanes)]
     flat += [decay.reshape(own * nj, lanes), surface_mask.reshape(own * nj, lanes)]
+    flat = [pltpu.with_memory_space_constraint(x, pltpu.HBM) for x in flat]
     rim = shape(5 + w - 1, nj, lanes)
     flow, adjoint, retention, l1, l2, m1, m2 = run(
         functools.partial(pack_kernel, own=own, nj=nj),
@@ -507,22 +553,27 @@
 
     _, n_map = map_layout(own)
     _, n_off = off_layout(own)
-    rate, maps, all_coef = run(
+    rate, gain, maps, all_coef = run(
         functools.partial(maps_kernel, rows=rows, nj=nj),
         [
-            shape(rows * nj, lanes),
+            shape(nj, 2, own, lanes),
+            shape(nj, 2, own, lanes),
             shape(n_map, own, lanes),
             shape(sum(map(len, REACH)), nj, own, lanes),
         ],
         [retention, m1, m2],
+        [
+            pltpu.VMEM((rows * nj, lanes), F32),
+            pltpu.VMEM((sum(map(len, REACH[:-1])), nj, own, lanes), F32),
+        ],
     )
     all_maps = collect(maps, "by")
 
     offs, last = run(
         functools.partial(offsets_kernel, rows=rows, nj=nj),
         [shape(n_off, own, lanes), shape(3, nj, own, lanes)],
-        [inner, h1, h2, rate],
-        [pltpu.VMEM((3, rows * nj, lanes), F32)],
+        [inner, h1, h2, rate, gain],
+        [pltpu.VMEM((3, rows * nj, lanes), F32), pltpu.VMEM((SWEEPS, 3, nj, 2, own, lanes), F32)],
     )
     all_offs = collect(offs, "by")
 
@@ -532,7 +583,10 @@
         [flow, adjoint, faces, m1, m2, l1, l2],
     )
 
-    scratch = [pltpu.VMEM((SWEEPS, 3, 2 * own, lanes), F32)]
+    scratch = [
+        pltpu.VMEM((SWEEPS, 3, 2, own, lanes), F32),
+        pltpu.VMEM((sum(map(len, REACH)), 3, own, lanes), F32),
+    ]
     if direct(nby):
         scratch += [
             pltpu.VMEM((nby, n_map, own, lanes), F32),

time: 46.7 us -> 40.8 us (0.87)
  local copies, waits for them, and re-layouts: 3.71 us -> 0.01 us
  Pallas kernels: 9.71 us -> 7.69 us
    unnamed x10 -> x2, local copies, waits for them, and re-layouts: 3.71 us -> 0.01 us
    pallas_call x6, Pallas kernels: 9.71 us -> 7.69 us  [call(): pl.pallas_call(kernel, out_shape=out_shape, in_specs=[pl.BlockSpec(memory...]
  transfers between devices with their start and end apart: 16 -> 16, of which waited for: 7 -> 7; matrix products, arithmetic and copies ran while one was open for 0% -> 0% of each run, Pallas kernels for 10% -> 8%
where the time goes in v3:
time: 40.8 us; the launch traced here: 40.7 us
  starting transfers between devices  19.8 us (49%)
  waiting for transfers between devices  12.4 us (30%)
  Pallas kernels  7.69 us (19%)
  between operations  0.77 us (2%)
    ppermute x6, starting transfers between devices, swap(): return lax.ppermute(x, axis, matching(axis, first))  11.2 us
    ppermute x6, waiting for transfers between devices, swap(): return lax.ppermute(x, axis, matching(axis, first))  8.73 us
    ppermute x10, starting transfers between devices, flip(): return lax.ppermute(x, axis, [(i, i ^ mask) for i in range(count)])  8.55 us
    pallas_call x6, Pallas kernels, call(): pl.pallas_call(kernel, out_shape=out_shape, in_specs=[pl.BlockSpec(memory...  7.69 us
    ppermute x10, waiting for transfers between devices, flip(): return lax.ppermute(x, axis, [(i, i ^ mask) for i in range(count)])  3.66 us
  transfers between devices with their start and end apart: 16, of which 7 were waited for; matrix products, arithmetic and copies ran while one was open for 0% of the time, Pallas kernels for 8%

profile of v3, /device:TPU:17, one launch (start us, length us, event | category | flops | bytes accessed | tf_op | source)
XLA Modules:
  0.0 40.7 jit_solution(9892638249419055946)
XLA Ops:
  0.6 0.0 copy-start
  0.6 1.3 %shard_map.68 = (f32[5,128,128]{2,1,0:T(8,128)S(1)}, f32[5,128,128]{2,1,0:T(8,128)S(1)}, f32[128,128]{1,0:T(8,128)S(1)}, f32[5,8,128]{2,1,0:T(8,128)S(1)}, f32[5...) custom-call(f32[5,128,128]{2,1,0:T(8,128)} %bitcast.21, f32[5,128,128]{2,1,0:T(8,128)} %bitcast.22, ...), custom_call_target="tpu_custom_call" | custom-call | tf_op jit(solution)/shard_map/pallas_call | solution.py:497
  1.9 1.4 %collective-permute-start = (f32[8,16,128]{2,1,0:T(8,128)S(1)}, f32[8,16,128]{2,1,0:T(8,128)S(1)}, u32[]{:S(2)}, u32[]{:S(2)}) collective-permute-start(f32[8,16,128]{2,1,0:T(8,128)S(1)} %get-tuple-element.20), channel_id=1, source_target_pairs={{0,8},{16,24},{8,0},{24,16},{1,9},{17,25},{9,1},{25,17},{2,10},{18... | collective-permute-start | bytes 196616 | tf_op jit(solution)/shard_map/ppermute | solution.py:31
  3.3 1.9 %collective-permute-start.1 = (f32[8,16,128]{2,1,0:T(8,128)S(1)}, f32[8,16,128]{2,1,0:T(8,128)S(1)}, u32[]{:S(2)}, u32[]{:S(2)}) collective-permute-start(f32[8,16,128]{2,1,0:T(8,128)S(1)} %get-tuple-element.21), channel_id=1, source_target_pairs={{8,16},{16,8},{9,17},{17,9},{10,18},{18,10},{11,19},{19,11},{12,20... | collective-permute-start | bytes 196616 | tf_op jit(solution)/shard_map/ppermute | solution.py:31
  5.2 0.0 collective-permute-done.first_ref
  5.2 3.1 %collective-permute-done.1.second_ref = f32[8,16,128]{2,1,0:T(8,128)S(1)} collective-permute-done((f32[8,16,128]{2,1,0:T(8,128)S(1)}, f32[8,16,128]{2,1,0:T(8,128)S(1)}, u32[]{:S(2)}, u32[]{:S(2)}) %collective-permute-start.1) | collective-permute-done | bytes 65568 | tf_op jit(solution)/shard_map/ppermute | solution.py:31
  8.3 0.8 %shard_map.71 = (f32[16,2,8,128]{3,2,1,0:T(8,128)S(1)}, f32[16,2,8,128]{3,2,1,0:T(8,128)S(1)}, f32[36,8,128]{2,1,0:T(8,128)S(1)}, f32[30,16,8,128]{3,2,1,0:T(8,128)S(1)}) custom-call(f32[128,128]{1,0:T(8,128)S(1)} %get-tuple-element.27.own_ref, f32[8,16,128]{2,1,0:T(8,128)S(1)} %collective-permute-done.first_ref, ...), custom_call_target="tpu_custom_call" | custom-call | tf_op jit(solution)/shard_map/pallas_call | solution.py:497
  9.1 2.2 %collective-permute-start.9 = (f32[36,8,128]{2,1,0:T(8,128)S(1)}, f32[36,8,128]{2,1,0:T(8,128)S(1)}, u32[]{:S(2)}, u32[]{:S(2)}) collective-permute-start(f32[36,8,128]{2,1,0:T(8,128)S(1)} %get-tuple-element.32), channel_id=1, source_target_pairs={{0,6},{1,7},{2,4},{3,5},{4,2},{5,3},{6,0},{7,1},{8,14},{9,15},{10,... | collective-permute-start | bytes 442376 | tf_op jit(solution)/shard_map/ppermute | solution.py:36
  11.3 0.2 collective-permute-start.8
  11.6 0.3 collective-permute-start.7
  11.8 2.9 %collective-permute-start.2 = (f32[5,8,128]{2,1,0:T(8,128)S(1)}, f32[5,8,128]{2,1,0:T(8,128)S(1)}, u32[]{:S(2)}, u32[]{:S(2)}) collective-permute-start(f32[5,8,128]{2,1,0:T(8,128)S(1)} %get-tuple-element.22), channel_id=1, source_target_pairs={{0,1},{2,3},{4,5},{6,7},{1,0},{3,2},{5,4},{7,6},{8,9},{10,11},{12,... | collective-permute-start | bytes 61448 | tf_op jit(solution)/shard_map/ppermute | solution.py:31
  14.8 3.0 %collective-permute-start.3 = (f32[5,8,128]{2,1,0:T(8,128)S(1)}, f32[5,8,128]{2,1,0:T(8,128)S(1)}, u32[]{:S(2)}, u32[]{:S(2)}) collective-permute-start(f32[5,8,128]{2,1,0:T(8,128)S(1)} %get-tuple-element.23), channel_id=1, source_target_pairs={{1,2},{3,4},{5,6},{2,1},{4,3},{6,5},{9,10},{11,12},{13,14},{10,9},... | collective-permute-start | bytes 61448 | tf_op jit(solution)/shard_map/ppermute | solution.py:31
  17.8 0.0 collective-permute-done.2.jfirst_ref
  17.8 2.4 %collective-permute-done.3.jsecond_ref = f32[5,8,128]{2,1,0:T(8,128)S(1)} collective-permute-done((f32[5,8,128]{2,1,0:T(8,128)S(1)}, f32[5,8,128]{2,1,0:T(8,128)S(1)}, u32[]{:S(2)}, u32[]{:S(2)}) %collective-permute-start.3) | collective-permute-done | bytes 20512 | tf_op jit(solution)/shard_map/ppermute | solution.py:31
  20.1 0.3 shard_map.70
  20.4 0.1 collective-permute-start.4
  20.5 1.9 %collective-permute-start.5 = (f32[3,4,16,128]{3,2,1,0:T(8,128)S(1)}, f32[3,4,16,128]{3,2,1,0:T(8,128)S(1)}, u32[]{:S(2)}, u32[]{:S(2)}) collective-permute-start(f32[3,4,16,128]{3,2,1,0:T(8,128)S(1)} %get-tuple-element.26), channel_id=1, source_target_pairs={{8,16},{16,8},{9,17},{17,9},{10,18},{18,10},{11,19},{19,11},{12,20... | collective-permute-start | bytes 294920 | tf_op jit(solution)/shard_map/ppermute | solution.py:31
  22.4 0.0 collective-permute-done.9
  22.5 0.0 collective-permute-done.8
  22.5 0.0 collective-permute-done.7
  22.5 0.1 collective-permute-start.10
  22.6 1.4 %collective-permute-done.4.first_ref = f32[3,4,16,128]{3,2,1,0:T(8,128)S(1)} collective-permute-done((f32[3,4,16,128]{3,2,1,0:T(8,128)S(1)}, f32[3,4,16,128]{3,2,1,0:T(8,128)S(1)}, u32[]{:S(2)}, u32[]{:S(2)}) %collective-permute-start.4) | collective-permute-done | bytes 98336 | tf_op jit(solution)/shard_map/ppermute | solution.py:31
  24.0 1.9 %collective-permute-done.5.second_ref = f32[3,4,16,128]{3,2,1,0:T(8,128)S(1)} collective-permute-done((f32[3,4,16,128]{3,2,1,0:T(8,128)S(1)}, f32[3,4,16,128]{3,2,1,0:T(8,128)S(1)}, u32[]{:S(2)}, u32[]{:S(2)}) %collective-permute-start.5) | collective-permute-done | bytes 98336 | tf_op jit(solution)/shard_map/ppermute | solution.py:31
  25.9 0.9 %shard_map.72 = (f32[18,8,128]{2,1,0:T(8,128)S(1)}, f32[3,16,8,128]{3,2,1,0:T(8,128)S(1)}) custom-call(f32[3,8,16,128]{3,2,1,0:T(8,128)S(1)} %get-tuple-element.24.own_ref, f32[3,4,16,128]{3,2,1,0:T(8,128)S(1)} %collective-permute-done.4.first_ref, f32[3,4,16,128]{3,2,1,0:T(8,128)S(1)} %collective-permute-done.5.second_ref, ...), custom_call_target="tpu_custom_call" | custom-call | tf_op jit(solution)/shard_map/pallas_call | solution.py:497
  26.8 0.1 collective-permute-start.14
  26.9 3.6 %collective-permute-start.13 = (f32[18,8,128]{2,1,0:T(8,128)S(1)}, f32[18,8,128]{2,1,0:T(8,128)S(1)}, u32[]{:S(2)}, u32[]{:S(2)}) collective-permute-start(f32[18,8,128]{2,1,0:T(8,128)S(1)} %get-tuple-element.33), channel_id=1, source_target_pairs={{0,4},{1,5},{2,6},{3,7},{4,0},{5,1},{6,2},{7,3},{8,12},{9,13},{10,... | collective-permute-start | bytes 221192 | tf_op jit(solution)/shard_map/ppermute | solution.py:36
  30.5 0.0 collective-permute-start.12
  30.5 0.5 %collective-permute-done.14 = f32[18,8,128]{2,1,0:T(8,128)S(1)} collective-permute-done((f32[18,8,128]{2,1,0:T(8,128)S(1)}, f32[18,8,128]{2,1,0:T(8,128)S(1)}, u32[]{:S(2)}, u32[]{:S(2)}) %collective-permute-start.14) | collective-permute-done | bytes 73760 | tf_op jit(solution)/shard_map/ppermute | solution.py:36
  30.9 1.6 %collective-permute-done.13 = f32[18,8,128]{2,1,0:T(8,128)S(1)} collective-permute-done((f32[18,8,128]{2,1,0:T(8,128)S(1)}, f32[18,8,128]{2,1,0:T(8,128)S(1)}, u32[]{:S(2)}, u32[]{:S(2)}) %collective-permute-start.13) | collective-permute-done | bytes 73760 | tf_op jit(solution)/shard_map/ppermute | solution.py:36
  32.6 1.5 %collective-permute-done.12 = f32[18,8,128]{2,1,0:T(8,128)S(1)} collective-permute-done((f32[18,8,128]{2,1,0:T(8,128)S(1)}, f32[18,8,128]{2,1,0:T(8,128)S(1)}, u32[]{:S(2)}, u32[]{:S(2)}) %collective-permute-start.12) | collective-permute-done | bytes 73760 | tf_op jit(solution)/shard_map/ppermute | solution.py:36
  34.1 1.6 %collective-permute-start.15 = (f32[3,18,8,128]{3,2,1,0:T(8,128)S(1)}, f32[3,18,8,128]{3,2,1,0:T(8,128)S(1)}, u32[]{:S(2)}, u32[]{:S(2)}) collective-permute-start(f32[3,18,8,128]{3,2,1,0:T(8,128)S(1)} %pad_maximum_fusion.1.refs_6_), channel_id=1, source_target_pairs={{0,1},{1,0},{2,3},{3,2},{4,5},{5,4},{6,7},{7,6},{8,9},{9,8},{10,11... | collective-permute-start | bytes 663560 | tf_op jit(solution)/shard_map/ppermute | solution.py:36
  35.7 0.1 collective-permute-start.6
  35.8 0.4 %collective-permute-start.11 = (f32[18,8,128]{2,1,0:T(8,128)S(1)}, f32[18,8,128]{2,1,0:T(8,128)S(1)}, u32[]{:S(2)}, u32[]{:S(2)}) collective-permute-start(f32[18,8,128]{2,1,0:T(8,128)S(1)} %get-tuple-element.33), channel_id=1, source_target_pairs={{0,1},{1,0},{2,3},{3,2},{4,5},{5,4},{6,7},{7,6},{8,9},{9,8},{10,11... | collective-permute-start | bytes 221192 | tf_op jit(solution)/shard_map/ppermute | solution.py:36
  36.2 0.0 copy-done
  36.2 1.9 %shard_map.69 = f32[5,8,16,128]{3,2,1,0:T(8,128)} custom-call(f32[5,8,16,128]{3,2,1,0:T(8,128)S(1)} %bitcast.16, f32[5,8,16,128]{3,2,1,0:T(8,128)S(1)} %bitcast.18, f32[6,3,8,16,128]{4,3,2,1,0:T(8,128)S(1)} %copy-done, f32[8,16,128]{2,1,0:T(8,128)S(1)} %collective-permute-done.first_ref, f32[8,16,128]{2,1,0:T(8,128)S(1)} %collective-permute-done.1.second_ref, ...), custom_call_target="tpu_custom_call" | custom-call | tf_op jit(solution)/shard_map/pallas_call | solution.py:497
  38.2 0.0 collective-permute-done.6
  38.2 0.0 collective-permute-done.11
  38.2 0.0 collective-permute-done.15.refs_7_
  38.2 0.0 collective-permute-done.10.refs_4_
  38.2 2.5 %shard_map.73 = f32[3,128,128]{2,1,0:T(8,128)} custom-call(f32[3,16,8,128]{3,2,1,0:T(8,128)S(1)} %get-tuple-element.30.refs_0_, f32[30,16,8,128]{3,2,1,0:T(8,128)S(1)} %get-tuple-element.31.refs_1_, f32[1,36,8,128]{3,2,1,0:T(8,128)S(1)} %bitcast.19, f32[3,36,8,128]{3,2,1,0:T(8,128)S(1)} %pad_maximum_fusion.refs_3_, ...), custom_call_target="tpu_custom_call" | custom-call | tf_op jit(solution)/shard_map/pallas_call | solution.py:497
  (2 shorter events, 0.1 us)
Async XLA Ops:
  0.6 35.6 %copy-start = (f32[6,3,8,16,128]{4,3,2,1,0:T(8,128)S(1)}, f32[6,3,8,16,128]{4,3,2,1,0:T(8,128)}, u32[]{:S(2)}) copy-start(f32[6,3,8,16,128]{4,3,2,1,0:T(8,128)} %faces_ref.1) | copy-start | bytes 3538948
  1.9 3.3 %collective-permute-start = (f32[8,16,128]{2,1,0:T(8,128)S(1)}, f32[8,16,128]{2,1,0:T(8,128)S(1)}, u32[]{:S(2)}, u32[]{:S(2)}) collective-permute-start(f32[8,16,128]{2,1,0:T(8,128)S(1)} %get-tuple-element.20), channel_id=1, source_target_pairs={{0,8},{16,24},{8,0},{24,16},{1,9},{17,25},{9,1},{25,17},{2,10},{18... | collective-permute-start | bytes 196616 | tf_op jit(solution)/shard_map/ppermute | solution.py:31
  3.3 5.0 %collective-permute-start.1 = (f32[8,16,128]{2,1,0:T(8,128)S(1)}, f32[8,16,128]{2,1,0:T(8,128)S(1)}, u32[]{:S(2)}, u32[]{:S(2)}) collective-permute-start(f32[8,16,128]{2,1,0:T(8,128)S(1)} %get-tuple-element.21), channel_id=1, source_target_pairs={{8,16},{16,8},{9,17},{17,9},{10,18},{18,10},{11,19},{19,11},{12,20... | collective-permute-start | bytes 196616 | tf_op jit(solution)/shard_map/ppermute | solution.py:31
  9.1 13.4 %collective-permute-start.9 = (f32[36,8,128]{2,1,0:T(8,128)S(1)}, f32[36,8,128]{2,1,0:T(8,128)S(1)}, u32[]{:S(2)}, u32[]{:S(2)}) collective-permute-start(f32[36,8,128]{2,1,0:T(8,128)S(1)} %get-tuple-element.32), channel_id=1, source_target_pairs={{0,6},{1,7},{2,4},{3,5},{4,2},{5,3},{6,0},{7,1},{8,14},{9,15},{10,... | collective-permute-start | bytes 442376 | tf_op jit(solution)/shard_map/ppermute | solution.py:36
  11.3 11.1 %collective-permute-start.8 = (f32[36,8,128]{2,1,0:T(8,128)S(1)}, f32[36,8,128]{2,1,0:T(8,128)S(1)}, u32[]{:S(2)}, u32[]{:S(2)}) collective-permute-start(f32[36,8,128]{2,1,0:T(8,128)S(1)} %get-tuple-element.32), channel_id=1, source_target_pairs={{0,4},{1,5},{2,6},{3,7},{4,0},{5,1},{6,2},{7,3},{8,12},{9,13},{10,... | collective-permute-start | bytes 442376 | tf_op jit(solution)/shard_map/ppermute | solution.py:36
  11.6 10.9 %collective-permute-start.7 = (f32[36,8,128]{2,1,0:T(8,128)S(1)}, f32[36,8,128]{2,1,0:T(8,128)S(1)}, u32[]{:S(2)}, u32[]{:S(2)}) collective-permute-start(f32[36,8,128]{2,1,0:T(8,128)S(1)} %get-tuple-element.32), channel_id=1, source_target_pairs={{0,2},{1,3},{2,0},{3,1},{4,6},{5,7},{6,4},{7,5},{8,10},{9,11},{10,... | collective-permute-start | bytes 442376 | tf_op jit(solution)/shard_map/ppermute | solution.py:36
  11.8 6.0 %collective-permute-start.2 = (f32[5,8,128]{2,1,0:T(8,128)S(1)}, f32[5,8,128]{2,1,0:T(8,128)S(1)}, u32[]{:S(2)}, u32[]{:S(2)}) collective-permute-start(f32[5,8,128]{2,1,0:T(8,128)S(1)} %get-tuple-element.22), channel_id=1, source_target_pairs={{0,1},{2,3},{4,5},{6,7},{1,0},{3,2},{5,4},{7,6},{8,9},{10,11},{12,... | collective-permute-start | bytes 61448 | tf_op jit(solution)/shard_map/ppermute | solution.py:31
  14.8 5.4 %collective-permute-start.3 = (f32[5,8,128]{2,1,0:T(8,128)S(1)}, f32[5,8,128]{2,1,0:T(8,128)S(1)}, u32[]{:S(2)}, u32[]{:S(2)}) collective-permute-start(f32[5,8,128]{2,1,0:T(8,128)S(1)} %get-tuple-element.23), channel_id=1, source_target_pairs={{1,2},{3,4},{5,6},{2,1},{4,3},{6,5},{9,10},{11,12},{13,14},{10,9},... | collective-permute-start | bytes 61448 | tf_op jit(solution)/shard_map/ppermute | solution.py:31
  20.4 3.5 %collective-permute-start.4 = (f32[3,4,16,128]{3,2,1,0:T(8,128)S(1)}, f32[3,4,16,128]{3,2,1,0:T(8,128)S(1)}, u32[]{:S(2)}, u32[]{:S(2)}) collective-permute-start(f32[3,4,16,128]{3,2,1,0:T(8,128)S(1)} %get-tuple-element.25), channel_id=1, source_target_pairs={{0,8},{16,24},{8,0},{24,16},{1,9},{17,25},{9,1},{25,17},{2,10},{18... | collective-permute-start | bytes 294920 | tf_op jit(solution)/shard_map/ppermute | solution.py:31
  20.5 5.4 %collective-permute-start.5 = (f32[3,4,16,128]{3,2,1,0:T(8,128)S(1)}, f32[3,4,16,128]{3,2,1,0:T(8,128)S(1)}, u32[]{:S(2)}, u32[]{:S(2)}) collective-permute-start(f32[3,4,16,128]{3,2,1,0:T(8,128)S(1)} %get-tuple-element.26), channel_id=1, source_target_pairs={{8,16},{16,8},{9,17},{17,9},{10,18},{18,10},{11,19},{19,11},{12,20... | collective-permute-start | bytes 294920 | tf_op jit(solution)/shard_map/ppermute | solution.py:31
  22.5 15.7 %collective-permute-start.10 = (f32[3,36,8,128]{3,2,1,0:T(8,128)S(1)}, f32[3,36,8,128]{3,2,1,0:T(8,128)S(1)}, u32[]{:S(2)}, u32[]{:S(2)}) collective-permute-start(f32[3,36,8,128]{3,2,1,0:T(8,128)S(1)} %pad_maximum_fusion.refs_3_), channel_id=1, source_target_pairs={{0,1},{1,0},{2,3},{3,2},{4,5},{5,4},{6,7},{7,6},{8,9},{9,8},{10,11... | collective-permute-start | bytes 1327112 | tf_op jit(solution)/shard_map/ppermute | solution.py:36
  26.8 4.2 %collective-permute-start.14 = (f32[18,8,128]{2,1,0:T(8,128)S(1)}, f32[18,8,128]{2,1,0:T(8,128)S(1)}, u32[]{:S(2)}, u32[]{:S(2)}) collective-permute-start(f32[18,8,128]{2,1,0:T(8,128)S(1)} %get-tuple-element.33), channel_id=1, source_target_pairs={{0,6},{1,7},{2,4},{3,5},{4,2},{5,3},{6,0},{7,1},{8,14},{9,15},{10,... | collective-permute-start | bytes 221192 | tf_op jit(solution)/shard_map/ppermute | solution.py:36
  26.9 5.7 %collective-permute-start.13 = (f32[18,8,128]{2,1,0:T(8,128)S(1)}, f32[18,8,128]{2,1,0:T(8,128)S(1)}, u32[]{:S(2)}, u32[]{:S(2)}) collective-permute-start(f32[18,8,128]{2,1,0:T(8,128)S(1)} %get-tuple-element.33), channel_id=1, source_target_pairs={{0,4},{1,5},{2,6},{3,7},{4,0},{5,1},{6,2},{7,3},{8,12},{9,13},{10,... | collective-permute-start | bytes 221192 | tf_op jit(solution)/shard_map/ppermute | solution.py:36
  30.5 3.6 %collective-permute-start.12 = (f32[18,8,128]{2,1,0:T(8,128)S(1)}, f32[18,8,128]{2,1,0:T(8,128)S(1)}, u32[]{:S(2)}, u32[]{:S(2)}) collective-permute-start(f32[18,8,128]{2,1,0:T(8,128)S(1)} %get-tuple-element.33), channel_id=1, source_target_pairs={{0,2},{1,3},{2,0},{3,1},{4,6},{5,7},{6,4},{7,5},{8,10},{9,11},{10,... | collective-permute-start | bytes 221192 | tf_op jit(solution)/shard_map/ppermute | solution.py:36
  34.1 4.0 %collective-permute-start.15 = (f32[3,18,8,128]{3,2,1,0:T(8,128)S(1)}, f32[3,18,8,128]{3,2,1,0:T(8,128)S(1)}, u32[]{:S(2)}, u32[]{:S(2)}) collective-permute-start(f32[3,18,8,128]{3,2,1,0:T(8,128)S(1)} %pad_maximum_fusion.1.refs_6_), channel_id=1, source_target_pairs={{0,1},{1,0},{2,3},{3,2},{4,5},{5,4},{6,7},{7,6},{8,9},{9,8},{10,11... | collective-permute-start | bytes 663560 | tf_op jit(solution)/shard_map/ppermute | solution.py:36
  35.7 2.5 %collective-permute-start.6 = (f32[36,8,128]{2,1,0:T(8,128)S(1)}, f32[36,8,128]{2,1,0:T(8,128)S(1)}, u32[]{:S(2)}, u32[]{:S(2)}) collective-permute-start(f32[36,8,128]{2,1,0:T(8,128)S(1)} %get-tuple-element.32), channel_id=1, source_target_pairs={{0,1},{1,0},{2,3},{3,2},{4,5},{5,4},{6,7},{7,6},{8,9},{9,8},{10,11... | collective-permute-start | bytes 442376 | tf_op jit(solution)/shard_map/ppermute | solution.py:36
  35.8 2.4 %collective-permute-start.11 = (f32[18,8,128]{2,1,0:T(8,128)S(1)}, f32[18,8,128]{2,1,0:T(8,128)S(1)}, u32[]{:S(2)}, u32[]{:S(2)}) collective-permute-start(f32[18,8,128]{2,1,0:T(8,128)S(1)} %get-tuple-element.33), channel_id=1, source_target_pairs={{0,1},{1,0},{2,3},{3,2},{4,5},{5,4},{6,7},{7,6},{8,9},{9,8},{10,11... | collective-permute-start | bytes 221192 | tf_op jit(solution)/shard_map/ppermute | solution.py:36

commit v4 on v3

--- a/solution.py
+++ b/solution.py
@@ -280,55 +280,58 @@
     return ends_at
 
 
-def volume_kernel(
-    flow_ref, adj_ref, first_ref, second_ref, jfirst_ref, jsecond_ref,
-    v_ref, out1_ref, out2_ref, *, nj,
-):
+def volume_part(flow, jump):
+    rho, m, energy = flow[0], flow[1:4], flow[4]
+    inv = 1.0 / rho
+    u = [x * inv for x in m]
+    mu = m[0] * u[0] + m[1] * u[1] + m[2] * u[2]
+    pressure = GAS * (energy - 0.5 * mu)
+    q = (
+        rho * jump[0]
+        + (m[0] * jump[1] + m[1] * jump[2] + m[2] * jump[3])
+        + (energy + pressure) * jump[4]
+    )
+    return [0.5 * (u[comp] * q + pressure * jump[comp + 1]) for comp in range(3)]
+
+
+def volume_kernel(flow_ref, adj_ref, jfirst_ref, jsecond_ref, v_ref, out1_ref, out2_ref, *, nj):
     own, lanes = flow_ref.shape[1], flow_ref.shape[-1]
     w = SWEEPS
     even = lax.axis_index("bx") % 2 == 0
     jeven = lax.axis_index("by") % 2 == 0
     sub = lax.broadcasted_iota(jnp.int32, (nj, lanes), 0)
-
-    def adjoint_at(comp, i):
-        if 0 <= i < own:
-            return adj_ref[comp, i]
-        if i >= own:
-            return jnp.where(even, first_ref[comp], second_ref[comp])
-        return jnp.where(even, second_ref[comp], first_ref[comp])
-
     for i in range(own):
         jump = []
         for comp in range(5):
-            here = adjoint_at(comp, i)
-            diff = adjoint_at(comp, i - 1) - adjoint_at(comp, i + 1)
+            here = adj_ref[comp, i]
+            if i == 0:
+                diff = -adj_ref[comp, 1]
+            elif i == own - 1:
+                diff = adj_ref[comp, own - 2]
+            else:
+                diff = adj_ref[comp, i - 1] - adj_ref[comp, i + 1]
             one, two = jfirst_ref[comp, i : i + 1, :], jsecond_ref[comp, i : i + 1, :]
             back = jnp.where(sub == 0, jnp.where(jeven, two, one), pltpu.roll(here, 1, 0))
             ahead = jnp.where(
                 sub == nj - 1, jnp.where(jeven, one, two), pltpu.roll(here, nj - 1, 0)
             )
             jump.append(diff + (back - ahead) + (edge_k(here, -1) - edge_k(here, 1)))
-        rho = flow_ref[0, i]
-        m = [flow_ref[comp, i] for comp in (1, 2, 3)]
-        energy = flow_ref[4, i]
-        inv = 1.0 / rho
-        u = [x * inv for x in m]
-        mu = m[0] * u[0] + m[1] * u[1] + m[2] * u[2]
-        pressure = GAS * (energy - 0.5 * mu)
-        q = (
-            rho * jump[0]
-            + (m[0] * jump[1] + m[1] * jump[2] + m[2] * jump[3])
-            + (energy + pressure) * jump[4]
-        )
+        part = volume_part([flow_ref[comp, i] for comp in range(5)], jump)
         for comp in range(3):
-            v_ref[comp, i] = 0.5 * (u[comp] * q + pressure * jump[comp + 1])
-    low, high = v_ref[:, 0:w], v_ref[:, own - w : own]
-    out1_ref[...] = jnp.where(even, high, low)
-    out2_ref[...] = jnp.where(even, low, high)
+            v_ref[comp, i] = part[comp]
+    for comp in range(3):
+        low, high = v_ref[comp, 0:w], v_ref[comp, own - w : own]
+        out1_ref[comp * w : (comp + 1) * w] = jnp.where(even, high, low)
+        out2_ref[comp * w : (comp + 1) * w] = jnp.where(even, low, high)
+    for comp in range(5):
+        low, high = flow_ref[comp, 0], flow_ref[comp, own - 1]
+        out1_ref[3 * w + comp] = jnp.where(even, high, low)
+        out2_ref[3 * w + comp] = jnp.where(even, low, high)
 
 
 def offsets_kernel(
-    own_ref, first_ref, second_ref, rate_t, gain_t, off_ref, last_ref, v_ref, warp_ref, *, rows, nj,
+    own_ref, first_ref, second_ref, flow_ref, adj_ref, rim1_ref, rim2_ref, rate_t, gain_t,
+    off_ref, last_ref, v_ref, warp_ref, *, rows, nj,
 ):
     lanes = own_ref.shape[-1]
     own = rows - 2 * SWEEPS
@@ -336,10 +339,30 @@
     even = lax.axis_index("bx") % 2 == 0
     for comp in range(3):
         v_ref[comp, 0 : own * nj, :] = own_ref[comp].reshape(own * nj, lanes)
-        one = first_ref[comp].reshape(w * nj, lanes)
-        two = second_ref[comp].reshape(w * nj, lanes)
+        one = first_ref[comp * w : (comp + 1) * w].reshape(w * nj, lanes)
+        two = second_ref[comp * w : (comp + 1) * w].reshape(w * nj, lanes)
         v_ref[comp, own * nj : (own + w) * nj, :] = jnp.where(even, one, two)
         v_ref[comp, (own + w) * nj : rows * nj, :] = jnp.where(even, two, one)
+
+    place, count = lax.axis_index("bx"), lax.axis_size("bx")
+    reach = range(5)
+    rim_up = [jnp.where(even, rim1_ref[c], rim2_ref[c]) for c in reach]
+    rim_low = [jnp.where(even, rim2_ref[c], rim1_ref[c]) for c in reach]
+    at = 3 * w
+    flow_up = [jnp.where(even, first_ref[at + c], second_ref[at + c]) for c in reach]
+    flow_low = [jnp.where(even, second_ref[at + c], first_ref[at + c]) for c in reach]
+
+    def add(row, flow, adjoint, sign, inside):
+        part = volume_part(flow, adjoint)
+        for comp in range(3):
+            lines = slice(row * nj, (row + 1) * nj)
+            term = part[comp] if inside is None else jnp.where(inside, part[comp], 0.0)
+            v_ref[comp, lines, :] = v_ref[comp, lines, :] + sign * term
+
+    add(0, [flow_ref[c, 0] for c in reach], rim_low, 1.0, None)
+    add(own - 1, [flow_ref[c, own - 1] for c in reach], rim_up, -1.0, None)
+    add(own, flow_up, [adj_ref[c, own - 1] for c in reach], 1.0, place < count - 1)
+    add(rows - 1, flow_low, [adj_ref[c, 0] for c in reach], -1.0, place > 0)
 
     ends_at = sweeps(v_ref, rate_t, gain_t, warp_ref, rows, nj, last_ref)
     places, _ = off_layout(own)
@@ -543,11 +566,11 @@
     l1, l2 = swap(l1, "by", 0), swap(l2, "by", 1)
     m1, m2 = swap(m1, "bx", 0), swap(m2, "bx", 1)
 
-    halo = shape(3, w, nj, lanes)
+    halo = shape(3 * w + 5, nj, lanes)
     inner, h1, h2 = run(
         functools.partial(volume_kernel, nj=nj),
         [shape(3, own, nj, lanes), halo, halo],
-        [flow, adjoint, m1, m2, l1, l2],
+        [flow, adjoint, l1, l2],
     )
     h1, h2 = swap(h1, "bx", 0), swap(h2, "bx", 1)
 
@@ -572,7 +595,7 @@
     offs, last = run(
         functools.partial(offsets_kernel, rows=rows, nj=nj),
         [shape(n_off, own, lanes), shape(3, nj, own, lanes)],
-        [inner, h1, h2, rate, gain],
+        [inner, h1, h2, flow, adjoint, m1, m2, rate, gain],
         [pltpu.VMEM((3, rows * nj, lanes), F32), pltpu.VMEM((SWEEPS, 3, nj, 2, own, lanes), F32)],
     )
     all_offs = collect(offs, "by")

time: 40.8 us -> 41.6 us (1.020)
  starting transfers between devices: 19.8 us -> 20.3 us
    ppermute x10, starting transfers between devices: 8.55 us -> 9.1 us  [flip(): return lax.ppermute(x, axis, [(i, i ^ mask) for i in range(count)])]
    ppermute x6, waiting for transfers between devices: 8.73 us -> 9.17 us  [swap(): return lax.ppermute(x, axis, matching(axis, first))]
  transfers between devices with their start and end apart: 16 -> 16, of which waited for: 7 -> 6; matrix products, arithmetic and copies ran while one was open for 0% -> 0% of each run, Pallas kernels for 8% -> 8%
where the time goes in v4:
time: 41.6 us; the launch traced here: 41.5 us
  starting transfers between devices  20.3 us (49%)
  waiting for transfers between devices  12.7 us (31%)
  Pallas kernels  7.6 us (18%)
  between operations  0.78 us (2%)
    ppermute x6, starting transfers between devices, swap(): return lax.ppermute(x, axis, matching(axis, first))  11.2 us
    ppermute x6, waiting for transfers between devices, swap(): return lax.ppermute(x, axis, matching(axis, first))  9.17 us
    ppermute x10, starting transfers between devices, flip(): return lax.ppermute(x, axis, [(i, i ^ mask) for i in range(count)])  9.1 us
    pallas_call x6, Pallas kernels, call(): pl.pallas_call(kernel, out_shape=out_shape, in_specs=[pl.BlockSpec(memory...  7.6 us
    ppermute x10, waiting for transfers between devices, flip(): return lax.ppermute(x, axis, [(i, i ^ mask) for i in range(count)])  3.55 us
  transfers between devices with their start and end apart: 16, of which 6 were waited for; matrix products, arithmetic and copies ran while one was open for 0% of the time, Pallas kernels for 8%

profile of v4, /device:TPU:17, one launch (start us, length us, event | category | flops | bytes accessed | tf_op | source)
XLA Modules:
  0.0 41.5 jit_solution(8630352302813150302)
XLA Ops:
  0.6 1.2 %shard_map.68 = (f32[5,128,128]{2,1,0:T(8,128)S(1)}, f32[5,128,128]{2,1,0:T(8,128)S(1)}, f32[128,128]{1,0:T(8,128)S(1)}, f32[5,8,128]{2,1,0:T(8,128)S(1)}, f32[5...) custom-call(f32[5,128,128]{2,1,0:T(8,128)} %bitcast.23, f32[5,128,128]{2,1,0:T(8,128)} %bitcast.24, ...), custom_call_target="tpu_custom_call" | custom-call | tf_op jit(solution)/shard_map/pallas_call | solution.py:520
  1.8 0.0 copy-start
  1.8 1.4 %collective-permute-start = (f32[8,16,128]{2,1,0:T(8,128)S(1)}, f32[8,16,128]{2,1,0:T(8,128)S(1)}, u32[]{:S(2)}, u32[]{:S(2)}) collective-permute-start(f32[8,16,128]{2,1,0:T(8,128)S(1)} %get-tuple-element.20), channel_id=1, source_target_pairs={{0,8},{16,24},{8,0},{24,16},{1,9},{17,25},{9,1},{25,17},{2,10},{18... | collective-permute-start | bytes 196616 | tf_op jit(solution)/shard_map/ppermute | solution.py:31
  3.2 1.9 %collective-permute-start.1 = (f32[8,16,128]{2,1,0:T(8,128)S(1)}, f32[8,16,128]{2,1,0:T(8,128)S(1)}, u32[]{:S(2)}, u32[]{:S(2)}) collective-permute-start(f32[8,16,128]{2,1,0:T(8,128)S(1)} %get-tuple-element.21), channel_id=1, source_target_pairs={{8,16},{16,8},{9,17},{17,9},{10,18},{18,10},{11,19},{19,11},{12,20... | collective-permute-start | bytes 196616 | tf_op jit(solution)/shard_map/ppermute | solution.py:31
  5.1 0.0 collective-permute-done.first_ref.rim1_ref
  5.1 3.1 %collective-permute-done.1.second_ref.rim2_ref = f32[8,16,128]{2,1,0:T(8,128)S(1)} collective-permute-done((f32[8,16,128]{2,1,0:T(8,128)S(1)}, f32[8,16,128]{2,1,0:T(8,128)S(1)}, u32[]{:S(2)}, u32[]{:S(2)}) %collective-permute-start.1) | collective-permute-done | bytes 65568 | tf_op jit(solution)/shard_map/ppermute | solution.py:31
  8.2 0.8 %shard_map.71 = (f32[16,2,8,128]{3,2,1,0:T(8,128)S(1)}, f32[16,2,8,128]{3,2,1,0:T(8,128)S(1)}, f32[36,8,128]{2,1,0:T(8,128)S(1)}, f32[30,16,8,128]{3,2,1,0:T(8,128)S(1)}) custom-call(f32[128,128]{1,0:T(8,128)S(1)} %get-tuple-element.27.own_ref, f32[8,16,128]{2,1,0:T(8,128)S(1)} %collective-permute-done.first_ref.rim1_ref, ...), custom_call_target="tpu_custom_call" | custom-call | tf_op jit(solution)/shard_map/pallas_call | solution.py:520
  9.0 2.2 %collective-permute-start.9 = (f32[36,8,128]{2,1,0:T(8,128)S(1)}, f32[36,8,128]{2,1,0:T(8,128)S(1)}, u32[]{:S(2)}, u32[]{:S(2)}) collective-permute-start(f32[36,8,128]{2,1,0:T(8,128)S(1)} %get-tuple-element.32), channel_id=1, source_target_pairs={{0,6},{1,7},{2,4},{3,5},{4,2},{5,3},{6,0},{7,1},{8,14},{9,15},{10,... | collective-permute-start | bytes 442376 | tf_op jit(solution)/shard_map/ppermute | solution.py:36
  11.2 0.2 collective-permute-start.8
  11.5 0.3 collective-permute-start.7
  11.7 2.9 %collective-permute-start.2 = (f32[5,8,128]{2,1,0:T(8,128)S(1)}, f32[5,8,128]{2,1,0:T(8,128)S(1)}, u32[]{:S(2)}, u32[]{:S(2)}) collective-permute-start(f32[5,8,128]{2,1,0:T(8,128)S(1)} %get-tuple-element.22), channel_id=1, source_target_pairs={{0,1},{2,3},{4,5},{6,7},{1,0},{3,2},{5,4},{7,6},{8,9},{10,11},{12,... | collective-permute-start | bytes 61448 | tf_op jit(solution)/shard_map/ppermute | solution.py:31
  14.7 3.0 %collective-permute-start.3 = (f32[5,8,128]{2,1,0:T(8,128)S(1)}, f32[5,8,128]{2,1,0:T(8,128)S(1)}, u32[]{:S(2)}, u32[]{:S(2)}) collective-permute-start(f32[5,8,128]{2,1,0:T(8,128)S(1)} %get-tuple-element.23), channel_id=1, source_target_pairs={{1,2},{3,4},{5,6},{2,1},{4,3},{6,5},{9,10},{11,12},{13,14},{10,9},... | collective-permute-start | bytes 61448 | tf_op jit(solution)/shard_map/ppermute | solution.py:31
  17.7 0.0 collective-permute-done.2.jfirst_ref
  17.7 2.4 %collective-permute-done.3.jsecond_ref = f32[5,8,128]{2,1,0:T(8,128)S(1)} collective-permute-done((f32[5,8,128]{2,1,0:T(8,128)S(1)}, f32[5,8,128]{2,1,0:T(8,128)S(1)}, u32[]{:S(2)}, u32[]{:S(2)}) %collective-permute-start.3) | collective-permute-done | bytes 20512 | tf_op jit(solution)/shard_map/ppermute | solution.py:31
  20.0 0.3 shard_map.70
  20.3 0.1 collective-permute-start.4
  20.4 1.9 %collective-permute-start.5 = (f32[17,16,128]{2,1,0:T(8,128)S(1)}, f32[17,16,128]{2,1,0:T(8,128)S(1)}, u32[]{:S(2)}, u32[]{:S(2)}) collective-permute-start(f32[17,16,128]{2,1,0:T(8,128)S(1)} %get-tuple-element.26), channel_id=1, source_target_pairs={{8,16},{16,8},{9,17},{17,9},{10,18},{18,10},{11,19},{19,11},{12,20... | collective-permute-start | bytes 417800 | tf_op jit(solution)/shard_map/ppermute | solution.py:31
  22.4 0.0 collective-permute-done.9
  22.4 0.0 collective-permute-done.8
  22.4 0.0 collective-permute-done.7
  22.4 0.1 collective-permute-start.10
  22.5 1.8 %collective-permute-done.4.first_ref = f32[17,16,128]{2,1,0:T(8,128)S(1)} collective-permute-done((f32[17,16,128]{2,1,0:T(8,128)S(1)}, f32[17,16,128]{2,1,0:T(8,128)S(1)}, u32[]{:S(2)}, u32[]{:S(2)}) %collective-permute-start.4) | collective-permute-done | bytes 139296 | tf_op jit(solution)/shard_map/ppermute | solution.py:31
  24.3 1.9 %collective-permute-done.5.second_ref = f32[17,16,128]{2,1,0:T(8,128)S(1)} collective-permute-done((f32[17,16,128]{2,1,0:T(8,128)S(1)}, f32[17,16,128]{2,1,0:T(8,128)S(1)}, u32[]{:S(2)}, u32[]{:S(2)}) %collective-permute-start.5) | collective-permute-done | bytes 139296 | tf_op jit(solution)/shard_map/ppermute | solution.py:31
  26.2 0.9 %shard_map.72 = (f32[18,8,128]{2,1,0:T(8,128)S(1)}, f32[3,16,8,128]{3,2,1,0:T(8,128)S(1)}) custom-call(f32[3,8,16,128]{3,2,1,0:T(8,128)S(1)} %get-tuple-element.24.own_ref, f32[17,16,128]{2,1,0:T(8,128)S(1)} %collective-permute-done.4.first_ref, f32[17,16,128]{2,1,0:T(8,128)S(1)} %collective-permute-done.5.second_ref, f32[5,8,16,128]{3,2,1,0:T(8,128)S(1)} %bitcast.16, ...), custom_call_target="tpu_custom_call" | custom-call | tf_op jit(solution)/shard_map/pallas_call | solution.py:520
  27.1 0.1 collective-permute-start.14
  27.2 4.0 %collective-permute-start.13 = (f32[18,8,128]{2,1,0:T(8,128)S(1)}, f32[18,8,128]{2,1,0:T(8,128)S(1)}, u32[]{:S(2)}, u32[]{:S(2)}) collective-permute-start(f32[18,8,128]{2,1,0:T(8,128)S(1)} %get-tuple-element.33), channel_id=1, source_target_pairs={{0,4},{1,5},{2,6},{3,7},{4,0},{5,1},{6,2},{7,3},{8,12},{9,13},{10,... | collective-permute-start | bytes 221192 | tf_op jit(solution)/shard_map/ppermute | solution.py:36
  31.2 0.0 collective-permute-start.12
  31.2 0.0 collective-permute-done.14
  31.3 1.7 %collective-permute-done.13 = f32[18,8,128]{2,1,0:T(8,128)S(1)} collective-permute-done((f32[18,8,128]{2,1,0:T(8,128)S(1)}, f32[18,8,128]{2,1,0:T(8,128)S(1)}, u32[]{:S(2)}, u32[]{:S(2)}) %collective-permute-start.13) | collective-permute-done | bytes 73760 | tf_op jit(solution)/shard_map/ppermute | solution.py:36
  33.0 1.8 %collective-permute-done.12 = f32[18,8,128]{2,1,0:T(8,128)S(1)} collective-permute-done((f32[18,8,128]{2,1,0:T(8,128)S(1)}, f32[18,8,128]{2,1,0:T(8,128)S(1)}, u32[]{:S(2)}, u32[]{:S(2)}) %collective-permute-start.12) | collective-permute-done | bytes 73760 | tf_op jit(solution)/shard_map/ppermute | solution.py:36
  34.8 1.7 %collective-permute-start.15 = (f32[3,18,8,128]{3,2,1,0:T(8,128)S(1)}, f32[3,18,8,128]{3,2,1,0:T(8,128)S(1)}, u32[]{:S(2)}, u32[]{:S(2)}) collective-permute-start(f32[3,18,8,128]{3,2,1,0:T(8,128)S(1)} %pad_maximum_fusion.1.refs_6_), channel_id=1, source_target_pairs={{0,1},{1,0},{2,3},{3,2},{4,5},{5,4},{6,7},{7,6},{8,9},{9,8},{10,11... | collective-permute-start | bytes 663560 | tf_op jit(solution)/shard_map/ppermute | solution.py:36
  36.5 0.1 collective-permute-start.6
  36.6 0.4 %collective-permute-start.11 = (f32[18,8,128]{2,1,0:T(8,128)S(1)}, f32[18,8,128]{2,1,0:T(8,128)S(1)}, u32[]{:S(2)}, u32[]{:S(2)}) collective-permute-start(f32[18,8,128]{2,1,0:T(8,128)S(1)} %get-tuple-element.33), channel_id=1, source_target_pairs={{0,1},{1,0},{2,3},{3,2},{4,5},{5,4},{6,7},{7,6},{8,9},{9,8},{10,11... | collective-permute-start | bytes 221192 | tf_op jit(solution)/shard_map/ppermute | solution.py:36
  37.0 0.0 copy-done
  37.0 1.9 %shard_map.69 = f32[5,8,16,128]{3,2,1,0:T(8,128)} custom-call(f32[5,8,16,128]{3,2,1,0:T(8,128)S(1)} %bitcast.17, f32[5,8,16,128]{3,2,1,0:T(8,128)S(1)} %bitcast.20, f32[6,3,8,16,128]{4,3,2,1,0:T(8,128)S(1)} %copy-done, f32[8,16,128]{2,1,0:T(8,128)S(1)} %collective-permute-done.first_ref.rim1_ref, ...), custom_call_target="tpu_custom_call" | custom-call | tf_op jit(solution)/shard_map/pallas_call | solution.py:520
  38.9 0.0 collective-permute-done.6
  39.0 0.0 collective-permute-done.11
  39.0 0.0 collective-permute-done.15.refs_7_
  39.0 0.0 collective-permute-done.10.refs_4_
  39.0 2.5 %shard_map.73 = f32[3,128,128]{2,1,0:T(8,128)} custom-call(f32[3,16,8,128]{3,2,1,0:T(8,128)S(1)} %get-tuple-element.30.refs_0_, f32[30,16,8,128]{3,2,1,0:T(8,128)S(1)} %get-tuple-element.31.refs_1_, f32[1,36,8,128]{3,2,1,0:T(8,128)S(1)} %bitcast.21, f32[3,36,8,128]{3,2,1,0:T(8,128)S(1)} %pad_maximum_fusion.refs_3_, ...), custom_call_target="tpu_custom_call" | custom-call | tf_op jit(solution)/shard_map/pallas_call | solution.py:520
  (2 shorter events, 0.1 us)
Async XLA Ops:
  1.8 35.2 %copy-start = (f32[6,3,8,16,128]{4,3,2,1,0:T(8,128)S(1)}, f32[6,3,8,16,128]{4,3,2,1,0:T(8,128)}, u32[]{:S(2)}) copy-start(f32[6,3,8,16,128]{4,3,2,1,0:T(8,128)} %faces_ref.1) | copy-start | bytes 3538948
  1.8 3.3 %collective-permute-start = (f32[8,16,128]{2,1,0:T(8,128)S(1)}, f32[8,16,128]{2,1,0:T(8,128)S(1)}, u32[]{:S(2)}, u32[]{:S(2)}) collective-permute-start(f32[8,16,128]{2,1,0:T(8,128)S(1)} %get-tuple-element.20), channel_id=1, source_target_pairs={{0,8},{16,24},{8,0},{24,16},{1,9},{17,25},{9,1},{25,17},{2,10},{18... | collective-permute-start | bytes 196616 | tf_op jit(solution)/shard_map/ppermute | solution.py:31
  3.2 5.0 %collective-permute-start.1 = (f32[8,16,128]{2,1,0:T(8,128)S(1)}, f32[8,16,128]{2,1,0:T(8,128)S(1)}, u32[]{:S(2)}, u32[]{:S(2)}) collective-permute-start(f32[8,16,128]{2,1,0:T(8,128)S(1)} %get-tuple-element.21), channel_id=1, source_target_pairs={{8,16},{16,8},{9,17},{17,9},{10,18},{18,10},{11,19},{19,11},{12,20... | collective-permute-start | bytes 196616 | tf_op jit(solution)/shard_map/ppermute | solution.py:31
  9.0 13.4 %collective-permute-start.9 = (f32[36,8,128]{2,1,0:T(8,128)S(1)}, f32[36,8,128]{2,1,0:T(8,128)S(1)}, u32[]{:S(2)}, u32[]{:S(2)}) collective-permute-start(f32[36,8,128]{2,1,0:T(8,128)S(1)} %get-tuple-element.32), channel_id=1, source_target_pairs={{0,6},{1,7},{2,4},{3,5},{4,2},{5,3},{6,0},{7,1},{8,14},{9,15},{10,... | collective-permute-start | bytes 442376 | tf_op jit(solution)/shard_map/ppermute | solution.py:36
  11.2 11.1 %collective-permute-start.8 = (f32[36,8,128]{2,1,0:T(8,128)S(1)}, f32[36,8,128]{2,1,0:T(8,128)S(1)}, u32[]{:S(2)}, u32[]{:S(2)}) collective-permute-start(f32[36,8,128]{2,1,0:T(8,128)S(1)} %get-tuple-element.32), channel_id=1, source_target_pairs={{0,4},{1,5},{2,6},{3,7},{4,0},{5,1},{6,2},{7,3},{8,12},{9,13},{10,... | collective-permute-start | bytes 442376 | tf_op jit(solution)/shard_map/ppermute | solution.py:36
  11.5 10.9 %collective-permute-start.7 = (f32[36,8,128]{2,1,0:T(8,128)S(1)}, f32[36,8,128]{2,1,0:T(8,128)S(1)}, u32[]{:S(2)}, u32[]{:S(2)}) collective-permute-start(f32[36,8,128]{2,1,0:T(8,128)S(1)} %get-tuple-element.32), channel_id=1, source_target_pairs={{0,2},{1,3},{2,0},{3,1},{4,6},{5,7},{6,4},{7,5},{8,10},{9,11},{10,... | collective-permute-start | bytes 442376 | tf_op jit(solution)/shard_map/ppermute | solution.py:36
  11.7 6.0 %collective-permute-start.2 = (f32[5,8,128]{2,1,0:T(8,128)S(1)}, f32[5,8,128]{2,1,0:T(8,128)S(1)}, u32[]{:S(2)}, u32[]{:S(2)}) collective-permute-start(f32[5,8,128]{2,1,0:T(8,128)S(1)} %get-tuple-element.22), channel_id=1, source_target_pairs={{0,1},{2,3},{4,5},{6,7},{1,0},{3,2},{5,4},{7,6},{8,9},{10,11},{12,... | collective-permute-start | bytes 61448 | tf_op jit(solution)/shard_map/ppermute | solution.py:31
  14.7 5.4 %collective-permute-start.3 = (f32[5,8,128]{2,1,0:T(8,128)S(1)}, f32[5,8,128]{2,1,0:T(8,128)S(1)}, u32[]{:S(2)}, u32[]{:S(2)}) collective-permute-start(f32[5,8,128]{2,1,0:T(8,128)S(1)} %get-tuple-element.23), channel_id=1, source_target_pairs={{1,2},{3,4},{5,6},{2,1},{4,3},{6,5},{9,10},{11,12},{13,14},{10,9},... | collective-permute-start | bytes 61448 | tf_op jit(solution)/shard_map/ppermute | solution.py:31
  20.3 4.0 %collective-permute-start.4 = (f32[17,16,128]{2,1,0:T(8,128)S(1)}, f32[17,16,128]{2,1,0:T(8,128)S(1)}, u32[]{:S(2)}, u32[]{:S(2)}) collective-permute-start(f32[17,16,128]{2,1,0:T(8,128)S(1)} %get-tuple-element.25), channel_id=1, source_target_pairs={{0,8},{16,24},{8,0},{24,16},{1,9},{17,25},{9,1},{25,17},{2,10},{18... | collective-permute-start | bytes 417800 | tf_op jit(solution)/shard_map/ppermute | solution.py:31
  20.4 5.8 %collective-permute-start.5 = (f32[17,16,128]{2,1,0:T(8,128)S(1)}, f32[17,16,128]{2,1,0:T(8,128)S(1)}, u32[]{:S(2)}, u32[]{:S(2)}) collective-permute-start(f32[17,16,128]{2,1,0:T(8,128)S(1)} %get-tuple-element.26), channel_id=1, source_target_pairs={{8,16},{16,8},{9,17},{17,9},{10,18},{18,10},{11,19},{19,11},{12,20... | collective-permute-start | bytes 417800 | tf_op jit(solution)/shard_map/ppermute | solution.py:31
  22.4 16.5 %collective-permute-start.10 = (f32[3,36,8,128]{3,2,1,0:T(8,128)S(1)}, f32[3,36,8,128]{3,2,1,0:T(8,128)S(1)}, u32[]{:S(2)}, u32[]{:S(2)}) collective-permute-start(f32[3,36,8,128]{3,2,1,0:T(8,128)S(1)} %pad_maximum_fusion.refs_3_), channel_id=1, source_target_pairs={{0,1},{1,0},{2,3},{3,2},{4,5},{5,4},{6,7},{7,6},{8,9},{9,8},{10,11... | collective-permute-start | bytes 1327112 | tf_op jit(solution)/shard_map/ppermute | solution.py:36
  27.1 4.2 %collective-permute-start.14 = (f32[18,8,128]{2,1,0:T(8,128)S(1)}, f32[18,8,128]{2,1,0:T(8,128)S(1)}, u32[]{:S(2)}, u32[]{:S(2)}) collective-permute-start(f32[18,8,128]{2,1,0:T(8,128)S(1)} %get-tuple-element.33), channel_id=1, source_target_pairs={{0,6},{1,7},{2,4},{3,5},{4,2},{5,3},{6,0},{7,1},{8,14},{9,15},{10,... | collective-permute-start | bytes 221192 | tf_op jit(solution)/shard_map/ppermute | solution.py:36
  27.2 5.8 %collective-permute-start.13 = (f32[18,8,128]{2,1,0:T(8,128)S(1)}, f32[18,8,128]{2,1,0:T(8,128)S(1)}, u32[]{:S(2)}, u32[]{:S(2)}) collective-permute-start(f32[18,8,128]{2,1,0:T(8,128)S(1)} %get-tuple-element.33), channel_id=1, source_target_pairs={{0,4},{1,5},{2,6},{3,7},{4,0},{5,1},{6,2},{7,3},{8,12},{9,13},{10,... | collective-permute-start | bytes 221192 | tf_op jit(solution)/shard_map/ppermute | solution.py:36
  31.2 3.5 %collective-permute-start.12 = (f32[18,8,128]{2,1,0:T(8,128)S(1)}, f32[18,8,128]{2,1,0:T(8,128)S(1)}, u32[]{:S(2)}, u32[]{:S(2)}) collective-permute-start(f32[18,8,128]{2,1,0:T(8,128)S(1)} %get-tuple-element.33), channel_id=1, source_target_pairs={{0,2},{1,3},{2,0},{3,1},{4,6},{5,7},{6,4},{7,5},{8,10},{9,11},{10,... | collective-permute-start | bytes 221192 | tf_op jit(solution)/shard_map/ppermute | solution.py:36
  34.8 4.2 %collective-permute-start.15 = (f32[3,18,8,128]{3,2,1,0:T(8,128)S(1)}, f32[3,18,8,128]{3,2,1,0:T(8,128)S(1)}, u32[]{:S(2)}, u32[]{:S(2)}) collective-permute-start(f32[3,18,8,128]{3,2,1,0:T(8,128)S(1)} %pad_maximum_fusion.1.refs_6_), channel_id=1, source_target_pairs={{0,1},{1,0},{2,3},{3,2},{4,5},{5,4},{6,7},{7,6},{8,9},{9,8},{10,11... | collective-permute-start | bytes 663560 | tf_op jit(solution)/shard_map/ppermute | solution.py:36
  36.5 2.5 %collective-permute-start.6 = (f32[36,8,128]{2,1,0:T(8,128)S(1)}, f32[36,8,128]{2,1,0:T(8,128)S(1)}, u32[]{:S(2)}, u32[]{:S(2)}) collective-permute-start(f32[36,8,128]{2,1,0:T(8,128)S(1)} %get-tuple-element.32), channel_id=1, source_target_pairs={{0,1},{1,0},{2,3},{3,2},{4,5},{5,4},{6,7},{7,6},{8,9},{9,8},{10,11... | collective-permute-start | bytes 442376 | tf_op jit(solution)/shard_map/ppermute | solution.py:36
  36.6 2.4 %collective-permute-start.11 = (f32[18,8,128]{2,1,0:T(8,128)S(1)}, f32[18,8,128]{2,1,0:T(8,128)S(1)}, u32[]{:S(2)}, u32[]{:S(2)}) collective-permute-start(f32[18,8,128]{2,1,0:T(8,128)S(1)} %get-tuple-element.33), channel_id=1, source_target_pairs={{0,1},{1,0},{2,3},{3,2},{4,5},{5,4},{6,7},{7,6},{8,9},{9,8},{10,11... | collective-permute-start | bytes 221192 | tf_op jit(solution)/shard_map/ppermute | solution.py:36

commit v5 on v4

--- a/solution.py
+++ b/solution.py
@@ -21,14 +21,16 @@
     )
 
 
-def matching(axis, first):
+def matching(axis, first, closed):
     count = lax.axis_size(axis)
     pairs = [(i, i + 1) for i in range(first, count - 1, 2)]
+    if closed and first and count % 2 == 0 and count > 2:
+        pairs.append((0, count - 1))
     return pairs + [(b, a) for a, b in pairs]
 
 
-def swap(x, axis, first):
-    return lax.ppermute(x, axis, matching(axis, first))
+def swap(x, axis, first, closed=False):
+    return lax.ppermute(x, axis, matching(axis, first, closed))
 
 
 def flip(x, axis, mask):
@@ -111,12 +113,14 @@
         copy.start()
     even = lax.axis_index("bx") % 2 == 0
     jeven = lax.axis_index("by") % 2 == 0
+    place = lax.axis_index("by")
+    inner = (place > 0) & (place < lax.axis_size("by") - 1)
     copies[0].wait()
     for comp in range(5):
         bottom = adj_ref[comp, pl.ds(0, own, stride=nj), :]
         top = adj_ref[comp, pl.ds(nj - 1, own, stride=nj), :]
         line1_ref[comp] = jnp.where(jeven, top, bottom)
-        line2_ref[comp] = jnp.where(jeven, bottom, top)
+        line2_ref[comp] = jnp.where(inner, jnp.where(jeven, bottom, top), 0.0)
         low = adj_ref[comp, 0:nj, :]
         high = adj_ref[comp, (own - 1) * nj : own * nj, :]
         rim1_ref[comp] = jnp.where(even, high, low)
@@ -563,7 +567,7 @@
         pltpu.HBM,
     )
     flow, adjoint = flow.reshape(5, own, nj, lanes), adjoint.reshape(5, own, nj, lanes)
-    l1, l2 = swap(l1, "by", 0), swap(l2, "by", 1)
+    l1, l2 = swap(l1, "by", 0), swap(l2, "by", 1, closed=True)
     m1, m2 = swap(m1, "bx", 0), swap(m2, "bx", 1)
 
     halo = shape(3 * w + 5, nj, lanes)

time: 41.6 us -> 40.6 us (0.976)
  starting transfers between devices: 20.3 us -> 15.9 us
  waiting for transfers between devices: 12.7 us -> 16.1 us
    ppermute x6, waiting for transfers between devices: 9.17 us -> 12.1 us  [swap(): return lax.ppermute(x, axis, matching(axis, first, closed))]
    ppermute x10, starting transfers between devices: 9.1 us -> 6.61 us  [flip(): return lax.ppermute(x, axis, [(i, i ^ mask) for i in range(count)])]
    ppermute x6, starting transfers between devices: 11.2 us -> 9.3 us  [swap(): return lax.ppermute(x, axis, matching(axis, first, closed))]
    ppermute x10, waiting for transfers between devices: 3.55 us -> 4 us  [flip(): return lax.ppermute(x, axis, [(i, i ^ mask) for i in range(count)])]
where the time goes in v5:
time: 40.6 us; the launch traced here: 40.5 us
  waiting for transfers between devices  16.1 us (40%)
  starting transfers between devices  15.9 us (39%)
  Pallas kernels  7.6 us (19%)
  between operations  0.75 us (2%)
    ppermute x6, waiting for transfers between devices, swap(): return lax.ppermute(x, axis, matching(axis, first, closed))  12.1 us
    ppermute x6, starting transfers between devices, swap(): return lax.ppermute(x, axis, matching(axis, first, closed))  9.3 us
    pallas_call x6, Pallas kernels, call(): pl.pallas_call(kernel, out_shape=out_shape, in_specs=[pl.BlockSpec(memory...  7.6 us
    ppermute x10, starting transfers between devices, flip(): return lax.ppermute(x, axis, [(i, i ^ mask) for i in range(count)])  6.61 us
    ppermute x10, waiting for transfers between devices, flip(): return lax.ppermute(x, axis, [(i, i ^ mask) for i in range(count)])  4 us
  transfers between devices with their start and end apart: 16, of which 6 were waited for; matrix products, arithmetic and copies ran while one was open for 0% of the time, Pallas kernels for 8%

profile of v5, /device:TPU:17, one launch (start us, length us, event | category | flops | bytes accessed | tf_op | source)
XLA Modules:
  0.0 40.5 jit_solution(18261839541666528736)
XLA Ops:
  0.6 1.2 %shard_map.68 = (f32[5,128,128]{2,1,0:T(8,128)S(1)}, f32[5,128,128]{2,1,0:T(8,128)S(1)}, f32[128,128]{1,0:T(8,128)S(1)}, f32[5,8,128]{2,1,0:T(8,128)S(1)}, f32[5...) custom-call(f32[5,128,128]{2,1,0:T(8,128)} %bitcast.23, f32[5,128,128]{2,1,0:T(8,128)} %bitcast.24, ...), custom_call_target="tpu_custom_call" | custom-call | tf_op jit(solution)/shard_map/pallas_call | solution.py:524
  1.8 0.0 copy-start
  1.8 1.4 %collective-permute-start = (f32[8,16,128]{2,1,0:T(8,128)S(1)}, f32[8,16,128]{2,1,0:T(8,128)S(1)}, u32[]{:S(2)}, u32[]{:S(2)}) collective-permute-start(f32[8,16,128]{2,1,0:T(8,128)S(1)} %get-tuple-element.20), channel_id=1, source_target_pairs={{0,8},{16,24},{8,0},{24,16},{1,9},{17,25},{9,1},{25,17},{2,10},{18... | collective-permute-start | bytes 196616 | tf_op jit(solution)/shard_map/ppermute | solution.py:33
  3.2 1.9 %collective-permute-start.1 = (f32[8,16,128]{2,1,0:T(8,128)S(1)}, f32[8,16,128]{2,1,0:T(8,128)S(1)}, u32[]{:S(2)}, u32[]{:S(2)}) collective-permute-start(f32[8,16,128]{2,1,0:T(8,128)S(1)} %get-tuple-element.21), channel_id=1, source_target_pairs={{8,16},{16,8},{9,17},{17,9},{10,18},{18,10},{11,19},{19,11},{12,20... | collective-permute-start | bytes 196616 | tf_op jit(solution)/shard_map/ppermute | solution.py:33
  5.1 0.0 collective-permute-done.first_ref.rim1_ref
  5.1 3.1 %collective-permute-done.1.second_ref.rim2_ref = f32[8,16,128]{2,1,0:T(8,128)S(1)} collective-permute-done((f32[8,16,128]{2,1,0:T(8,128)S(1)}, f32[8,16,128]{2,1,0:T(8,128)S(1)}, u32[]{:S(2)}, u32[]{:S(2)}) %collective-permute-start.1) | collective-permute-done | bytes 65568 | tf_op jit(solution)/shard_map/ppermute | solution.py:33
  8.2 0.8 %shard_map.71 = (f32[16,2,8,128]{3,2,1,0:T(8,128)S(1)}, f32[16,2,8,128]{3,2,1,0:T(8,128)S(1)}, f32[36,8,128]{2,1,0:T(8,128)S(1)}, f32[30,16,8,128]{3,2,1,0:T(8,128)S(1)}) custom-call(f32[128,128]{1,0:T(8,128)S(1)} %get-tuple-element.27.own_ref, f32[8,16,128]{2,1,0:T(8,128)S(1)} %collective-permute-done.first_ref.rim1_ref, ...), custom_call_target="tpu_custom_call" | custom-call | tf_op jit(solution)/shard_map/pallas_call | solution.py:524
  9.0 2.2 %collective-permute-start.9 = (f32[36,8,128]{2,1,0:T(8,128)S(1)}, f32[36,8,128]{2,1,0:T(8,128)S(1)}, u32[]{:S(2)}, u32[]{:S(2)}) collective-permute-start(f32[36,8,128]{2,1,0:T(8,128)S(1)} %get-tuple-element.32), channel_id=1, source_target_pairs={{0,6},{1,7},{2,4},{3,5},{4,2},{5,3},{6,0},{7,1},{8,14},{9,15},{10,... | collective-permute-start | bytes 442376 | tf_op jit(solution)/shard_map/ppermute | solution.py:38
  11.2 0.2 collective-permute-start.8
  11.5 0.3 collective-permute-start.7
  11.7 2.9 %collective-permute-start.2 = (f32[5,8,128]{2,1,0:T(8,128)S(1)}, f32[5,8,128]{2,1,0:T(8,128)S(1)}, u32[]{:S(2)}, u32[]{:S(2)}) collective-permute-start(f32[5,8,128]{2,1,0:T(8,128)S(1)} %get-tuple-element.22), channel_id=1, source_target_pairs={{0,1},{2,3},{4,5},{6,7},{1,0},{3,2},{5,4},{7,6},{8,9},{10,11},{12,... | collective-permute-start | bytes 61448 | tf_op jit(solution)/shard_map/ppermute | solution.py:33
  14.7 1.1 %collective-permute-start.3 = (f32[5,8,128]{2,1,0:T(8,128)S(1)}, f32[5,8,128]{2,1,0:T(8,128)S(1)}, u32[]{:S(2)}, u32[]{:S(2)}) collective-permute-start(f32[5,8,128]{2,1,0:T(8,128)S(1)} %get-tuple-element.23), channel_id=1, source_target_pairs={{1,2},{3,4},{5,6},{0,7},{2,1},{4,3},{6,5},{7,0},{9,10},{11,12},{13... | collective-permute-start | bytes 61448 | tf_op jit(solution)/shard_map/ppermute | solution.py:33
  15.8 0.0 collective-permute-done.2.jfirst_ref
  15.8 3.6 %collective-permute-done.3.jsecond_ref = f32[5,8,128]{2,1,0:T(8,128)S(1)} collective-permute-done((f32[5,8,128]{2,1,0:T(8,128)S(1)}, f32[5,8,128]{2,1,0:T(8,128)S(1)}, u32[]{:S(2)}, u32[]{:S(2)}) %collective-permute-start.3) | collective-permute-done | bytes 20512 | tf_op jit(solution)/shard_map/ppermute | solution.py:33
  19.4 0.3 shard_map.70
  19.7 0.1 collective-permute-start.4
  19.8 1.9 %collective-permute-start.5 = (f32[17,16,128]{2,1,0:T(8,128)S(1)}, f32[17,16,128]{2,1,0:T(8,128)S(1)}, u32[]{:S(2)}, u32[]{:S(2)}) collective-permute-start(f32[17,16,128]{2,1,0:T(8,128)S(1)} %get-tuple-element.26), channel_id=1, source_target_pairs={{8,16},{16,8},{9,17},{17,9},{10,18},{18,10},{11,19},{19,11},{12,20... | collective-permute-start | bytes 417800 | tf_op jit(solution)/shard_map/ppermute | solution.py:33
  21.7 0.0 collective-permute-done.9
  21.7 0.0 collective-permute-done.8
  21.7 0.0 collective-permute-done.7
  21.8 0.1 collective-permute-start.10
  21.9 3.5 %collective-permute-done.4.first_ref = f32[17,16,128]{2,1,0:T(8,128)S(1)} collective-permute-done((f32[17,16,128]{2,1,0:T(8,128)S(1)}, f32[17,16,128]{2,1,0:T(8,128)S(1)}, u32[]{:S(2)}, u32[]{:S(2)}) %collective-permute-start.4) | collective-permute-done | bytes 139296 | tf_op jit(solution)/shard_map/ppermute | solution.py:33
  25.4 1.9 %collective-permute-done.5.second_ref = f32[17,16,128]{2,1,0:T(8,128)S(1)} collective-permute-done((f32[17,16,128]{2,1,0:T(8,128)S(1)}, f32[17,16,128]{2,1,0:T(8,128)S(1)}, u32[]{:S(2)}, u32[]{:S(2)}) %collective-permute-start.5) | collective-permute-done | bytes 139296 | tf_op jit(solution)/shard_map/ppermute | solution.py:33
  27.3 0.9 %shard_map.72 = (f32[18,8,128]{2,1,0:T(8,128)S(1)}, f32[3,16,8,128]{3,2,1,0:T(8,128)S(1)}) custom-call(f32[3,8,16,128]{3,2,1,0:T(8,128)S(1)} %get-tuple-element.24.own_ref, f32[17,16,128]{2,1,0:T(8,128)S(1)} %collective-permute-done.4.first_ref, f32[17,16,128]{2,1,0:T(8,128)S(1)} %collective-permute-done.5.second_ref, f32[5,8,16,128]{3,2,1,0:T(8,128)S(1)} %bitcast.16, ...), custom_call_target="tpu_custom_call" | custom-call | tf_op jit(solution)/shard_map/pallas_call | solution.py:524
  28.2 1.2 %collective-permute-start.14 = (f32[18,8,128]{2,1,0:T(8,128)S(1)}, f32[18,8,128]{2,1,0:T(8,128)S(1)}, u32[]{:S(2)}, u32[]{:S(2)}) collective-permute-start(f32[18,8,128]{2,1,0:T(8,128)S(1)} %get-tuple-element.33), channel_id=1, source_target_pairs={{0,6},{1,7},{2,4},{3,5},{4,2},{5,3},{6,0},{7,1},{8,14},{9,15},{10,... | collective-permute-start | bytes 221192 | tf_op jit(solution)/shard_map/ppermute | solution.py:38
  29.4 0.2 collective-permute-start.13
  29.6 1.3 %collective-permute-start.12 = (f32[18,8,128]{2,1,0:T(8,128)S(1)}, f32[18,8,128]{2,1,0:T(8,128)S(1)}, u32[]{:S(2)}, u32[]{:S(2)}) collective-permute-start(f32[18,8,128]{2,1,0:T(8,128)S(1)} %get-tuple-element.33), channel_id=1, source_target_pairs={{0,2},{1,3},{2,0},{3,1},{4,6},{5,7},{6,4},{7,5},{8,10},{9,11},{10,... | collective-permute-start | bytes 221192 | tf_op jit(solution)/shard_map/ppermute | solution.py:38
  30.9 1.5 %collective-permute-done.14 = f32[18,8,128]{2,1,0:T(8,128)S(1)} collective-permute-done((f32[18,8,128]{2,1,0:T(8,128)S(1)}, f32[18,8,128]{2,1,0:T(8,128)S(1)}, u32[]{:S(2)}, u32[]{:S(2)}) %collective-permute-start.14) | collective-permute-done | bytes 73760 | tf_op jit(solution)/shard_map/ppermute | solution.py:38
  32.4 2.5 %collective-permute-done.13 = f32[18,8,128]{2,1,0:T(8,128)S(1)} collective-permute-done((f32[18,8,128]{2,1,0:T(8,128)S(1)}, f32[18,8,128]{2,1,0:T(8,128)S(1)}, u32[]{:S(2)}, u32[]{:S(2)}) %collective-permute-start.13) | collective-permute-done | bytes 73760 | tf_op jit(solution)/shard_map/ppermute | solution.py:38
  34.9 0.0 collective-permute-done.12
  34.9 0.6 %collective-permute-start.15 = (f32[3,18,8,128]{3,2,1,0:T(8,128)S(1)}, f32[3,18,8,128]{3,2,1,0:T(8,128)S(1)}, u32[]{:S(2)}, u32[]{:S(2)}) collective-permute-start(f32[3,18,8,128]{3,2,1,0:T(8,128)S(1)} %pad_maximum_fusion.1.refs_6_), channel_id=1, source_target_pairs={{0,1},{1,0},{2,3},{3,2},{4,5},{5,4},{6,7},{7,6},{8,9},{9,8},{10,11... | collective-permute-start | bytes 663560 | tf_op jit(solution)/shard_map/ppermute | solution.py:38
  35.5 0.1 collective-permute-start.6
  35.6 0.4 %collective-permute-start.11 = (f32[18,8,128]{2,1,0:T(8,128)S(1)}, f32[18,8,128]{2,1,0:T(8,128)S(1)}, u32[]{:S(2)}, u32[]{:S(2)}) collective-permute-start(f32[18,8,128]{2,1,0:T(8,128)S(1)} %get-tuple-element.33), channel_id=1, source_target_pairs={{0,1},{1,0},{2,3},{3,2},{4,5},{5,4},{6,7},{7,6},{8,9},{9,8},{10,11... | collective-permute-start | bytes 221192 | tf_op jit(solution)/shard_map/ppermute | solution.py:38
  36.0 0.0 copy-done
  36.0 1.9 %shard_map.69 = f32[5,8,16,128]{3,2,1,0:T(8,128)} custom-call(f32[5,8,16,128]{3,2,1,0:T(8,128)S(1)} %bitcast.17, f32[5,8,16,128]{3,2,1,0:T(8,128)S(1)} %bitcast.20, f32[6,3,8,16,128]{4,3,2,1,0:T(8,128)S(1)} %copy-done, f32[8,16,128]{2,1,0:T(8,128)S(1)} %collective-permute-done.first_ref.rim1_ref, ...), custom_call_target="tpu_custom_call" | custom-call | tf_op jit(solution)/shard_map/pallas_call | solution.py:524
  38.0 0.0 collective-permute-done.6
  38.0 0.0 collective-permute-done.11
  38.0 0.0 collective-permute-done.15.refs_7_
  38.0 0.0 collective-permute-done.10.refs_4_
  38.0 2.5 %shard_map.73 = f32[3,128,128]{2,1,0:T(8,128)} custom-call(f32[3,16,8,128]{3,2,1,0:T(8,128)S(1)} %get-tuple-element.30.refs_0_, f32[30,16,8,128]{3,2,1,0:T(8,128)S(1)} %get-tuple-element.31.refs_1_, f32[1,36,8,128]{3,2,1,0:T(8,128)S(1)} %bitcast.21, f32[3,36,8,128]{3,2,1,0:T(8,128)S(1)} %pad_maximum_fusion.refs_3_, ...), custom_call_target="tpu_custom_call" | custom-call | tf_op jit(solution)/shard_map/pallas_call | solution.py:524
  (2 shorter events, 0.1 us)
Async XLA Ops:
  1.8 34.2 %copy-start = (f32[6,3,8,16,128]{4,3,2,1,0:T(8,128)S(1)}, f32[6,3,8,16,128]{4,3,2,1,0:T(8,128)}, u32[]{:S(2)}) copy-start(f32[6,3,8,16,128]{4,3,2,1,0:T(8,128)} %faces_ref.1) | copy-start | bytes 3538948
  1.8 3.3 %collective-permute-start = (f32[8,16,128]{2,1,0:T(8,128)S(1)}, f32[8,16,128]{2,1,0:T(8,128)S(1)}, u32[]{:S(2)}, u32[]{:S(2)}) collective-permute-start(f32[8,16,128]{2,1,0:T(8,128)S(1)} %get-tuple-element.20), channel_id=1, source_target_pairs={{0,8},{16,24},{8,0},{24,16},{1,9},{17,25},{9,1},{25,17},{2,10},{18... | collective-permute-start | bytes 196616 | tf_op jit(solution)/shard_map/ppermute | solution.py:33
  3.2 5.0 %collective-permute-start.1 = (f32[8,16,128]{2,1,0:T(8,128)S(1)}, f32[8,16,128]{2,1,0:T(8,128)S(1)}, u32[]{:S(2)}, u32[]{:S(2)}) collective-permute-start(f32[8,16,128]{2,1,0:T(8,128)S(1)} %get-tuple-element.21), channel_id=1, source_target_pairs={{8,16},{16,8},{9,17},{17,9},{10,18},{18,10},{11,19},{19,11},{12,20... | collective-permute-start | bytes 196616 | tf_op jit(solution)/shard_map/ppermute | solution.py:33
  9.0 12.7 %collective-permute-start.9 = (f32[36,8,128]{2,1,0:T(8,128)S(1)}, f32[36,8,128]{2,1,0:T(8,128)S(1)}, u32[]{:S(2)}, u32[]{:S(2)}) collective-permute-start(f32[36,8,128]{2,1,0:T(8,128)S(1)} %get-tuple-element.32), channel_id=1, source_target_pairs={{0,6},{1,7},{2,4},{3,5},{4,2},{5,3},{6,0},{7,1},{8,14},{9,15},{10,... | collective-permute-start | bytes 442376 | tf_op jit(solution)/shard_map/ppermute | solution.py:38
  11.2 10.5 %collective-permute-start.8 = (f32[36,8,128]{2,1,0:T(8,128)S(1)}, f32[36,8,128]{2,1,0:T(8,128)S(1)}, u32[]{:S(2)}, u32[]{:S(2)}) collective-permute-start(f32[36,8,128]{2,1,0:T(8,128)S(1)} %get-tuple-element.32), channel_id=1, source_target_pairs={{0,4},{1,5},{2,6},{3,7},{4,0},{5,1},{6,2},{7,3},{8,12},{9,13},{10,... | collective-permute-start | bytes 442376 | tf_op jit(solution)/shard_map/ppermute | solution.py:38
  11.5 10.3 %collective-permute-start.7 = (f32[36,8,128]{2,1,0:T(8,128)S(1)}, f32[36,8,128]{2,1,0:T(8,128)S(1)}, u32[]{:S(2)}, u32[]{:S(2)}) collective-permute-start(f32[36,8,128]{2,1,0:T(8,128)S(1)} %get-tuple-element.32), channel_id=1, source_target_pairs={{0,2},{1,3},{2,0},{3,1},{4,6},{5,7},{6,4},{7,5},{8,10},{9,11},{10,... | collective-permute-start | bytes 442376 | tf_op jit(solution)/shard_map/ppermute | solution.py:38
  11.7 4.0 %collective-permute-start.2 = (f32[5,8,128]{2,1,0:T(8,128)S(1)}, f32[5,8,128]{2,1,0:T(8,128)S(1)}, u32[]{:S(2)}, u32[]{:S(2)}) collective-permute-start(f32[5,8,128]{2,1,0:T(8,128)S(1)} %get-tuple-element.22), channel_id=1, source_target_pairs={{0,1},{2,3},{4,5},{6,7},{1,0},{3,2},{5,4},{7,6},{8,9},{10,11},{12,... | collective-permute-start | bytes 61448 | tf_op jit(solution)/shard_map/ppermute | solution.py:33
  14.7 4.7 %collective-permute-start.3 = (f32[5,8,128]{2,1,0:T(8,128)S(1)}, f32[5,8,128]{2,1,0:T(8,128)S(1)}, u32[]{:S(2)}, u32[]{:S(2)}) collective-permute-start(f32[5,8,128]{2,1,0:T(8,128)S(1)} %get-tuple-element.23), channel_id=1, source_target_pairs={{1,2},{3,4},{5,6},{0,7},{2,1},{4,3},{6,5},{7,0},{9,10},{11,12},{13... | collective-permute-start | bytes 61448 | tf_op jit(solution)/shard_map/ppermute | solution.py:33
  19.7 5.7 %collective-permute-start.4 = (f32[17,16,128]{2,1,0:T(8,128)S(1)}, f32[17,16,128]{2,1,0:T(8,128)S(1)}, u32[]{:S(2)}, u32[]{:S(2)}) collective-permute-start(f32[17,16,128]{2,1,0:T(8,128)S(1)} %get-tuple-element.25), channel_id=1, source_target_pairs={{0,8},{16,24},{8,0},{24,16},{1,9},{17,25},{9,1},{25,17},{2,10},{18... | collective-permute-start | bytes 417800 | tf_op jit(solution)/shard_map/ppermute | solution.py:33
  19.8 7.5 %collective-permute-start.5 = (f32[17,16,128]{2,1,0:T(8,128)S(1)}, f32[17,16,128]{2,1,0:T(8,128)S(1)}, u32[]{:S(2)}, u32[]{:S(2)}) collective-permute-start(f32[17,16,128]{2,1,0:T(8,128)S(1)} %get-tuple-element.26), channel_id=1, source_target_pairs={{8,16},{16,8},{9,17},{17,9},{10,18},{18,10},{11,19},{19,11},{12,20... | collective-permute-start | bytes 417800 | tf_op jit(solution)/shard_map/ppermute | solution.py:33
  21.8 16.2 %collective-permute-start.10 = (f32[3,36,8,128]{3,2,1,0:T(8,128)S(1)}, f32[3,36,8,128]{3,2,1,0:T(8,128)S(1)}, u32[]{:S(2)}, u32[]{:S(2)}) collective-permute-start(f32[3,36,8,128]{3,2,1,0:T(8,128)S(1)} %pad_maximum_fusion.refs_3_), channel_id=1, source_target_pairs={{0,1},{1,0},{2,3},{3,2},{4,5},{5,4},{6,7},{7,6},{8,9},{9,8},{10,11... | collective-permute-start | bytes 1327112 | tf_op jit(solution)/shard_map/ppermute | solution.py:38
  28.2 4.2 %collective-permute-start.14 = (f32[18,8,128]{2,1,0:T(8,128)S(1)}, f32[18,8,128]{2,1,0:T(8,128)S(1)}, u32[]{:S(2)}, u32[]{:S(2)}) collective-permute-start(f32[18,8,128]{2,1,0:T(8,128)S(1)} %get-tuple-element.33), channel_id=1, source_target_pairs={{0,6},{1,7},{2,4},{3,5},{4,2},{5,3},{6,0},{7,1},{8,14},{9,15},{10,... | collective-permute-start | bytes 221192 | tf_op jit(solution)/shard_map/ppermute | solution.py:38
  29.4 5.5 %collective-permute-start.13 = (f32[18,8,128]{2,1,0:T(8,128)S(1)}, f32[18,8,128]{2,1,0:T(8,128)S(1)}, u32[]{:S(2)}, u32[]{:S(2)}) collective-permute-start(f32[18,8,128]{2,1,0:T(8,128)S(1)} %get-tuple-element.33), channel_id=1, source_target_pairs={{0,4},{1,5},{2,6},{3,7},{4,0},{5,1},{6,2},{7,3},{8,12},{9,13},{10,... | collective-permute-start | bytes 221192 | tf_op jit(solution)/shard_map/ppermute | solution.py:38
  29.6 5.3 %collective-permute-start.12 = (f32[18,8,128]{2,1,0:T(8,128)S(1)}, f32[18,8,128]{2,1,0:T(8,128)S(1)}, u32[]{:S(2)}, u32[]{:S(2)}) collective-permute-start(f32[18,8,128]{2,1,0:T(8,128)S(1)} %get-tuple-element.33), channel_id=1, source_target_pairs={{0,2},{1,3},{2,0},{3,1},{4,6},{5,7},{6,4},{7,5},{8,10},{9,11},{10,... | collective-permute-start | bytes 221192 | tf_op jit(solution)/shard_map/ppermute | solution.py:38
  34.9 3.1 %collective-permute-start.15 = (f32[3,18,8,128]{3,2,1,0:T(8,128)S(1)}, f32[3,18,8,128]{3,2,1,0:T(8,128)S(1)}, u32[]{:S(2)}, u32[]{:S(2)}) collective-permute-start(f32[3,18,8,128]{3,2,1,0:T(8,128)S(1)} %pad_maximum_fusion.1.refs_6_), channel_id=1, source_target_pairs={{0,1},{1,0},{2,3},{3,2},{4,5},{5,4},{6,7},{7,6},{8,9},{9,8},{10,11... | collective-permute-start | bytes 663560 | tf_op jit(solution)/shard_map/ppermute | solution.py:38
  35.5 2.5 %collective-permute-start.6 = (f32[36,8,128]{2,1,0:T(8,128)S(1)}, f32[36,8,128]{2,1,0:T(8,128)S(1)}, u32[]{:S(2)}, u32[]{:S(2)}) collective-permute-start(f32[36,8,128]{2,1,0:T(8,128)S(1)} %get-tuple-element.32), channel_id=1, source_target_pairs={{0,1},{1,0},{2,3},{3,2},{4,5},{5,4},{6,7},{7,6},{8,9},{9,8},{10,11... | collective-permute-start | bytes 442376 | tf_op jit(solution)/shard_map/ppermute | solution.py:38
  35.6 2.4 %collective-permute-start.11 = (f32[18,8,128]{2,1,0:T(8,128)S(1)}, f32[18,8,128]{2,1,0:T(8,128)S(1)}, u32[]{:S(2)}, u32[]{:S(2)}) collective-permute-start(f32[18,8,128]{2,1,0:T(8,128)S(1)} %get-tuple-element.33), channel_id=1, source_target_pairs={{0,1},{1,0},{2,3},{3,2},{4,5},{5,4},{6,7},{7,6},{8,9},{9,8},{10,11... | collective-permute-start | bytes 221192 | tf_op jit(solution)/shard_map/ppermute | solution.py:38

commit v6 on v5

--- a/solution.py
+++ b/solution.py
@@ -60,10 +60,12 @@
 
 
 def shift_i(x, step, n):
+    if step == 0:
+        return x[:n]
     size = x[0].shape[0]
     turned = [pltpu.roll(tile, (-step) % size, 0) for tile in x]
     row = lax.broadcasted_iota(jnp.int32, x[0].shape, 0)
-    edge = row == (size - 1 if step > 0 else 0)
+    edge = row >= size - step if step > 0 else row < -step
     return [jnp.where(edge, turned[1 - t], turned[t]) for t in range(n)]
 
 
@@ -397,42 +399,55 @@
     def get(s, comp):
         return [x_ref[s, comp, t] for t in range(tiles(s))]
 
-    x_ref[...] = jnp.zeros(x_ref.shape, F32)
-
     def shifted(x, reach, n):
-        deep = max(abs(o[0]) for o in reach)
-        by_row = {0: x}
-        for step in range(1, deep + 1):
-            count_out = 2 if step < deep else n
-            by_row[step] = shift_i(by_row[step - 1], 1, count_out)
-            by_row[-step] = shift_i(by_row[1 - step], -1, count_out)
+        by_row = {i: shift_i(x, i, n) for i in sorted({o[0] for o in reach})}
         out = {}
         for i, k in reach:
             out[i, k] = [roll_k(tile, k) if k else tile for tile in by_row[i][:n]]
         return out
 
-    def through(hop, carry):
-        block = count - 1 - hop
+    def through(block, x):
         coef = {key: load_tiles(map_ref, block, place) for key, place in map_places.items()}
         fresh = {}
         for comp in range(3):
             total = [load_tiles(off_ref, block, off_places[s, comp]) for s in range(SWEEPS)]
-            for s in range(SWEEPS):
-                x = get(s, comp)
-                for d in range(SWEEPS - s):
-                    n = tiles(s + d)
-                    moved = shifted(x, REACH[d], n)
-                    for o in REACH[d]:
+            if x is not None:
+                for s in range(SWEEPS):
+                    for d in range(SWEEPS - s):
+                        n = tiles(s + d)
+                        moved = shifted(x[s, comp], REACH[d], n)
                         for t in range(n):
-                            total[s + d][t] = total[s + d][t] + coef[d, o][t] * moved[o][t]
+                            terms = [coef[d, o][t] * moved[o][t] for o in REACH[d]]
+                            while len(terms) > 1:
+                                pairs = [terms[i : i + 2] for i in range(0, len(terms), 2)]
+                                terms = [functools.reduce(jnp.add, pair) for pair in pairs]
+                            total[s + d][t] = total[s + d][t] + terms[0]
             for s in range(SWEEPS):
                 fresh[s, comp] = total[s]
-        for (s, comp), value in fresh.items():
+        return fresh
+
+    if direct(count):
+        x = None
+        for block in range(count - 1, 0, -1):
+            fresh = through(block, x)
+            for key, value in fresh.items():
+                held = [jnp.zeros_like(tile) for tile in value] if x is None else x[key]
+                fresh[key] = [jnp.where(block > me, a, b) for a, b in zip(value, held)]
+            x = fresh
+        for (s, comp), value in x.items():
             for t, tile in enumerate(value):
                 x_ref[s, comp, t] = tile
-        return carry
-
-    lax.fori_loop(0, count - 1 - me, through, 0)
+    else:
+
+        def step(hop, carry):
+            x = {(s, comp): get(s, comp) for s in range(SWEEPS) for comp in range(3)}
+            for (s, comp), value in through(count - 1 - hop, x).items():
+                for t, tile in enumerate(value):
+                    x_ref[s, comp, t] = tile
+            return carry
+
+        x_ref[...] = jnp.zeros(x_ref.shape, F32)
+        lax.fori_loop(0, count - 1 - me, step, 0)
 
     for comp in range(3):
         at = 0

time: 40.6 us -> 40.2 us (level)
  no operation moved by 1% of the time
where the time goes in v6:
time: 40.2 us; the launch traced here: 40.1 us
  waiting for transfers between devices  16.1 us (40%)
  starting transfers between devices  15.9 us (40%)
  Pallas kernels  7.21 us (18%)
  between operations  0.75 us (2%)
    ppermute x6, waiting for transfers between devices, swap(): return lax.ppermute(x, axis, matching(axis, first, closed))  12.1 us
    ppermute x6, starting transfers between devices, swap(): return lax.ppermute(x, axis, matching(axis, first, closed))  9.3 us
    pallas_call x6, Pallas kernels, call(): pl.pallas_call(kernel, out_shape=out_shape, in_specs=[pl.BlockSpec(memory...  7.21 us
    ppermute x10, starting transfers between devices, flip(): return lax.ppermute(x, axis, [(i, i ^ mask) for i in range(count)])  6.61 us
    ppermute x10, waiting for transfers between devices, flip(): return lax.ppermute(x, axis, [(i, i ^ mask) for i in range(count)])  4 us
  transfers between devices with their start and end apart: 16, of which 6 were waited for; matrix products, arithmetic and copies ran while one was open for 0% of the time, Pallas kernels for 8%

profile of v6, /device:TPU:17, one launch (start us, length us, event | category | flops | bytes accessed | tf_op | source)
XLA Modules:
  0.0 40.1 jit_solution(10003453029780561645)
XLA Ops:
  0.6 1.2 %shard_map.68 = (f32[5,128,128]{2,1,0:T(8,128)S(1)}, f32[5,128,128]{2,1,0:T(8,128)S(1)}, f32[128,128]{1,0:T(8,128)S(1)}, f32[5,8,128]{2,1,0:T(8,128)S(1)}, f32[5...) custom-call(f32[5,128,128]{2,1,0:T(8,128)} %bitcast.23, f32[5,128,128]{2,1,0:T(8,128)} %bitcast.24, ...), custom_call_target="tpu_custom_call" | custom-call | tf_op jit(solution)/shard_map/pallas_call | solution.py:539
  1.8 0.0 copy-start
  1.8 1.4 %collective-permute-start = (f32[8,16,128]{2,1,0:T(8,128)S(1)}, f32[8,16,128]{2,1,0:T(8,128)S(1)}, u32[]{:S(2)}, u32[]{:S(2)}) collective-permute-start(f32[8,16,128]{2,1,0:T(8,128)S(1)} %get-tuple-element.20), channel_id=1, source_target_pairs={{0,8},{16,24},{8,0},{24,16},{1,9},{17,25},{9,1},{25,17},{2,10},{18... | collective-permute-start | bytes 196616 | tf_op jit(solution)/shard_map/ppermute | solution.py:33
  3.2 1.9 %collective-permute-start.1 = (f32[8,16,128]{2,1,0:T(8,128)S(1)}, f32[8,16,128]{2,1,0:T(8,128)S(1)}, u32[]{:S(2)}, u32[]{:S(2)}) collective-permute-start(f32[8,16,128]{2,1,0:T(8,128)S(1)} %get-tuple-element.21), channel_id=1, source_target_pairs={{8,16},{16,8},{9,17},{17,9},{10,18},{18,10},{11,19},{19,11},{12,20... | collective-permute-start | bytes 196616 | tf_op jit(solution)/shard_map/ppermute | solution.py:33
  5.1 0.0 collective-permute-done.first_ref.rim1_ref
  5.1 3.1 %collective-permute-done.1.second_ref.rim2_ref = f32[8,16,128]{2,1,0:T(8,128)S(1)} collective-permute-done((f32[8,16,128]{2,1,0:T(8,128)S(1)}, f32[8,16,128]{2,1,0:T(8,128)S(1)}, u32[]{:S(2)}, u32[]{:S(2)}) %collective-permute-start.1) | collective-permute-done | bytes 65568 | tf_op jit(solution)/shard_map/ppermute | solution.py:33
  8.2 0.8 %shard_map.71 = (f32[16,2,8,128]{3,2,1,0:T(8,128)S(1)}, f32[16,2,8,128]{3,2,1,0:T(8,128)S(1)}, f32[36,8,128]{2,1,0:T(8,128)S(1)}, f32[30,16,8,128]{3,2,1,0:T(8,128)S(1)}) custom-call(f32[128,128]{1,0:T(8,128)S(1)} %get-tuple-element.27.own_ref, f32[8,16,128]{2,1,0:T(8,128)S(1)} %collective-permute-done.first_ref.rim1_ref, ...), custom_call_target="tpu_custom_call" | custom-call | tf_op jit(solution)/shard_map/pallas_call | solution.py:539
  9.0 2.2 %collective-permute-start.9 = (f32[36,8,128]{2,1,0:T(8,128)S(1)}, f32[36,8,128]{2,1,0:T(8,128)S(1)}, u32[]{:S(2)}, u32[]{:S(2)}) collective-permute-start(f32[36,8,128]{2,1,0:T(8,128)S(1)} %get-tuple-element.32), channel_id=1, source_target_pairs={{0,6},{1,7},{2,4},{3,5},{4,2},{5,3},{6,0},{7,1},{8,14},{9,15},{10,... | collective-permute-start | bytes 442376 | tf_op jit(solution)/shard_map/ppermute | solution.py:38
  11.2 0.2 collective-permute-start.8
  11.5 0.3 collective-permute-start.7
  11.7 2.9 %collective-permute-start.2 = (f32[5,8,128]{2,1,0:T(8,128)S(1)}, f32[5,8,128]{2,1,0:T(8,128)S(1)}, u32[]{:S(2)}, u32[]{:S(2)}) collective-permute-start(f32[5,8,128]{2,1,0:T(8,128)S(1)} %get-tuple-element.22), channel_id=1, source_target_pairs={{0,1},{2,3},{4,5},{6,7},{1,0},{3,2},{5,4},{7,6},{8,9},{10,11},{12,... | collective-permute-start | bytes 61448 | tf_op jit(solution)/shard_map/ppermute | solution.py:33
  14.7 1.1 %collective-permute-start.3 = (f32[5,8,128]{2,1,0:T(8,128)S(1)}, f32[5,8,128]{2,1,0:T(8,128)S(1)}, u32[]{:S(2)}, u32[]{:S(2)}) collective-permute-start(f32[5,8,128]{2,1,0:T(8,128)S(1)} %get-tuple-element.23), channel_id=1, source_target_pairs={{1,2},{3,4},{5,6},{0,7},{2,1},{4,3},{6,5},{7,0},{9,10},{11,12},{13... | collective-permute-start | bytes 61448 | tf_op jit(solution)/shard_map/ppermute | solution.py:33
  15.8 0.0 collective-permute-done.2.jfirst_ref
  15.8 3.6 %collective-permute-done.3.jsecond_ref = f32[5,8,128]{2,1,0:T(8,128)S(1)} collective-permute-done((f32[5,8,128]{2,1,0:T(8,128)S(1)}, f32[5,8,128]{2,1,0:T(8,128)S(1)}, u32[]{:S(2)}, u32[]{:S(2)}) %collective-permute-start.3) | collective-permute-done | bytes 20512 | tf_op jit(solution)/shard_map/ppermute | solution.py:33
  19.4 0.3 shard_map.70
  19.7 0.1 collective-permute-start.4
  19.8 1.9 %collective-permute-start.5 = (f32[17,16,128]{2,1,0:T(8,128)S(1)}, f32[17,16,128]{2,1,0:T(8,128)S(1)}, u32[]{:S(2)}, u32[]{:S(2)}) collective-permute-start(f32[17,16,128]{2,1,0:T(8,128)S(1)} %get-tuple-element.26), channel_id=1, source_target_pairs={{8,16},{16,8},{9,17},{17,9},{10,18},{18,10},{11,19},{19,11},{12,20... | collective-permute-start | bytes 417800 | tf_op jit(solution)/shard_map/ppermute | solution.py:33
  21.7 0.0 collective-permute-done.9
  21.7 0.0 collective-permute-done.8
  21.7 0.0 collective-permute-done.7
  21.8 0.1 collective-permute-start.10
  21.9 3.5 %collective-permute-done.4.first_ref = f32[17,16,128]{2,1,0:T(8,128)S(1)} collective-permute-done((f32[17,16,128]{2,1,0:T(8,128)S(1)}, f32[17,16,128]{2,1,0:T(8,128)S(1)}, u32[]{:S(2)}, u32[]{:S(2)}) %collective-permute-start.4) | collective-permute-done | bytes 139296 | tf_op jit(solution)/shard_map/ppermute | solution.py:33
  25.4 1.9 %collective-permute-done.5.second_ref = f32[17,16,128]{2,1,0:T(8,128)S(1)} collective-permute-done((f32[17,16,128]{2,1,0:T(8,128)S(1)}, f32[17,16,128]{2,1,0:T(8,128)S(1)}, u32[]{:S(2)}, u32[]{:S(2)}) %collective-permute-start.5) | collective-permute-done | bytes 139296 | tf_op jit(solution)/shard_map/ppermute | solution.py:33
  27.3 0.9 %shard_map.72 = (f32[18,8,128]{2,1,0:T(8,128)S(1)}, f32[3,16,8,128]{3,2,1,0:T(8,128)S(1)}) custom-call(f32[3,8,16,128]{3,2,1,0:T(8,128)S(1)} %get-tuple-element.24.own_ref, f32[17,16,128]{2,1,0:T(8,128)S(1)} %collective-permute-done.4.first_ref, f32[17,16,128]{2,1,0:T(8,128)S(1)} %collective-permute-done.5.second_ref, f32[5,8,16,128]{3,2,1,0:T(8,128)S(1)} %bitcast.16, ...), custom_call_target="tpu_custom_call" | custom-call | tf_op jit(solution)/shard_map/pallas_call | solution.py:539
  28.2 1.2 %collective-permute-start.14 = (f32[18,8,128]{2,1,0:T(8,128)S(1)}, f32[18,8,128]{2,1,0:T(8,128)S(1)}, u32[]{:S(2)}, u32[]{:S(2)}) collective-permute-start(f32[18,8,128]{2,1,0:T(8,128)S(1)} %get-tuple-element.33), channel_id=1, source_target_pairs={{0,6},{1,7},{2,4},{3,5},{4,2},{5,3},{6,0},{7,1},{8,14},{9,15},{10,... | collective-permute-start | bytes 221192 | tf_op jit(solution)/shard_map/ppermute | solution.py:38
  29.4 0.2 collective-permute-start.13
  29.6 1.3 %collective-permute-start.12 = (f32[18,8,128]{2,1,0:T(8,128)S(1)}, f32[18,8,128]{2,1,0:T(8,128)S(1)}, u32[]{:S(2)}, u32[]{:S(2)}) collective-permute-start(f32[18,8,128]{2,1,0:T(8,128)S(1)} %get-tuple-element.33), channel_id=1, source_target_pairs={{0,2},{1,3},{2,0},{3,1},{4,6},{5,7},{6,4},{7,5},{8,10},{9,11},{10,... | collective-permute-start | bytes 221192 | tf_op jit(solution)/shard_map/ppermute | solution.py:38
  30.9 1.5 %collective-permute-done.14 = f32[18,8,128]{2,1,0:T(8,128)S(1)} collective-permute-done((f32[18,8,128]{2,1,0:T(8,128)S(1)}, f32[18,8,128]{2,1,0:T(8,128)S(1)}, u32[]{:S(2)}, u32[]{:S(2)}) %collective-permute-start.14) | collective-permute-done | bytes 73760 | tf_op jit(solution)/shard_map/ppermute | solution.py:38
  32.4 2.5 %collective-permute-done.13 = f32[18,8,128]{2,1,0:T(8,128)S(1)} collective-permute-done((f32[18,8,128]{2,1,0:T(8,128)S(1)}, f32[18,8,128]{2,1,0:T(8,128)S(1)}, u32[]{:S(2)}, u32[]{:S(2)}) %collective-permute-start.13) | collective-permute-done | bytes 73760 | tf_op jit(solution)/shard_map/ppermute | solution.py:38
  34.9 0.0 collective-permute-done.12
  34.9 0.6 %collective-permute-start.15 = (f32[3,18,8,128]{3,2,1,0:T(8,128)S(1)}, f32[3,18,8,128]{3,2,1,0:T(8,128)S(1)}, u32[]{:S(2)}, u32[]{:S(2)}) collective-permute-start(f32[3,18,8,128]{3,2,1,0:T(8,128)S(1)} %pad_maximum_fusion.1.refs_6_), channel_id=1, source_target_pairs={{0,1},{1,0},{2,3},{3,2},{4,5},{5,4},{6,7},{7,6},{8,9},{9,8},{10,11... | collective-permute-start | bytes 663560 | tf_op jit(solution)/shard_map/ppermute | solution.py:38
  35.5 0.1 collective-permute-start.6
  35.6 0.4 %collective-permute-start.11 = (f32[18,8,128]{2,1,0:T(8,128)S(1)}, f32[18,8,128]{2,1,0:T(8,128)S(1)}, u32[]{:S(2)}, u32[]{:S(2)}) collective-permute-start(f32[18,8,128]{2,1,0:T(8,128)S(1)} %get-tuple-element.33), channel_id=1, source_target_pairs={{0,1},{1,0},{2,3},{3,2},{4,5},{5,4},{6,7},{7,6},{8,9},{9,8},{10,11... | collective-permute-start | bytes 221192 | tf_op jit(solution)/shard_map/ppermute | solution.py:38
  36.0 0.0 copy-done
  36.0 1.9 %shard_map.69 = f32[5,8,16,128]{3,2,1,0:T(8,128)} custom-call(f32[5,8,16,128]{3,2,1,0:T(8,128)S(1)} %bitcast.17, f32[5,8,16,128]{3,2,1,0:T(8,128)S(1)} %bitcast.20, f32[6,3,8,16,128]{4,3,2,1,0:T(8,128)S(1)} %copy-done, f32[8,16,128]{2,1,0:T(8,128)S(1)} %collective-permute-done.first_ref.rim1_ref, ...), custom_call_target="tpu_custom_call" | custom-call | tf_op jit(solution)/shard_map/pallas_call | solution.py:539
  38.0 0.0 collective-permute-done.6
  38.0 0.0 collective-permute-done.11
  38.0 0.0 collective-permute-done.15.refs_7_
  38.0 0.0 collective-permute-done.10.refs_4_
  38.0 2.1 %shard_map.73 = f32[3,128,128]{2,1,0:T(8,128)} custom-call(f32[3,16,8,128]{3,2,1,0:T(8,128)S(1)} %get-tuple-element.30.refs_0_, f32[30,16,8,128]{3,2,1,0:T(8,128)S(1)} %get-tuple-element.31.refs_1_, f32[1,36,8,128]{3,2,1,0:T(8,128)S(1)} %bitcast.21, f32[3,36,8,128]{3,2,1,0:T(8,128)S(1)} %pad_maximum_fusion.refs_3_, ...), custom_call_target="tpu_custom_call" | custom-call | tf_op jit(solution)/shard_map/pallas_call | solution.py:539
  (2 shorter events, 0.1 us)
Async XLA Ops:
  1.8 34.2 %copy-start = (f32[6,3,8,16,128]{4,3,2,1,0:T(8,128)S(1)}, f32[6,3,8,16,128]{4,3,2,1,0:T(8,128)}, u32[]{:S(2)}) copy-start(f32[6,3,8,16,128]{4,3,2,1,0:T(8,128)} %faces_ref.1) | copy-start | bytes 3538948
  1.8 3.3 %collective-permute-start = (f32[8,16,128]{2,1,0:T(8,128)S(1)}, f32[8,16,128]{2,1,0:T(8,128)S(1)}, u32[]{:S(2)}, u32[]{:S(2)}) collective-permute-start(f32[8,16,128]{2,1,0:T(8,128)S(1)} %get-tuple-element.20), channel_id=1, source_target_pairs={{0,8},{16,24},{8,0},{24,16},{1,9},{17,25},{9,1},{25,17},{2,10},{18... | collective-permute-start | bytes 196616 | tf_op jit(solution)/shard_map/ppermute | solution.py:33
  3.2 5.0 %collective-permute-start.1 = (f32[8,16,128]{2,1,0:T(8,128)S(1)}, f32[8,16,128]{2,1,0:T(8,128)S(1)}, u32[]{:S(2)}, u32[]{:S(2)}) collective-permute-start(f32[8,16,128]{2,1,0:T(8,128)S(1)} %get-tuple-element.21), channel_id=1, source_target_pairs={{8,16},{16,8},{9,17},{17,9},{10,18},{18,10},{11,19},{19,11},{12,20... | collective-permute-start | bytes 196616 | tf_op jit(solution)/shard_map/ppermute | solution.py:33
  9.0 12.7 %collective-permute-start.9 = (f32[36,8,128]{2,1,0:T(8,128)S(1)}, f32[36,8,128]{2,1,0:T(8,128)S(1)}, u32[]{:S(2)}, u32[]{:S(2)}) collective-permute-start(f32[36,8,128]{2,1,0:T(8,128)S(1)} %get-tuple-element.32), channel_id=1, source_target_pairs={{0,6},{1,7},{2,4},{3,5},{4,2},{5,3},{6,0},{7,1},{8,14},{9,15},{10,... | collective-permute-start | bytes 442376 | tf_op jit(solution)/shard_map/ppermute | solution.py:38
  11.2 10.5 %collective-permute-start.8 = (f32[36,8,128]{2,1,0:T(8,128)S(1)}, f32[36,8,128]{2,1,0:T(8,128)S(1)}, u32[]{:S(2)}, u32[]{:S(2)}) collective-permute-start(f32[36,8,128]{2,1,0:T(8,128)S(1)} %get-tuple-element.32), channel_id=1, source_target_pairs={{0,4},{1,5},{2,6},{3,7},{4,0},{5,1},{6,2},{7,3},{8,12},{9,13},{10,... | collective-permute-start | bytes 442376 | tf_op jit(solution)/shard_map/ppermute | solution.py:38
  11.5 10.3 %collective-permute-start.7 = (f32[36,8,128]{2,1,0:T(8,128)S(1)}, f32[36,8,128]{2,1,0:T(8,128)S(1)}, u32[]{:S(2)}, u32[]{:S(2)}) collective-permute-start(f32[36,8,128]{2,1,0:T(8,128)S(1)} %get-tuple-element.32), channel_id=1, source_target_pairs={{0,2},{1,3},{2,0},{3,1},{4,6},{5,7},{6,4},{7,5},{8,10},{9,11},{10,... | collective-permute-start | bytes 442376 | tf_op jit(solution)/shard_map/ppermute | solution.py:38
  11.7 4.0 %collective-permute-start.2 = (f32[5,8,128]{2,1,0:T(8,128)S(1)}, f32[5,8,128]{2,1,0:T(8,128)S(1)}, u32[]{:S(2)}, u32[]{:S(2)}) collective-permute-start(f32[5,8,128]{2,1,0:T(8,128)S(1)} %get-tuple-element.22), channel_id=1, source_target_pairs={{0,1},{2,3},{4,5},{6,7},{1,0},{3,2},{5,4},{7,6},{8,9},{10,11},{12,... | collective-permute-start | bytes 61448 | tf_op jit(solution)/shard_map/ppermute | solution.py:33
  14.7 4.7 %collective-permute-start.3 = (f32[5,8,128]{2,1,0:T(8,128)S(1)}, f32[5,8,128]{2,1,0:T(8,128)S(1)}, u32[]{:S(2)}, u32[]{:S(2)}) collective-permute-start(f32[5,8,128]{2,1,0:T(8,128)S(1)} %get-tuple-element.23), channel_id=1, source_target_pairs={{1,2},{3,4},{5,6},{0,7},{2,1},{4,3},{6,5},{7,0},{9,10},{11,12},{13... | collective-permute-start | bytes 61448 | tf_op jit(solution)/shard_map/ppermute | solution.py:33
  19.7 5.7 %collective-permute-start.4 = (f32[17,16,128]{2,1,0:T(8,128)S(1)}, f32[17,16,128]{2,1,0:T(8,128)S(1)}, u32[]{:S(2)}, u32[]{:S(2)}) collective-permute-start(f32[17,16,128]{2,1,0:T(8,128)S(1)} %get-tuple-element.25), channel_id=1, source_target_pairs={{0,8},{16,24},{8,0},{24,16},{1,9},{17,25},{9,1},{25,17},{2,10},{18... | collective-permute-start | bytes 417800 | tf_op jit(solution)/shard_map/ppermute | solution.py:33
  19.8 7.5 %collective-permute-start.5 = (f32[17,16,128]{2,1,0:T(8,128)S(1)}, f32[17,16,128]{2,1,0:T(8,128)S(1)}, u32[]{:S(2)}, u32[]{:S(2)}) collective-permute-start(f32[17,16,128]{2,1,0:T(8,128)S(1)} %get-tuple-element.26), channel_id=1, source_target_pairs={{8,16},{16,8},{9,17},{17,9},{10,18},{18,10},{11,19},{19,11},{12,20... | collective-permute-start | bytes 417800 | tf_op jit(solution)/shard_map/ppermute | solution.py:33
  21.8 16.2 %collective-permute-start.10 = (f32[3,36,8,128]{3,2,1,0:T(8,128)S(1)}, f32[3,36,8,128]{3,2,1,0:T(8,128)S(1)}, u32[]{:S(2)}, u32[]{:S(2)}) collective-permute-start(f32[3,36,8,128]{3,2,1,0:T(8,128)S(1)} %pad_maximum_fusion.refs_3_), channel_id=1, source_target_pairs={{0,1},{1,0},{2,3},{3,2},{4,5},{5,4},{6,7},{7,6},{8,9},{9,8},{10,11... | collective-permute-start | bytes 1327112 | tf_op jit(solution)/shard_map/ppermute | solution.py:38
  28.2 4.2 %collective-permute-start.14 = (f32[18,8,128]{2,1,0:T(8,128)S(1)}, f32[18,8,128]{2,1,0:T(8,128)S(1)}, u32[]{:S(2)}, u32[]{:S(2)}) collective-permute-start(f32[18,8,128]{2,1,0:T(8,128)S(1)} %get-tuple-element.33), channel_id=1, source_target_pairs={{0,6},{1,7},{2,4},{3,5},{4,2},{5,3},{6,0},{7,1},{8,14},{9,15},{10,... | collective-permute-start | bytes 221192 | tf_op jit(solution)/shard_map/ppermute | solution.py:38
  29.4 5.5 %collective-permute-start.13 = (f32[18,8,128]{2,1,0:T(8,128)S(1)}, f32[18,8,128]{2,1,0:T(8,128)S(1)}, u32[]{:S(2)}, u32[]{:S(2)}) collective-permute-start(f32[18,8,128]{2,1,0:T(8,128)S(1)} %get-tuple-element.33), channel_id=1, source_target_pairs={{0,4},{1,5},{2,6},{3,7},{4,0},{5,1},{6,2},{7,3},{8,12},{9,13},{10,... | collective-permute-start | bytes 221192 | tf_op jit(solution)/shard_map/ppermute | solution.py:38
  29.6 5.3 %collective-permute-start.12 = (f32[18,8,128]{2,1,0:T(8,128)S(1)}, f32[18,8,128]{2,1,0:T(8,128)S(1)}, u32[]{:S(2)}, u32[]{:S(2)}) collective-permute-start(f32[18,8,128]{2,1,0:T(8,128)S(1)} %get-tuple-element.33), channel_id=1, source_target_pairs={{0,2},{1,3},{2,0},{3,1},{4,6},{5,7},{6,4},{7,5},{8,10},{9,11},{10,... | collective-permute-start | bytes 221192 | tf_op jit(solution)/shard_map/ppermute | solution.py:38
  34.9 3.1 %collective-permute-start.15 = (f32[3,18,8,128]{3,2,1,0:T(8,128)S(1)}, f32[3,18,8,128]{3,2,1,0:T(8,128)S(1)}, u32[]{:S(2)}, u32[]{:S(2)}) collective-permute-start(f32[3,18,8,128]{3,2,1,0:T(8,128)S(1)} %pad_maximum_fusion.1.refs_6_), channel_id=1, source_target_pairs={{0,1},{1,0},{2,3},{3,2},{4,5},{5,4},{6,7},{7,6},{8,9},{9,8},{10,11... | collective-permute-start | bytes 663560 | tf_op jit(solution)/shard_map/ppermute | solution.py:38
  35.5 2.5 %collective-permute-start.6 = (f32[36,8,128]{2,1,0:T(8,128)S(1)}, f32[36,8,128]{2,1,0:T(8,128)S(1)}, u32[]{:S(2)}, u32[]{:S(2)}) collective-permute-start(f32[36,8,128]{2,1,0:T(8,128)S(1)} %get-tuple-element.32), channel_id=1, source_target_pairs={{0,1},{1,0},{2,3},{3,2},{4,5},{5,4},{6,7},{7,6},{8,9},{9,8},{10,11... | collective-permute-start | bytes 442376 | tf_op jit(solution)/shard_map/ppermute | solution.py:38
  35.6 2.4 %collective-permute-start.11 = (f32[18,8,128]{2,1,0:T(8,128)S(1)}, f32[18,8,128]{2,1,0:T(8,128)S(1)}, u32[]{:S(2)}, u32[]{:S(2)}) collective-permute-start(f32[18,8,128]{2,1,0:T(8,128)S(1)} %get-tuple-element.33), channel_id=1, source_target_pairs={{0,1},{1,0},{2,3},{3,2},{4,5},{5,4},{6,7},{7,6},{8,9},{9,8},{10,11... | collective-permute-start | bytes 221192 | tf_op jit(solution)/shard_map/ppermute | solution.py:38

commit v7 on v6

--- a/solution.py
+++ b/solution.py
@@ -250,7 +250,8 @@
                     side_ref[index[o], j] = coef[o][1]
         final.update({(d, o): coef[o] for o in REACH[d]})
         begin, at = at, at + len(REACH[d])
-    store_tiles(map_ref, places, final)
+    turned = {(d, o): [roll_k(t, -o[1]) if o[1] else t for t in c] for (d, o), c in final.items()}
+    store_tiles(map_ref, places, turned)
 
 
 def sweeps(v_ref, rate_t, gain_t, warp_ref, rows, nj, last_ref):
@@ -412,16 +413,21 @@
         for comp in range(3):
             total = [load_tiles(off_ref, block, off_places[s, comp]) for s in range(SWEEPS)]
             if x is not None:
+                sums = {}
                 for s in range(SWEEPS):
                     for d in range(SWEEPS - s):
                         n = tiles(s + d)
-                        moved = shifted(x[s, comp], REACH[d], n)
-                        for t in range(n):
-                            terms = [coef[d, o][t] * moved[o][t] for o in REACH[d]]
-                            while len(terms) > 1:
-                                pairs = [terms[i : i + 2] for i in range(0, len(terms), 2)]
-                                terms = [functools.reduce(jnp.add, pair) for pair in pairs]
-                            total[s + d][t] = total[s + d][t] + terms[0]
+                        for i in sorted({o[0] for o in REACH[d]}):
+                            moved = shift_i(x[s, comp], i, n)
+                            for k in (o[1] for o in REACH[d] if o[0] == i):
+                                for t in range(n):
+                                    term = coef[d, (i, k)][t] * moved[t]
+                                    sums.setdefault((s + d, t, k), []).append(term)
+                for (s, t, k), terms in sums.items():
+                    while len(terms) > 1:
+                        pairs = [terms[i : i + 2] for i in range(0, len(terms), 2)]
+                        terms = [functools.reduce(jnp.add, pair) for pair in pairs]
+                    total[s][t] = total[s][t] + (roll_k(terms[0], k) if k else terms[0])
             for s in range(SWEEPS):
                 fresh[s, comp] = total[s]
         return fresh

time: 40.2 us -> 40.1 us (level)
  no operation moved by 1% of the time
where the time goes in v7:
time: 40.1 us; the launch traced here: 39.9 us
  waiting for transfers between devices  16.1 us (40%)
  starting transfers between devices  15.9 us (40%)
  Pallas kernels  7.04 us (18%)
  between operations  0.75 us (2%)
    ppermute x6, waiting for transfers between devices, swap(): return lax.ppermute(x, axis, matching(axis, first, closed))  12.1 us
    ppermute x6, starting transfers between devices, swap(): return lax.ppermute(x, axis, matching(axis, first, closed))  9.3 us
    pallas_call x6, Pallas kernels, call(): pl.pallas_call(kernel, out_shape=out_shape, in_specs=[pl.BlockSpec(memory...  7.04 us
    ppermute x10, starting transfers between devices, flip(): return lax.ppermute(x, axis, [(i, i ^ mask) for i in range(count)])  6.6 us
    ppermute x10, waiting for transfers between devices, flip(): return lax.ppermute(x, axis, [(i, i ^ mask) for i in range(count)])  4 us
  transfers between devices with their start and end apart: 16, of which 6 were waited for; matrix products, arithmetic and copies ran while one was open for 0% of the time, Pallas kernels for 8%

profile of v7, /device:TPU:17, one launch (start us, length us, event | category | flops | bytes accessed | tf_op | source)
XLA Modules:
  0.0 39.9 jit_solution(2446747106118321558)
XLA Ops:
  0.6 1.2 %shard_map.68 = (f32[5,128,128]{2,1,0:T(8,128)S(1)}, f32[5,128,128]{2,1,0:T(8,128)S(1)}, f32[128,128]{1,0:T(8,128)S(1)}, f32[5,8,128]{2,1,0:T(8,128)S(1)}, f32[5...) custom-call(f32[5,128,128]{2,1,0:T(8,128)} %bitcast.23, f32[5,128,128]{2,1,0:T(8,128)} %bitcast.24, ...), custom_call_target="tpu_custom_call" | custom-call | tf_op jit(solution)/shard_map/pallas_call | solution.py:545
  1.8 0.0 copy-start
  1.8 1.4 %collective-permute-start = (f32[8,16,128]{2,1,0:T(8,128)S(1)}, f32[8,16,128]{2,1,0:T(8,128)S(1)}, u32[]{:S(2)}, u32[]{:S(2)}) collective-permute-start(f32[8,16,128]{2,1,0:T(8,128)S(1)} %get-tuple-element.20), channel_id=1, source_target_pairs={{0,8},{16,24},{8,0},{24,16},{1,9},{17,25},{9,1},{25,17},{2,10},{18... | collective-permute-start | bytes 196616 | tf_op jit(solution)/shard_map/ppermute | solution.py:33
  3.2 1.9 %collective-permute-start.1 = (f32[8,16,128]{2,1,0:T(8,128)S(1)}, f32[8,16,128]{2,1,0:T(8,128)S(1)}, u32[]{:S(2)}, u32[]{:S(2)}) collective-permute-start(f32[8,16,128]{2,1,0:T(8,128)S(1)} %get-tuple-element.21), channel_id=1, source_target_pairs={{8,16},{16,8},{9,17},{17,9},{10,18},{18,10},{11,19},{19,11},{12,20... | collective-permute-start | bytes 196616 | tf_op jit(solution)/shard_map/ppermute | solution.py:33
  5.1 0.0 collective-permute-done.first_ref.rim1_ref
  5.1 3.1 %collective-permute-done.1.second_ref.rim2_ref = f32[8,16,128]{2,1,0:T(8,128)S(1)} collective-permute-done((f32[8,16,128]{2,1,0:T(8,128)S(1)}, f32[8,16,128]{2,1,0:T(8,128)S(1)}, u32[]{:S(2)}, u32[]{:S(2)}) %collective-permute-start.1) | collective-permute-done | bytes 65568 | tf_op jit(solution)/shard_map/ppermute | solution.py:33
  8.2 0.9 %shard_map.71 = (f32[16,2,8,128]{3,2,1,0:T(8,128)S(1)}, f32[16,2,8,128]{3,2,1,0:T(8,128)S(1)}, f32[36,8,128]{2,1,0:T(8,128)S(1)}, f32[30,16,8,128]{3,2,1,0:T(8,128)S(1)}) custom-call(f32[128,128]{1,0:T(8,128)S(1)} %get-tuple-element.27.own_ref, f32[8,16,128]{2,1,0:T(8,128)S(1)} %collective-permute-done.first_ref.rim1_ref, ...), custom_call_target="tpu_custom_call" | custom-call | tf_op jit(solution)/shard_map/pallas_call | solution.py:545
  9.1 2.2 %collective-permute-start.9 = (f32[36,8,128]{2,1,0:T(8,128)S(1)}, f32[36,8,128]{2,1,0:T(8,128)S(1)}, u32[]{:S(2)}, u32[]{:S(2)}) collective-permute-start(f32[36,8,128]{2,1,0:T(8,128)S(1)} %get-tuple-element.32), channel_id=1, source_target_pairs={{0,6},{1,7},{2,4},{3,5},{4,2},{5,3},{6,0},{7,1},{8,14},{9,15},{10,... | collective-permute-start | bytes 442376 | tf_op jit(solution)/shard_map/ppermute | solution.py:38
  11.3 0.2 collective-permute-start.8
  11.5 0.3 collective-permute-start.7
  11.8 2.9 %collective-permute-start.2 = (f32[5,8,128]{2,1,0:T(8,128)S(1)}, f32[5,8,128]{2,1,0:T(8,128)S(1)}, u32[]{:S(2)}, u32[]{:S(2)}) collective-permute-start(f32[5,8,128]{2,1,0:T(8,128)S(1)} %get-tuple-element.22), channel_id=1, source_target_pairs={{0,1},{2,3},{4,5},{6,7},{1,0},{3,2},{5,4},{7,6},{8,9},{10,11},{12,... | collective-permute-start | bytes 61448 | tf_op jit(solution)/shard_map/ppermute | solution.py:33
  14.7 1.1 %collective-permute-start.3 = (f32[5,8,128]{2,1,0:T(8,128)S(1)}, f32[5,8,128]{2,1,0:T(8,128)S(1)}, u32[]{:S(2)}, u32[]{:S(2)}) collective-permute-start(f32[5,8,128]{2,1,0:T(8,128)S(1)} %get-tuple-element.23), channel_id=1, source_target_pairs={{1,2},{3,4},{5,6},{0,7},{2,1},{4,3},{6,5},{7,0},{9,10},{11,12},{13... | collective-permute-start | bytes 61448 | tf_op jit(solution)/shard_map/ppermute | solution.py:33
  15.8 0.0 collective-permute-done.2.jfirst_ref
  15.8 3.6 %collective-permute-done.3.jsecond_ref = f32[5,8,128]{2,1,0:T(8,128)S(1)} collective-permute-done((f32[5,8,128]{2,1,0:T(8,128)S(1)}, f32[5,8,128]{2,1,0:T(8,128)S(1)}, u32[]{:S(2)}, u32[]{:S(2)}) %collective-permute-start.3) | collective-permute-done | bytes 20512 | tf_op jit(solution)/shard_map/ppermute | solution.py:33
  19.5 0.3 shard_map.70
  19.8 0.1 collective-permute-start.4
  19.8 1.9 %collective-permute-start.5 = (f32[17,16,128]{2,1,0:T(8,128)S(1)}, f32[17,16,128]{2,1,0:T(8,128)S(1)}, u32[]{:S(2)}, u32[]{:S(2)}) collective-permute-start(f32[17,16,128]{2,1,0:T(8,128)S(1)} %get-tuple-element.26), channel_id=1, source_target_pairs={{8,16},{16,8},{9,17},{17,9},{10,18},{18,10},{11,19},{19,11},{12,20... | collective-permute-start | bytes 417800 | tf_op jit(solution)/shard_map/ppermute | solution.py:33
  21.8 0.0 collective-permute-done.9
  21.8 0.0 collective-permute-done.8
  21.8 0.0 collective-permute-done.7
  21.8 0.1 collective-permute-start.10
  21.9 3.5 %collective-permute-done.4.first_ref = f32[17,16,128]{2,1,0:T(8,128)S(1)} collective-permute-done((f32[17,16,128]{2,1,0:T(8,128)S(1)}, f32[17,16,128]{2,1,0:T(8,128)S(1)}, u32[]{:S(2)}, u32[]{:S(2)}) %collective-permute-start.4) | collective-permute-done | bytes 139296 | tf_op jit(solution)/shard_map/ppermute | solution.py:33
  25.5 1.9 %collective-permute-done.5.second_ref = f32[17,16,128]{2,1,0:T(8,128)S(1)} collective-permute-done((f32[17,16,128]{2,1,0:T(8,128)S(1)}, f32[17,16,128]{2,1,0:T(8,128)S(1)}, u32[]{:S(2)}, u32[]{:S(2)}) %collective-permute-start.5) | collective-permute-done | bytes 139296 | tf_op jit(solution)/shard_map/ppermute | solution.py:33
  27.4 0.9 %shard_map.72 = (f32[18,8,128]{2,1,0:T(8,128)S(1)}, f32[3,16,8,128]{3,2,1,0:T(8,128)S(1)}) custom-call(f32[3,8,16,128]{3,2,1,0:T(8,128)S(1)} %get-tuple-element.24.own_ref, f32[17,16,128]{2,1,0:T(8,128)S(1)} %collective-permute-done.4.first_ref, f32[17,16,128]{2,1,0:T(8,128)S(1)} %collective-permute-done.5.second_ref, f32[5,8,16,128]{3,2,1,0:T(8,128)S(1)} %bitcast.16, ...), custom_call_target="tpu_custom_call" | custom-call | tf_op jit(solution)/shard_map/pallas_call | solution.py:545
  28.3 1.2 %collective-permute-start.14 = (f32[18,8,128]{2,1,0:T(8,128)S(1)}, f32[18,8,128]{2,1,0:T(8,128)S(1)}, u32[]{:S(2)}, u32[]{:S(2)}) collective-permute-start(f32[18,8,128]{2,1,0:T(8,128)S(1)} %get-tuple-element.33), channel_id=1, source_target_pairs={{0,6},{1,7},{2,4},{3,5},{4,2},{5,3},{6,0},{7,1},{8,14},{9,15},{10,... | collective-permute-start | bytes 221192 | tf_op jit(solution)/shard_map/ppermute | solution.py:38
  29.4 0.2 collective-permute-start.13
  29.7 1.3 %collective-permute-start.12 = (f32[18,8,128]{2,1,0:T(8,128)S(1)}, f32[18,8,128]{2,1,0:T(8,128)S(1)}, u32[]{:S(2)}, u32[]{:S(2)}) collective-permute-start(f32[18,8,128]{2,1,0:T(8,128)S(1)} %get-tuple-element.33), channel_id=1, source_target_pairs={{0,2},{1,3},{2,0},{3,1},{4,6},{5,7},{6,4},{7,5},{8,10},{9,11},{10,... | collective-permute-start | bytes 221192 | tf_op jit(solution)/shard_map/ppermute | solution.py:38
  31.0 1.5 %collective-permute-done.14 = f32[18,8,128]{2,1,0:T(8,128)S(1)} collective-permute-done((f32[18,8,128]{2,1,0:T(8,128)S(1)}, f32[18,8,128]{2,1,0:T(8,128)S(1)}, u32[]{:S(2)}, u32[]{:S(2)}) %collective-permute-start.14) | collective-permute-done | bytes 73760 | tf_op jit(solution)/shard_map/ppermute | solution.py:38
  32.5 2.5 %collective-permute-done.13 = f32[18,8,128]{2,1,0:T(8,128)S(1)} collective-permute-done((f32[18,8,128]{2,1,0:T(8,128)S(1)}, f32[18,8,128]{2,1,0:T(8,128)S(1)}, u32[]{:S(2)}, u32[]{:S(2)}) %collective-permute-start.13) | collective-permute-done | bytes 73760 | tf_op jit(solution)/shard_map/ppermute | solution.py:38
  34.9 0.0 collective-permute-done.12
  35.0 0.6 %collective-permute-start.15 = (f32[3,18,8,128]{3,2,1,0:T(8,128)S(1)}, f32[3,18,8,128]{3,2,1,0:T(8,128)S(1)}, u32[]{:S(2)}, u32[]{:S(2)}) collective-permute-start(f32[3,18,8,128]{3,2,1,0:T(8,128)S(1)} %pad_maximum_fusion.1.refs_6_), channel_id=1, source_target_pairs={{0,1},{1,0},{2,3},{3,2},{4,5},{5,4},{6,7},{7,6},{8,9},{9,8},{10,11... | collective-permute-start | bytes 663560 | tf_op jit(solution)/shard_map/ppermute | solution.py:38
  35.6 0.1 collective-permute-start.6
  35.7 0.4 %collective-permute-start.11 = (f32[18,8,128]{2,1,0:T(8,128)S(1)}, f32[18,8,128]{2,1,0:T(8,128)S(1)}, u32[]{:S(2)}, u32[]{:S(2)}) collective-permute-start(f32[18,8,128]{2,1,0:T(8,128)S(1)} %get-tuple-element.33), channel_id=1, source_target_pairs={{0,1},{1,0},{2,3},{3,2},{4,5},{5,4},{6,7},{7,6},{8,9},{9,8},{10,11... | collective-permute-start | bytes 221192 | tf_op jit(solution)/shard_map/ppermute | solution.py:38
  36.1 0.0 copy-done
  36.1 1.9 %shard_map.69 = f32[5,8,16,128]{3,2,1,0:T(8,128)} custom-call(f32[5,8,16,128]{3,2,1,0:T(8,128)S(1)} %bitcast.17, f32[5,8,16,128]{3,2,1,0:T(8,128)S(1)} %bitcast.20, f32[6,3,8,16,128]{4,3,2,1,0:T(8,128)S(1)} %copy-done, f32[8,16,128]{2,1,0:T(8,128)S(1)} %collective-permute-done.first_ref.rim1_ref, ...), custom_call_target="tpu_custom_call" | custom-call | tf_op jit(solution)/shard_map/pallas_call | solution.py:545
  38.0 0.0 collective-permute-done.6
  38.0 0.0 collective-permute-done.11
  38.0 0.0 collective-permute-done.15.refs_7_
  38.0 0.0 collective-permute-done.10.refs_4_
  38.0 1.8 %shard_map.73 = f32[3,128,128]{2,1,0:T(8,128)} custom-call(f32[3,16,8,128]{3,2,1,0:T(8,128)S(1)} %get-tuple-element.30.refs_0_, f32[30,16,8,128]{3,2,1,0:T(8,128)S(1)} %get-tuple-element.31.refs_1_, f32[1,36,8,128]{3,2,1,0:T(8,128)S(1)} %bitcast.21, f32[3,36,8,128]{3,2,1,0:T(8,128)S(1)} %pad_maximum_fusion.refs_3_, ...), custom_call_target="tpu_custom_call" | custom-call | tf_op jit(solution)/shard_map/pallas_call | solution.py:545
  (2 shorter events, 0.1 us)
Async XLA Ops:
  1.8 34.3 %copy-start = (f32[6,3,8,16,128]{4,3,2,1,0:T(8,128)S(1)}, f32[6,3,8,16,128]{4,3,2,1,0:T(8,128)}, u32[]{:S(2)}) copy-start(f32[6,3,8,16,128]{4,3,2,1,0:T(8,128)} %faces_ref.1) | copy-start | bytes 3538948
  1.8 3.3 %collective-permute-start = (f32[8,16,128]{2,1,0:T(8,128)S(1)}, f32[8,16,128]{2,1,0:T(8,128)S(1)}, u32[]{:S(2)}, u32[]{:S(2)}) collective-permute-start(f32[8,16,128]{2,1,0:T(8,128)S(1)} %get-tuple-element.20), channel_id=1, source_target_pairs={{0,8},{16,24},{8,0},{24,16},{1,9},{17,25},{9,1},{25,17},{2,10},{18... | collective-permute-start | bytes 196616 | tf_op jit(solution)/shard_map/ppermute | solution.py:33
  3.2 5.0 %collective-permute-start.1 = (f32[8,16,128]{2,1,0:T(8,128)S(1)}, f32[8,16,128]{2,1,0:T(8,128)S(1)}, u32[]{:S(2)}, u32[]{:S(2)}) collective-permute-start(f32[8,16,128]{2,1,0:T(8,128)S(1)} %get-tuple-element.21), channel_id=1, source_target_pairs={{8,16},{16,8},{9,17},{17,9},{10,18},{18,10},{11,19},{19,11},{12,20... | collective-permute-start | bytes 196616 | tf_op jit(solution)/shard_map/ppermute | solution.py:33
  9.1 12.7 %collective-permute-start.9 = (f32[36,8,128]{2,1,0:T(8,128)S(1)}, f32[36,8,128]{2,1,0:T(8,128)S(1)}, u32[]{:S(2)}, u32[]{:S(2)}) collective-permute-start(f32[36,8,128]{2,1,0:T(8,128)S(1)} %get-tuple-element.32), channel_id=1, source_target_pairs={{0,6},{1,7},{2,4},{3,5},{4,2},{5,3},{6,0},{7,1},{8,14},{9,15},{10,... | collective-permute-start | bytes 442376 | tf_op jit(solution)/shard_map/ppermute | solution.py:38
  11.3 10.5 %collective-permute-start.8 = (f32[36,8,128]{2,1,0:T(8,128)S(1)}, f32[36,8,128]{2,1,0:T(8,128)S(1)}, u32[]{:S(2)}, u32[]{:S(2)}) collective-permute-start(f32[36,8,128]{2,1,0:T(8,128)S(1)} %get-tuple-element.32), channel_id=1, source_target_pairs={{0,4},{1,5},{2,6},{3,7},{4,0},{5,1},{6,2},{7,3},{8,12},{9,13},{10,... | collective-permute-start | bytes 442376 | tf_op jit(solution)/shard_map/ppermute | solution.py:38
  11.5 10.3 %collective-permute-start.7 = (f32[36,8,128]{2,1,0:T(8,128)S(1)}, f32[36,8,128]{2,1,0:T(8,128)S(1)}, u32[]{:S(2)}, u32[]{:S(2)}) collective-permute-start(f32[36,8,128]{2,1,0:T(8,128)S(1)} %get-tuple-element.32), channel_id=1, source_target_pairs={{0,2},{1,3},{2,0},{3,1},{4,6},{5,7},{6,4},{7,5},{8,10},{9,11},{10,... | collective-permute-start | bytes 442376 | tf_op jit(solution)/shard_map/ppermute | solution.py:38
  11.8 4.0 %collective-permute-start.2 = (f32[5,8,128]{2,1,0:T(8,128)S(1)}, f32[5,8,128]{2,1,0:T(8,128)S(1)}, u32[]{:S(2)}, u32[]{:S(2)}) collective-permute-start(f32[5,8,128]{2,1,0:T(8,128)S(1)} %get-tuple-element.22), channel_id=1, source_target_pairs={{0,1},{2,3},{4,5},{6,7},{1,0},{3,2},{5,4},{7,6},{8,9},{10,11},{12,... | collective-permute-start | bytes 61448 | tf_op jit(solution)/shard_map/ppermute | solution.py:33
  14.7 4.7 %collective-permute-start.3 = (f32[5,8,128]{2,1,0:T(8,128)S(1)}, f32[5,8,128]{2,1,0:T(8,128)S(1)}, u32[]{:S(2)}, u32[]{:S(2)}) collective-permute-start(f32[5,8,128]{2,1,0:T(8,128)S(1)} %get-tuple-element.23), channel_id=1, source_target_pairs={{1,2},{3,4},{5,6},{0,7},{2,1},{4,3},{6,5},{7,0},{9,10},{11,12},{13... | collective-permute-start | bytes 61448 | tf_op jit(solution)/shard_map/ppermute | solution.py:33
  19.8 5.7 %collective-permute-start.4 = (f32[17,16,128]{2,1,0:T(8,128)S(1)}, f32[17,16,128]{2,1,0:T(8,128)S(1)}, u32[]{:S(2)}, u32[]{:S(2)}) collective-permute-start(f32[17,16,128]{2,1,0:T(8,128)S(1)} %get-tuple-element.25), channel_id=1, source_target_pairs={{0,8},{16,24},{8,0},{24,16},{1,9},{17,25},{9,1},{25,17},{2,10},{18... | collective-permute-start | bytes 417800 | tf_op jit(solution)/shard_map/ppermute | solution.py:33
  19.8 7.5 %collective-permute-start.5 = (f32[17,16,128]{2,1,0:T(8,128)S(1)}, f32[17,16,128]{2,1,0:T(8,128)S(1)}, u32[]{:S(2)}, u32[]{:S(2)}) collective-permute-start(f32[17,16,128]{2,1,0:T(8,128)S(1)} %get-tuple-element.26), channel_id=1, source_target_pairs={{8,16},{16,8},{9,17},{17,9},{10,18},{18,10},{11,19},{19,11},{12,20... | collective-permute-start | bytes 417800 | tf_op jit(solution)/shard_map/ppermute | solution.py:33
  21.8 16.2 %collective-permute-start.10 = (f32[3,36,8,128]{3,2,1,0:T(8,128)S(1)}, f32[3,36,8,128]{3,2,1,0:T(8,128)S(1)}, u32[]{:S(2)}, u32[]{:S(2)}) collective-permute-start(f32[3,36,8,128]{3,2,1,0:T(8,128)S(1)} %pad_maximum_fusion.refs_3_), channel_id=1, source_target_pairs={{0,1},{1,0},{2,3},{3,2},{4,5},{5,4},{6,7},{7,6},{8,9},{9,8},{10,11... | collective-permute-start | bytes 1327112 | tf_op jit(solution)/shard_map/ppermute | solution.py:38
  28.3 4.2 %collective-permute-start.14 = (f32[18,8,128]{2,1,0:T(8,128)S(1)}, f32[18,8,128]{2,1,0:T(8,128)S(1)}, u32[]{:S(2)}, u32[]{:S(2)}) collective-permute-start(f32[18,8,128]{2,1,0:T(8,128)S(1)} %get-tuple-element.33), channel_id=1, source_target_pairs={{0,6},{1,7},{2,4},{3,5},{4,2},{5,3},{6,0},{7,1},{8,14},{9,15},{10,... | collective-permute-start | bytes 221192 | tf_op jit(solution)/shard_map/ppermute | solution.py:38
  29.4 5.5 %collective-permute-start.13 = (f32[18,8,128]{2,1,0:T(8,128)S(1)}, f32[18,8,128]{2,1,0:T(8,128)S(1)}, u32[]{:S(2)}, u32[]{:S(2)}) collective-permute-start(f32[18,8,128]{2,1,0:T(8,128)S(1)} %get-tuple-element.33), channel_id=1, source_target_pairs={{0,4},{1,5},{2,6},{3,7},{4,0},{5,1},{6,2},{7,3},{8,12},{9,13},{10,... | collective-permute-start | bytes 221192 | tf_op jit(solution)/shard_map/ppermute | solution.py:38
  29.7 5.3 %collective-permute-start.12 = (f32[18,8,128]{2,1,0:T(8,128)S(1)}, f32[18,8,128]{2,1,0:T(8,128)S(1)}, u32[]{:S(2)}, u32[]{:S(2)}) collective-permute-start(f32[18,8,128]{2,1,0:T(8,128)S(1)} %get-tuple-element.33), channel_id=1, source_target_pairs={{0,2},{1,3},{2,0},{3,1},{4,6},{5,7},{6,4},{7,5},{8,10},{9,11},{10,... | collective-permute-start | bytes 221192 | tf_op jit(solution)/shard_map/ppermute | solution.py:38
  35.0 3.1 %collective-permute-start.15 = (f32[3,18,8,128]{3,2,1,0:T(8,128)S(1)}, f32[3,18,8,128]{3,2,1,0:T(8,128)S(1)}, u32[]{:S(2)}, u32[]{:S(2)}) collective-permute-start(f32[3,18,8,128]{3,2,1,0:T(8,128)S(1)} %pad_maximum_fusion.1.refs_6_), channel_id=1, source_target_pairs={{0,1},{1,0},{2,3},{3,2},{4,5},{5,4},{6,7},{7,6},{8,9},{9,8},{10,11... | collective-permute-start | bytes 663560 | tf_op jit(solution)/shard_map/ppermute | solution.py:38
  35.6 2.5 %collective-permute-start.6 = (f32[36,8,128]{2,1,0:T(8,128)S(1)}, f32[36,8,128]{2,1,0:T(8,128)S(1)}, u32[]{:S(2)}, u32[]{:S(2)}) collective-permute-start(f32[36,8,128]{2,1,0:T(8,128)S(1)} %get-tuple-element.32), channel_id=1, source_target_pairs={{0,1},{1,0},{2,3},{3,2},{4,5},{5,4},{6,7},{7,6},{8,9},{9,8},{10,11... | collective-permute-start | bytes 442376 | tf_op jit(solution)/shard_map/ppermute | solution.py:38
  35.7 2.4 %collective-permute-start.11 = (f32[18,8,128]{2,1,0:T(8,128)S(1)}, f32[18,8,128]{2,1,0:T(8,128)S(1)}, u32[]{:S(2)}, u32[]{:S(2)}) collective-permute-start(f32[18,8,128]{2,1,0:T(8,128)S(1)} %get-tuple-element.33), channel_id=1, source_target_pairs={{0,1},{1,0},{2,3},{3,2},{4,5},{5,4},{6,7},{7,6},{8,9},{9,8},{10,11... | collective-permute-start | bytes 221192 | tf_op jit(solution)/shard_map/ppermute | solution.py:38
